TPU v7x, 256 devices: a whole 4x4x8 slice. The times are simulated.
256 devices in a mesh: seq: 32 (over z, x), mp: 8 (over y, core).
Axes of the slice: x: 4, y: 4, z: 8, core: 2. Of those that a mesh axis runs over, the one named last changes fastest.
Arguments:
- win_query: bfloat16 [16384, 4096], P('seq', 'mp'), may hold values from -8 to 8
- win_key: bfloat16 [16384, 4096], P('seq', 'mp'), may hold values from -8 to 8
- win_value: bfloat16 [16384, 4096], P('seq', 'mp'), may hold values from -6 to 6
- win_dout: bfloat16 [16384, 4096], P('seq', 'mp'), may hold values from -16 to 16
- cross_query: bfloat16 [16384, 4096], P('seq', 'mp'), may hold values from -8 to 8
- cross_dout: bfloat16 [16384, 4096], P('seq', 'mp'), may hold values from -16 to 16
- patch_key: bfloat16 [4096, 4096], P('seq', 'mp'), may hold values from -8 to 8
- patch_value: bfloat16 [4096, 4096], P('seq', 'mp'), may hold values from -6 to 6
- patch_len: int32 [64, 64], P('seq'), may hold values from 1 to 16, 256 in all within a row
- patch_owner: int32 [4096, 1], P('seq'), may hold values from 0 to 31; in each aligned block of 128 rows (0 to 127, 128 to 255, ...) at most 8 rows name the same one
- w_query: bfloat16 [4096, 4096], P('seq', 'mp'), may hold values from -0.09375 to 0.09375
Outputs:
- win_dq: bfloat16 [16384, 4096], P('seq', 'mp')
- win_dk: bfloat16 [16384, 4096], P('seq', 'mp')
- win_dv: bfloat16 [16384, 4096], P('seq', 'mp')
- patch_grads: bfloat16 [2, 8192, 4096], P(None, 'seq', 'mp')
- byte_grads: bfloat16 [16384, 4096], P('seq', 'mp')
Inputs may be any that keep to these rules, and one draw needn't show every extreme that they name: `patch_len`: each row lists the byte lengths of the patches of one stored block in order; they sum to 256 and the largest is exactly 16. `patch_owner`: within each aligned block of 128 rows (the patch rows of one device) no owner is named more than 8 times, a bound that some block reaches.
All inputs are finite; a program needn't handle non-finite values.
Results may differ from a plain program's by a relative error of at most 0.017.
Values may be sent and summed in bfloat16 or wider, within the bound.
No kernel may reach another device: no remote copies, remote signals or barrier semaphores. Data moves between devices by JAX's collectives and lax.ppermute only.
A program may use at most 64 MiB of HBM per device.

v0:
```python
import math

import jax
import jax.numpy as jnp
from jax import lax
from jax.sharding import PartitionSpec as P

HD = 128
WIN = 256


def shifted(block, axis, distance):
    devices = range(lax.axis_size(axis))
    route = [(i - distance, i) for i in devices if i - distance in devices]
    return lax.ppermute(block, axis, route)


def head_split(values):
    return values.reshape(values.shape[0], values.shape[1] // HD, HD)


def row_stats(scores, allowed):
    masked = jnp.where(allowed, scores, -1e30)
    row_top = jnp.max(masked, axis=-1, keepdims=True)
    row_total = jnp.sum(
        jnp.exp(jnp.where(allowed, scores - row_top, -1e30)), axis=-1, keepdims=True
    )
    return row_top + jnp.log(row_total)


def window_part(query_rows, dout_rows, key_ext, value_ext, tail_valid):
    window = WIN
    inv_root = 1.0 / math.sqrt(HD)
    length = query_rows.shape[0]
    width = query_rows.shape[1]
    head_count = width // HD
    query_heads = head_split(query_rows)
    dout_heads = head_split(dout_rows)
    key_heads = head_split(key_ext)
    value_heads = head_split(value_ext)
    rows_at = lax.broadcasted_iota(jnp.int32, (window, 2 * window), 0)
    cols_at = lax.broadcasted_iota(jnp.int32, (window, 2 * window), 1)
    gap = cols_at - rows_at

    def one_step(sub_step, state_in):
        dq_acc, dk_acc, dv_acc, total_acc, delta_acc = state_in
        offset = sub_step * window
        allowed = ((gap >= 0) & (gap <= window) & ((cols_at + offset >= window) | tail_valid))[None]
        scores = (
            jnp.einsum("qhd,khd->hqk", query_heads, key_heads, preferred_element_type=jnp.float32)
            * inv_root
        )
        log_total = row_stats(scores, allowed)
        prob_rows = jnp.exp(jnp.where(allowed, scores - log_total, -1e30))
        dprobs = jnp.einsum(
            "qhd,khd->hqk", dout_heads, value_heads, preferred_element_type=jnp.float32
        )
        row_delta = jnp.sum(prob_rows * dprobs, axis=-1, keepdims=True)
        grad_scores = (prob_rows * (dprobs - row_delta) * inv_root).astype(jnp.bfloat16)
        probs_low = prob_rows.astype(jnp.bfloat16)
        dq_sub = jnp.einsum(
            "hqk,khd->qhd", grad_scores, key_heads, preferred_element_type=jnp.float32
        )
        dk_sub = jnp.einsum(
            "hqk,qhd->khd", grad_scores, query_heads, preferred_element_type=jnp.float32
        )
        dv_sub = jnp.einsum(
            "hqk,qhd->khd", probs_low, dout_heads, preferred_element_type=jnp.float32
        )
        dq_acc = dq_sub
        dk_acc = dk_acc + dk_sub
        dv_acc = dv_acc + dv_sub
        total_acc = log_total[:, :, 0].T
        delta_acc = row_delta[:, :, 0].T
        return (dq_acc, dk_acc, dv_acc, total_acc, delta_acc)

    start_state = (
        jnp.zeros((length, head_count, HD), jnp.float32),
        jnp.zeros((length + window, head_count, HD), jnp.float32),
        jnp.zeros((length + window, head_count, HD), jnp.float32),
        jnp.zeros((length, head_count), jnp.float32),
        jnp.zeros((length, head_count), jnp.float32),
    )
    dq_acc, dk_acc, dv_acc, total_acc, delta_acc = lax.fori_loop(
        0, length // window, one_step, start_state
    )
    return (
        dq_acc.reshape(length, width),
        dk_acc.reshape(length + window, width),
        dv_acc.reshape(length + window, width),
        total_acc,
        delta_acc,
    )


def local(
    win_query,
    win_key,
    win_value,
    win_dout,
    cross_query,
    cross_dout,
    patch_key,
    patch_value,
    patch_len,
    patch_owner,
    w_query,
):
    window = WIN
    row_count = win_query.shape[0]
    block_rows = row_count // 2
    width = win_query.shape[1]
    head_count = width // HD
    inv_root = 1.0 / math.sqrt(HD)
    seq_count = lax.axis_size("seq")
    seq_index = lax.axis_index("seq")
    is_last = seq_index == seq_count - 1
    low_valid = seq_index > 0
    low_rim = jnp.stack(
        [win_key[block_rows - window : block_rows], win_value[block_rows - window : block_rows]]
    )
    high_rim = jnp.stack([win_key[row_count - window :], win_value[row_count - window :]])
    from_before = shifted(low_rim, "seq", 1)
    from_after = shifted(high_rim, "seq", -1)
    high_prev = jnp.where(is_last, low_rim, from_after)
    low_part = window_part(
        win_query[:block_rows],
        win_dout[:block_rows],
        jnp.concatenate([from_before[0], win_key[:block_rows]], axis=0),
        jnp.concatenate([from_before[1], win_value[:block_rows]], axis=0),
        low_valid,
    )
    high_part = window_part(
        win_query[block_rows:],
        win_dout[block_rows:],
        jnp.concatenate([high_prev[0], win_key[block_rows:]], axis=0),
        jnp.concatenate([high_prev[1], win_value[block_rows:]], axis=0),
        jnp.array(True),
    )
    low_send = jnp.stack([low_part[1][:window], low_part[2][:window]])
    high_send = jnp.stack([high_part[1][:window], high_part[2][:window]])
    low_back = shifted(low_send.astype(jnp.bfloat16), "seq", -1).astype(low_send.dtype)
    high_back = shifted(high_send.astype(jnp.bfloat16), "seq", 1).astype(high_send.dtype)
    low_extra = low_back + jnp.where(is_last, high_send, 0.0)
    dk_low = low_part[1][window:].at[block_rows - window :].add(low_extra[0])
    dv_low = low_part[2][window:].at[block_rows - window :].add(low_extra[1])
    dk_high = high_part[1][window:].at[block_rows - window :].add(high_back[0])
    dv_high = high_part[2][window:].at[block_rows - window :].add(high_back[1])
    win_dq = jnp.concatenate([low_part[0], high_part[0]], axis=0).astype(jnp.bfloat16)
    win_dk = jnp.concatenate([dk_low, dk_high], axis=0).astype(jnp.bfloat16)
    win_dv = jnp.concatenate([dv_low, dv_high], axis=0).astype(jnp.bfloat16)
    patch_rows = patch_key.shape[0]
    per_block = patch_rows // 2
    cross_heads = cross_query.reshape(2, block_rows, head_count, HD)
    grad_heads = cross_dout.reshape(2, block_rows, head_count, HD)
    key_heads = patch_key.reshape(2, per_block, head_count, HD)
    value_heads = patch_value.reshape(2, per_block, head_count, HD)
    starts = jnp.cumsum(patch_len, axis=1) - patch_len
    within = lax.broadcasted_iota(jnp.int32, (block_rows, per_block), 0)
    allowed = (starts[:, None, :] <= within[None])[:, None]
    scores = (
        jnp.einsum("bqhd,bkhd->bhqk", cross_heads, key_heads, preferred_element_type=jnp.float32)
        * inv_root
    )
    log_total = row_stats(scores, allowed)
    prob_rows = jnp.exp(jnp.where(allowed, scores - log_total, -1e30))
    dprobs = jnp.einsum(
        "bqhd,bkhd->bhqk", grad_heads, value_heads, preferred_element_type=jnp.float32
    )
    row_delta = jnp.sum(prob_rows * dprobs, axis=-1, keepdims=True)
    cross_grad = (prob_rows * (dprobs - row_delta) * inv_root).astype(jnp.bfloat16)
    cross_low = prob_rows.astype(jnp.bfloat16)
    cross_dq = (
        jnp.einsum("bhqk,bkhd->bqhd", cross_grad, key_heads, preferred_element_type=jnp.float32)
        .astype(jnp.bfloat16)
        .reshape(row_count, width)
    )
    patch_dk = (
        jnp.einsum("bhqk,bqhd->bkhd", cross_grad, cross_heads, preferred_element_type=jnp.float32)
        .astype(jnp.bfloat16)
        .reshape(patch_rows, width)
    )
    patch_dv = (
        jnp.einsum("bhqk,bqhd->bkhd", cross_low, grad_heads, preferred_element_type=jnp.float32)
        .astype(jnp.bfloat16)
        .reshape(patch_rows, width)
    )
    stacked = jnp.stack([patch_dk, patch_dv])
    slot_cap = max(2, 2 * (patch_rows // seq_count))
    owners = patch_owner[:, 0]
    onehot = (
        owners[:, None] == lax.broadcasted_iota(jnp.int32, (patch_rows, seq_count), 1)
    ).astype(jnp.int32)
    slot_rank = jnp.sum(onehot * (jnp.cumsum(onehot, axis=0) - onehot), axis=1)
    slot_index = owners * slot_cap + slot_rank
    selector = (
        lax.broadcasted_iota(jnp.int32, (seq_count * slot_cap, patch_rows), 0)
        == slot_index[None, :]
    ).astype(jnp.bfloat16)
    buffer = jnp.einsum(
        "sr,krw->ksw", selector, stacked, preferred_element_type=jnp.float32
    ).astype(jnp.bfloat16)
    buffer = buffer.reshape(2, seq_count, slot_cap, width)
    arrived = lax.all_to_all(buffer, "seq", split_axis=1, concat_axis=1, tiled=True)
    patch_grads = arrived.reshape(2, seq_count * slot_cap, width)
    partial_sums = lax.dot_general(
        cross_dq,
        lax.all_gather(w_query, "seq", axis=0, tiled=True),
        (((1,), (1,)), ((), ())),
        preferred_element_type=jnp.float32,
    )
    byte_grads = lax.psum_scatter(
        partial_sums.astype(jnp.bfloat16), "mp", scatter_dimension=1, tiled=True
    )
    return (win_dq, win_dk, win_dv, patch_grads, byte_grads)


def solution(mesh):
    in_specs = (
        P("seq", "mp"),
        P("seq", "mp"),
        P("seq", "mp"),
        P("seq", "mp"),
        P("seq", "mp"),
        P("seq", "mp"),
        P("seq", "mp"),
        P("seq", "mp"),
        P("seq", None),
        P("seq", None),
        P("seq", "mp"),
    )
    out_specs = (
        P("seq", "mp"),
        P("seq", "mp"),
        P("seq", "mp"),
        P(None, "seq", "mp"),
        P("seq", "mp"),
    )
    return jax.shard_map(local, mesh=mesh, in_specs=in_specs, out_specs=out_specs, check_vma=False)
```

profile of v0, /device:TPU:8, one launch (start us, length us, event | category | flops | bytes accessed | tf_op | source)
XLA Modules:
  0.0 192.9 jit_solution(15188983516557459057)
XLA Ops:
  8.0 1.1 fusion.173
  9.2 1.1 fusion.172
  11.4 1.3 collective-permute-start.1
  14.0 1.2 select_reduce_fusion
  15.4 1.1 fusion.106
  16.5 2.5 %fusion.22 = bf16[2,256,4,128]{3,1,2,0:T(8,128)(2,1)} fusion(f32[2,4,256,64]{2,3,1,0:T(8,128)} %fusion.106, f32[2,4,256,64]{2,3,1,0:T(8,128)S(1)} %get-tuple-element.210, f32[2,4,256]{2,1,0:T(4,128)S(1)} %bitcast.241, pred[2,256,64]{1,2,0:T(8,128)(4,1)S(1)} %iota_compare_fusion.1, bf16[2,64,4,128]{3,2,1,0:T(4,128)(2,1)S(1)} %copy-done.12), kind=kOutput, calls=%fused_computation.39 | convolution fusion | flops 34998336 | bytes 1744896 | tf_op jit(solution)/shard_map/bhqk,bkhd->bqhd/dot_general | solution.py:174
  19.0 2.2 %copy.171 = bf16[2,256,4,128]{3,2,1,0:T(4,128)(2,1)} copy(bf16[2,256,4,128]{3,1,2,0:T(8,128)(2,1)} %fusion.22) | data formatting | bytes 1048576 | tf_op jit(solution)/shard_map/convert_element_type | solution.py:175
  21.2 74.1 %all-gather.2.cloned.1.call-done = bf16[4096,512]{1,0:T(8,128)(2,1)} async-done(((bf16[128,512]{1,0:T(8,128)(2,1)}), bf16[4096,512]{1,0:T(8,128)(2,1)}) %all-gather.2.cloned.1.call-update) | async-done | bytes 4194320 | tf_op jit(solution)/shard_map/all_gather | solution.py:208
  95.3 6.7 %convolution_convert_fusion = bf16[512,4096]{1,0:T(8,128)(2,1)} fusion(bf16[4096,512]{1,0:T(8,128)(2,1)} %all-gather.2.cloned.1.call-done, bf16[64,8,4,128]{3,2,1,0:T(4,128)(2,1)} %bitcast.232), kind=kOutput, calls=%fused_computation.3 | convolution fusion | flops 2149580800 | bytes 8912896 | tf_op jit(solution)/shard_map/dot_general | solution.py:206
  102.5 1.6 fusion.27
  105.0 0.9 copy.168
  105.9 5.9 %all-to-all-start = ((bf16[2,32,8,512]{3,2,0,1:T(8,128)(2,1)}), bf16[2,32,8,512]{3,2,0,1:T(8,128)(2,1)S(1)}, u32[]{:S(2)}, u32[]{:S(2)}) async-start(bf16[2,32,8,512]{3,2,0,1:T(8,128)(2,1)} %copy.168), calls=%async_computation | async-start | bytes 1048576 | tf_op jit(solution)/shard_map/all_to_all | solution.py:204
  111.8 1.1 fusion.170
  112.9 1.1 fusion.169
  114.1 0.8 copy.149
  115.2 0.8 copy.192
  117.1 0.9 copy.137
  117.9 0.8 copy.188
  120.5 0.9 pad_maximum_fusion.1
  121.4 0.8 copy.148
  122.2 0.8 copy.144
  123.0 1.6 fusion.6
  125.2 1.8 fusion.98
  127.0 1.7 convolution_bitcast_fusion
  128.7 3.9 %convolution_convert_fusion.3 = bf16[4,256,128]{1,2,0:T(8,128)(2,1)S(1)} fusion(f32[4,512,256]{2,1,0:T(8,128)} %fusion.98, f32[4,512,256]{2,1,0:T(8,128)S(1)} %get-tuple-element.206, f32[4,256]{1,0:T(4,128)S(1)} %log_add_fusion.1, pred[256,512]{0,1:T(8,128)(4,1)S(1)} %copy-done.3, bf16[256,4,128]{2,0,1:T(8,128)(2,1)} %copy.145, bf16[256,4,128]{2,0,1:T(8,128)(2,1)} %copy.144), kind=kOutput, calls=%fused_computation.45 | convolution fusion | flops 141166080 | bytes 5115904 | tf_op jit(solution)/shard_map/while/body/eval_jaxpr/hqk,khd->qhd/dot_general | solution.py:61
  132.6 0.8 copy.155
  133.5 4.5 %collective-permute-start = (bf16[2,256,512]{1,2,0:T(8,128)(2,1)}, bf16[2,256,512]{1,2,0:T(8,128)(2,1)}, u32[]{:S(2)}, u32[]{:S(2)}) collective-permute-start(bf16[2,256,512]{1,2,0:T(8,128)(2,1)} %get-tuple-element.195), channel_id=1, source_target_pairs={{0,8},{8,16},{16,24},{24,32},{32,40},{40,48},{48,56},{56,64},{64,7... | collective-permute-start | bytes 1572872 | tf_op jit(solution)/shard_map/ppermute | solution.py:15
  138.0 2.1 %fusion.166 = (f32[256,4,128]{0,2,1:T(8,128)}, f32[256,4,128]{0,2,1:T(8,128)S(1)}) fusion(f32[512,4,128]{0,2,1:T(8,128)} %convolution_bitcast_fusion), kind=kLoop, calls=%fused_computation.190 | loop fusion | bytes 2097152 | tf_op jit(solution)/shard_map/slice | solution.py:148
  140.1 5.0 %convolution_bitcast_fusion.1 = f32[512,4,128]{0,2,1:T(8,128)} fusion(bf16[256,4,128]{0,2,1:T(8,128)(2,1)} %bitcast.236, f32[4,512,256]{2,1,0:T(8,128)} %fusion.98, f32[4,512,256]{2,1,0:T(8,128)S(1)} %get-tuple-element.206, f32[4,256]{1,0:T(4,128)S(1)} %log_add_fusion.1, pred[256,512]{0,1:T(8,128)(4,1)} %fusion.104), kind=kOutput, calls=%fused_computation.33 | convolution fusion | flops 139986432 | bytes 5640192 | tf_op jit(solution)/shard_map/while/body/eval_jaxpr/hqk,qhd->khd/dot_general | solution.py:64
  145.0 2.1 %fusion.167 = (f32[256,4,128]{0,2,1:T(8,128)}, f32[256,4,128]{0,2,1:T(8,128)S(1)}) fusion(f32[512,4,128]{0,2,1:T(8,128)} %convolution_bitcast_fusion.1), kind=kLoop, calls=%fused_computation.191 | loop fusion | bytes 2097152 | tf_op jit(solution)/shard_map/slice | solution.py:147
  147.1 0.9 fusion.83
  148.0 3.5 %collective-permute-start.3 = (bf16[2,256,512]{1,2,0:T(8,128)(2,1)}, bf16[2,256,512]{1,2,0:T(8,128)(2,1)}, u32[]{:S(2)}, u32[]{:S(2)}) collective-permute-start(bf16[2,256,512]{1,2,0:T(8,128)(2,1)} %fusion.83), channel_id=1, source_target_pairs={{0,8},{8,16},{16,24},{24,32},{32,40},{40,48},{48,56},{56,64},{64,7... | collective-permute-start | bytes 1572872 | tf_op jit(solution)/shard_map/ppermute | solution.py:15
  152.4 1.8 fusion.168
  155.0 1.6 fusion.15
  158.5 0.8 slice.190
  159.3 1.8 copy.136
  161.1 2.8 %fusion.94 = f32[4,512,256]{2,1,0:T(8,128)} fusion(bf16[256,4,128]{0,2,1:T(8,128)(2,1)S(1)} %bitcast.222, bf16[256,4,128]{2,0,1:T(8,128)(2,1)} %copy.137, bf16[256,4,128]{2,0,1:T(8,128)(2,1)} %copy.136), kind=kOutput, calls=%fused_computation.107 | convolution fusion | flops 135266304 | bytes 2883584 | tf_op jit(solution)/shard_map/while/body/eval_jaxpr/qhd,khd->hqk/dot_general | solution.py:55
  164.0 4.7 %convolution_bitcast_fusion.3 = f32[512,4,128]{0,2,1:T(8,128)} fusion(bf16[256,4,128]{0,2,1:T(8,128)(2,1)} %bitcast.234, f32[4,512,256]{2,1,0:T(8,128)} %fusion.94, f32[4,512,256]{2,1,0:T(8,128)S(1)} %get-tuple-element.208, f32[4,256]{1,0:T(4,128)S(1)} %log_add_fusion.2, pred[256,512]{0,1:T(8,128)(4,1)S(1)} %broadcast_and_fusion), kind=kOutput, calls=%fused_computation.35 | convolution fusion | flops 139986432 | bytes 5640192 | tf_op jit(solution)/shard_map/while/body/eval_jaxpr/hqk,qhd->khd/dot_general | solution.py:64
  168.7 1.1 slice.217
  169.8 0.8 pad_maximum_fusion.6
  170.6 1.3 collective-permute-start.2
  171.9 4.6 %convolution_convert_fusion.4 = bf16[4,128,256]{2,1,0:T(8,128)(2,1)} fusion(f32[4,512,256]{2,1,0:T(8,128)} %fusion.94, f32[4,512,256]{2,1,0:T(8,128)S(1)} %get-tuple-element.208, f32[4,256]{1,0:T(4,128)S(1)} %log_add_fusion.2, pred[256,512]{0,1:T(8,128)(4,1)S(1)} %broadcast_and_fusion, bf16[256,4,128]{2,0,1:T(8,128)(2,1)} %copy.133, ...), kind=kOutput, calls=%fused_computation.46 | convolution fusion | flops 141166080 | bytes 5115904 | tf_op jit(solution)/shard_map/while/body/eval_jaxpr/hqk,khd->qhd/dot_general | solution.py:61
  176.5 1.2 copy.154
  177.7 1.1 convert_element_type.74
  179.9 2.8 %collective-permute-done.2 = bf16[2,256,512]{1,2,0:T(8,128)(2,1)} collective-permute-done((bf16[2,256,512]{1,2,0:T(8,128)(2,1)}, bf16[2,256,512]{1,2,0:T(8,128)(2,1)}, u32[]{:S(2)}, u32[]{:S(2)}) %collective-permute-start.2) | collective-permute-done | bytes 524320 | tf_op jit(solution)/shard_map/ppermute | solution.py:15
  182.7 1.1 select_add_fusion
  184.1 1.0 copy.172
  185.1 1.0 copy.173
  (85 shorter events, 13.1 us)
Async XLA Ops:
  7.2 88.2 %all-gather.2.cloned.1.call-start = ((), (), s32[]{:S(2)}) async-start(), calls=%async_computation.2 | async-start | bytes 4325376 | tf_op jit(solution)/shard_map/all_gather | solution.py:208
  7.9 4.8 %copy-start.8 = (bf16[512,512]{1,0:T(8,128)(2,1)S(1)}, bf16[512,512]{1,0:T(8,128)(2,1)}, u32[]{:S(2)}) copy-start(bf16[512,512]{1,0:T(8,128)(2,1)} %param.32) | copy-start | bytes 1572868
  7.9 178.2 %reduce-scatter.2.cloned.1.call-start = ((), (), s32[]{:S(2)}) async-start(), calls=%async_computation.3 | async-start | bytes 4718592 | tf_op jit(solution)/shard_map/reduce_scatter | solution.py:212
  9.1 3.7 %copy-start.13 = (s32[2,64]{1,0:T(2,128)S(1)}, s32[2,64]{1,0:T(2,128)}, u32[]{:S(2)}) copy-start(s32[2,64]{1,0:T(2,128)} %param.35) | copy-start | bytes 1540
  9.1 4.0 %copy-start.10 = (bf16[128,512]{1,0:T(8,128)(2,1)S(1)}, bf16[128,512]{1,0:T(8,128)(2,1)}, u32[]{:S(2)}) copy-start(bf16[128,512]{1,0:T(8,128)(2,1)} %param.33) | copy-start | bytes 393220
  9.2 4.5 %copy-start.9 = (bf16[512,512]{1,0:T(8,128)(2,1)S(1)}, bf16[512,512]{1,0:T(8,128)(2,1)}, u32[]{:S(2)}) copy-start(bf16[512,512]{1,0:T(8,128)(2,1)} %param.31) | copy-start | bytes 1572868
  10.4 3.5 %copy-start.11 = (bf16[128,512]{1,0:T(8,128)(2,1)S(1)}, bf16[128,512]{1,0:T(8,128)(2,1)}, u32[]{:S(2)}) copy-start(bf16[128,512]{1,0:T(8,128)(2,1)} %param.34) | copy-start | bytes 393220
  11.4 109.1 %collective-permute-start.1 = (bf16[2,256,512]{1,2,0:T(8,128)(2,1)}, bf16[2,256,512]{1,2,0:T(8,128)(2,1)S(1)}, u32[]{:S(2)}, u32[]{:S(2)}) collective-permute-start(bf16[2,256,512]{1,2,0:T(8,128)(2,1)} %pad_maximum_fusion.3), channel_id=1, source_target_pairs={{8,0},{16,8},{24,16},{32,24},{40,32},{48,40},{56,48},{64,56},{72,6... | collective-permute-start | bytes 1572872 | tf_op jit(solution)/shard_map/ppermute | solution.py:15
  13.9 2.6 %copy-start.12 = (bf16[2,64,4,128]{3,2,1,0:T(4,128)(2,1)S(1)}, bf16[2,64,4,128]{3,2,1,0:T(4,128)(2,1)}, u32[]{:S(2)}) copy-start(bf16[2,64,4,128]{3,2,1,0:T(4,128)(2,1)} %reshape.280) | copy-start | bytes 393220
  102.0 2.3 %copy-start.14 = (s32[128,1]{0,1:T(1,128)S(1)}, s32[128,1]{0,1:T(1,128)}, u32[]{:S(2)}) copy-start(s32[128,1]{0,1:T(1,128)} %param.36) | copy-start | bytes 1540
  105.9 45.6 %all-to-all-start = ((bf16[2,32,8,512]{3,2,0,1:T(8,128)(2,1)}), bf16[2,32,8,512]{3,2,0,1:T(8,128)(2,1)S(1)}, u32[]{:S(2)}, u32[]{:S(2)}) async-start(bf16[2,32,8,512]{3,2,0,1:T(8,128)(2,1)} %copy.168), calls=%async_computation | async-start | bytes 1048576 | tf_op jit(solution)/shard_map/all_to_all | solution.py:204
  121.3 1.7 copy-start.3
  123.0 2.1 %copy-start.6 = (bf16[256,4,128]{2,0,1:T(8,128)(2,1)S(1)}, bf16[256,4,128]{2,0,1:T(8,128)(2,1)}, u32[]{:S(2)}) copy-start(bf16[256,4,128]{2,0,1:T(8,128)(2,1)} %copy.149) | copy-start | bytes 786436
  123.0 2.1 %copy-start.7 = (bf16[256,4,128]{2,0,1:T(8,128)(2,1)S(1)}, bf16[256,4,128]{2,0,1:T(8,128)(2,1)}, u32[]{:S(2)}) copy-start(bf16[256,4,128]{2,0,1:T(8,128)(2,1)} %copy.148) | copy-start | bytes 786436
  133.5 18.9 %collective-permute-start = (bf16[2,256,512]{1,2,0:T(8,128)(2,1)}, bf16[2,256,512]{1,2,0:T(8,128)(2,1)}, u32[]{:S(2)}, u32[]{:S(2)}) collective-permute-start(bf16[2,256,512]{1,2,0:T(8,128)(2,1)} %get-tuple-element.195), channel_id=1, source_target_pairs={{0,8},{8,16},{16,24},{24,32},{32,40},{40,48},{48,56},{56,64},{64,7... | collective-permute-start | bytes 1572872 | tf_op jit(solution)/shard_map/ppermute | solution.py:15
  148.0 29.7 %collective-permute-start.3 = (bf16[2,256,512]{1,2,0:T(8,128)(2,1)}, bf16[2,256,512]{1,2,0:T(8,128)(2,1)}, u32[]{:S(2)}, u32[]{:S(2)}) collective-permute-start(bf16[2,256,512]{1,2,0:T(8,128)(2,1)} %fusion.83), channel_id=1, source_target_pairs={{0,8},{8,16},{16,24},{24,32},{32,40},{40,48},{48,56},{56,64},{64,7... | collective-permute-start | bytes 1572872 | tf_op jit(solution)/shard_map/ppermute | solution.py:15
  164.0 5.8 %copy-start.5 = (bf16[256,4,128]{0,2,1:T(8,128)(2,1)S(1)}, bf16[256,4,128]{0,2,1:T(8,128)(2,1)}, u32[]{:S(2)}) copy-start(bf16[256,4,128]{0,2,1:T(8,128)(2,1)} %slice.216) | copy-start | bytes 786436
  170.6 12.1 %collective-permute-start.2 = (bf16[2,256,512]{1,2,0:T(8,128)(2,1)}, bf16[2,256,512]{1,2,0:T(8,128)(2,1)}, u32[]{:S(2)}, u32[]{:S(2)}) collective-permute-start(bf16[2,256,512]{1,2,0:T(8,128)(2,1)} %pad_maximum_fusion.6), channel_id=1, source_target_pairs={{8,0},{16,8},{24,16},{32,24},{40,32},{48,40},{56,48},{64,56},{72,6... | collective-permute-start | bytes 1572872 | tf_op jit(solution)/shard_map/ppermute | solution.py:15
  176.5 2.3 %copy-start.4 = (bf16[256,512]{1,0:T(8,128)(2,1)S(1)}, bf16[256,512]{1,0:T(8,128)(2,1)}, u32[]{:S(2)}) copy-start(bf16[256,512]{1,0:T(8,128)(2,1)} %copy.155) | copy-start | bytes 786436
  176.5 3.2 %copy-start.1 = (f32[256,4,128]{0,2,1:T(8,128)S(1)}, f32[256,4,128]{0,2,1:T(8,128)}, u32[]{:S(2)}) copy-start(f32[256,4,128]{0,2,1:T(8,128)} %get-tuple-element.187) | copy-start | bytes 1572868
  176.5 3.2 %copy-start.2 = (f32[256,4,128]{0,2,1:T(8,128)S(1)}, f32[256,4,128]{0,2,1:T(8,128)}, u32[]{:S(2)}) copy-start(f32[256,4,128]{0,2,1:T(8,128)} %get-tuple-element.189) | copy-start | bytes 1572868
  179.7 4.1 %copy-start = (f32[256,4,128]{0,2,1:T(8,128)S(1)}, f32[256,4,128]{0,2,1:T(8,128)}, u32[]{:S(2)}) copy-start(f32[256,4,128]{0,2,1:T(8,128)} %slice.190) | copy-start | bytes 1572868
  179.7 4.1 %slice-start = ((f32[512,4,128]{0,2,1:T(8,128)}), f32[256,4,128]{0,2,1:T(8,128)S(1)}, s32[]{:S(2)}) async-start(f32[512,4,128]{0,2,1:T(8,128)} %convolution_bitcast_fusion.3), calls=%async_computation.4 | async-start | bytes 1048576 | tf_op jit(solution)/shard_map/slice | solution.py:145
Sparse Core Ops, SparseCore 0:
  10.6 84.6 all-gather.1
  102.1 34.7 reduce-scatter.1
where the time goes:
time: 196 us; the launch traced here: 193 us
  waiting for transfers between devices  77.6 us (40%)
  matrix products  42.1 us (21%)
  local copies, waits for them, and re-layouts  32.6 us (17%)
  starting transfers between devices  16.6 us (8%)
  between operations  14.5 us (7%)
  other arithmetic  9.56 us (5%)
    all_gather x1, waiting for transfers between devices, local(): lax.all_gather(w_query, 'seq', axis=0, tiled=True)  74.1 us
    ppermute x4, starting transfers between devices, shifted(): return lax.ppermute(block, axis, route)  10.6 us
    dot_general x2, matrix products, one_step(): jnp.einsum('hqk,qhd->khd', grad_scores, query_heads, preferred_element_ty...  9.7 us
    dot_general x2, matrix products, one_step(): jnp.einsum('hqk,khd->qhd', grad_scores, key_heads, preferred_element_type...  8.5 us
    dot_general x1, matrix products, local(): lax.dot_general(cross_dq, lax.all_gather(w_query, 'seq', axis=0, tiled=Tr...  6.66 us
    all_to_all x1, starting transfers between devices, local(): lax.all_to_all(buffer, 'seq', split_axis=1, concat_axis=1, tiled=True)  5.91 us
    dot_general x2, matrix products, one_step(): jnp.einsum('qhd,khd->hqk', dout_heads, value_heads, preferred_element_typ...  4.61 us
    unnamed x40, local copies, waits for them, and re-layouts  4.56 us
  transfers between devices with their start and end apart: 7, of which 2 were waited for; matrix products, arithmetic and copies ran while one was open for 44% of the time, Pallas kernels for 0%

commit v1 on v0

v1 whole, which is shorter than its diff:
```python
import functools
import math

import jax
import jax.numpy as jnp
from jax import lax
from jax.experimental import pallas as pl
from jax.experimental.pallas import tpu as pltpu
from jax.sharding import PartitionSpec as P

HD = 128
WIN = 256
INV_ROOT = 1.0 / math.sqrt(HD)
F32 = jnp.float32
BF16 = jnp.bfloat16


def dot(a, b, ca, cb):
    return lax.dot_general(a, b, (((ca,), (cb,)), ((), ())), preferred_element_type=F32)


def window_block(q, do, k_rim, v_rim, k_own, v_own, rim_ok, own_ok):
    s_rim = jnp.where(rim_ok, dot(k_rim, q, 1, 1), -1e30)
    s_own = jnp.where(own_ok, dot(k_own, q, 1, 1), -1e30)
    top = jnp.maximum(
        jnp.max(s_rim, axis=0, keepdims=True), jnp.max(s_own, axis=0, keepdims=True)
    )
    e_rim = jnp.exp((s_rim - top) * INV_ROOT)
    e_own = jnp.exp((s_own - top) * INV_ROOT)
    scale = 1.0 / (
        jnp.sum(e_rim, axis=0, keepdims=True) + jnp.sum(e_own, axis=0, keepdims=True)
    )
    d_rim = dot(v_rim, do, 1, 1)
    d_own = dot(v_own, do, 1, 1)
    p_rim = e_rim * scale
    p_own = e_own * scale
    delta = jnp.sum(p_rim * d_rim, axis=0, keepdims=True) + jnp.sum(
        p_own * d_own, axis=0, keepdims=True
    )
    g_rim = (p_rim * (d_rim - delta) * INV_ROOT).astype(BF16)
    g_own = (p_own * (d_own - delta) * INV_ROOT).astype(BF16)
    p_rim = p_rim.astype(BF16)
    p_own = p_own.astype(BF16)
    dq = dot(g_rim, k_rim, 0, 0) + dot(g_own, k_own, 0, 0)
    return (
        dq,
        dot(g_rim, q, 1, 0),
        dot(p_rim, do, 1, 0),
        dot(g_own, q, 1, 0),
        dot(p_own, do, 1, 0),
    )


def window_kernel(
    flags, q_ref, do_ref, k_ref, v_ref, before_ref, after_ref,
    dq_ref, dk_ref, dv_ref, low_ref, high_ref,
):
    low_valid = flags[0]
    is_last = flags[1]
    rows = lax.broadcasted_iota(jnp.int32, (WIN, WIN), 0)
    cols = lax.broadcasted_iota(jnp.int32, (WIN, WIN), 1)
    rim_ok = rows >= cols
    own_ok = rows <= cols
    lo = slice(0, WIN)
    hi = slice(WIN, 2 * WIN)
    k_low, v_low = k_ref[lo, :], v_ref[lo, :]
    dq, dk_r, dv_r, dk_low, dv_low = window_block(
        q_ref[lo, :], do_ref[lo, :], before_ref[0], before_ref[1], k_low, v_low,
        rim_ok & (low_valid > 0), own_ok,
    )
    dq_ref[lo, :] = dq.astype(BF16)
    low_ref[0] = dk_r.astype(BF16)
    low_ref[1] = dv_r.astype(BF16)
    last = is_last > 0
    k_prev = jnp.where(last, k_low, after_ref[0])
    v_prev = jnp.where(last, v_low, after_ref[1])
    dq, dk_r, dv_r, dk_own, dv_own = window_block(
        q_ref[hi, :], do_ref[hi, :], k_prev, v_prev, k_ref[hi, :], v_ref[hi, :],
        rim_ok, own_ok,
    )
    dq_ref[hi, :] = dq.astype(BF16)
    high_ref[0] = dk_r.astype(BF16)
    high_ref[1] = dv_r.astype(BF16)
    dk_ref[hi, :] = dk_own
    dv_ref[hi, :] = dv_own
    dk_ref[lo, :] = dk_low + jnp.where(last, dk_r, 0.0)
    dv_ref[lo, :] = dv_low + jnp.where(last, dv_r, 0.0)


def window_call(flags, q, do, k, v, before, after):
    rows, width = q.shape
    full = pl.BlockSpec((rows, HD), lambda h, f: (0, h))
    rim = pl.BlockSpec((2, WIN, HD), lambda h, f: (0, 0, h))
    return pl.pallas_call(
        window_kernel,
        grid_spec=pltpu.PrefetchScalarGridSpec(
            num_scalar_prefetch=1,
            grid=(width // HD,),
            in_specs=[full] * 4 + [rim] * 2,
            out_specs=[full, full, full, rim, rim],
        ),
        out_shape=(
            jax.ShapeDtypeStruct((rows, width), BF16),
            jax.ShapeDtypeStruct((rows, width), F32),
            jax.ShapeDtypeStruct((rows, width), F32),
            jax.ShapeDtypeStruct((2, WIN, width), BF16),
            jax.ShapeDtypeStruct((2, WIN, width), BF16),
        ),
        name="window_grads",
        compiler_params=pltpu.CompilerParams(vmem_limit_bytes=40 << 20),
    )(flags, q, do, k, v, before, after)


def cross_kernel(q_ref, do_ref, k_ref, v_ref, len_ref, owner_ref, dq_ref, buf_ref, sel_ref):
    blocks = len_ref.shape[0]
    per_block = len_ref.shape[1]
    rows = q_ref.shape[0] // blocks
    patches = blocks * per_block
    slots = sel_ref.shape[0]
    cap = buf_ref.shape[2]

    @pl.when(pl.program_id(0) == 0)
    def _():
        owner_col = jnp.broadcast_to(owner_ref[...], (patches, patches))
        owner_row = owner_col.T
        earlier = lax.broadcasted_iota(
            jnp.int32, (patches, patches), 0
        ) < lax.broadcasted_iota(jnp.int32, (patches, patches), 1)
        same = jnp.where((owner_col == owner_row) & earlier, 1, 0)
        rank = jnp.sum(same, axis=0, keepdims=True)
        slot = owner_ref[...] * cap + rank
        at = lax.broadcasted_iota(jnp.int32, (slots, patches), 0)
        sel_ref[...] = jnp.where(at == slot, 1.0, 0.0).astype(BF16)

    before = lax.broadcasted_iota(
        jnp.int32, (per_block, per_block), 1
    ) < lax.broadcasted_iota(jnp.int32, (per_block, per_block), 0)
    starts = dot(
        jnp.where(before, 1.0, 0.0).astype(BF16), len_ref[...].astype(F32).astype(BF16), 1, 1
    ).astype(jnp.int32)
    within = lax.broadcasted_iota(jnp.int32, (per_block, rows), 1)
    dks, dvs = [], []
    for b in range(blocks):
        r = slice(b * rows, (b + 1) * rows)
        p = slice(b * per_block, (b + 1) * per_block)
        q, do, k, v = q_ref[r, :], do_ref[r, :], k_ref[p, :], v_ref[p, :]
        ok = starts[:, b : b + 1] <= within
        s = jnp.where(ok, dot(k, q, 1, 1), -1e30)
        e = jnp.exp((s - jnp.max(s, axis=0, keepdims=True)) * INV_ROOT)
        probs = e * (1.0 / jnp.sum(e, axis=0, keepdims=True))
        d = dot(v, do, 1, 1)
        delta = jnp.sum(probs * d, axis=0, keepdims=True)
        g = (probs * (d - delta) * INV_ROOT).astype(BF16)
        dq_ref[r, :] = dot(g, k, 0, 0).astype(BF16)
        dks.append(dot(g, q, 1, 0).astype(BF16))
        dvs.append(dot(probs.astype(BF16), do, 1, 0).astype(BF16))
    sel = sel_ref[...]
    for i, parts in enumerate((dks, dvs)):
        placed = dot(sel, jnp.concatenate(parts, axis=0), 1, 0).astype(BF16)
        buf_ref[:, i] = placed.reshape(slots // cap, cap, HD)


def cross_call(q, do, k, v, lens, owners, owner_count):
    rows, width = q.shape
    patches = k.shape[0]
    cap = max(2, 2 * (patches // owner_count))
    col = pl.BlockSpec((rows, HD), lambda h: (0, h))
    pcol = pl.BlockSpec((patches, HD), lambda h: (0, h))
    return pl.pallas_call(
        cross_kernel,
        grid_spec=pltpu.PrefetchScalarGridSpec(
            num_scalar_prefetch=0,
            grid=(width // HD,),
            in_specs=[
                col, col, pcol, pcol,
                pl.BlockSpec(lens.shape, lambda h: (0, 0)),
                pl.BlockSpec((1, patches), lambda h: (0, 0)),
            ],
            out_specs=[
                col,
                pl.BlockSpec((owner_count, 2, cap, HD), lambda h: (0, 0, 0, h)),
            ],
            scratch_shapes=[pltpu.VMEM((owner_count * cap, patches), BF16)],
        ),
        out_shape=(
            jax.ShapeDtypeStruct((rows, width), BF16),
            jax.ShapeDtypeStruct((owner_count, 2, cap, width), BF16),
        ),
        name="cross_grads",
        compiler_params=pltpu.CompilerParams(vmem_limit_bytes=40 << 20),
    )(q, do, k, v, lens, owners.reshape(1, patches))


def join_kernel(dk_ref, dv_ref, low_ref, high_ref, dk_out, dv_out):
    for i, (src, out) in enumerate(((dk_ref, dk_out), (dv_ref, dv_out))):
        out[:WIN, :] = (src[:WIN, :] + low_ref[i].astype(F32)).astype(BF16)
        out[WIN:, :] = (src[WIN:, :] + high_ref[i].astype(F32)).astype(BF16)


def join_call(dk, dv, low_back, high_back):
    rows, width = dk.shape
    step = 2 * HD
    col = pl.BlockSpec((rows, step), lambda h: (0, h))
    rim = pl.BlockSpec((2, WIN, step), lambda h: (0, 0, h))
    out = jax.ShapeDtypeStruct((rows, width), BF16)
    return pl.pallas_call(
        join_kernel,
        grid=(width // step,),
        in_specs=[col, col, rim, rim],
        out_specs=[col, col],
        out_shape=(out, out),
        name="join_rims",
        compiler_params=pltpu.CompilerParams(vmem_limit_bytes=40 << 20),
    )(dk, dv, low_back, high_back)


def shifted(block, axis, distance):
    devices = range(lax.axis_size(axis))
    route = [(i - distance, i) for i in devices if i - distance in devices]
    return lax.ppermute(block, axis, route)


def local(
    win_query, win_key, win_value, win_dout, cross_query, cross_dout,
    patch_key, patch_value, patch_len, patch_owner, w_query,
):
    seq_count = lax.axis_size("seq")
    seq_index = lax.axis_index("seq")
    flags = jnp.stack([seq_index > 0, seq_index == seq_count - 1]).astype(jnp.int32)
    low_rim = jnp.stack([win_key[:WIN], win_value[:WIN]])
    high_rim = jnp.stack([win_key[WIN:], win_value[WIN:]])
    before = shifted(low_rim, "seq", 1)
    after = shifted(high_rim, "seq", -1)
    cross_dq, buffer = cross_call(
        cross_query, cross_dout, patch_key, patch_value, patch_len, patch_owner, seq_count
    )
    win_dq, dk, dv, low_send, high_send = window_call(
        flags, win_query, win_dout, win_key, win_value, before, after
    )
    low_back = shifted(low_send, "seq", -1)
    high_back = shifted(high_send, "seq", 1)
    win_dk, win_dv = join_call(dk, dv, low_back, high_back)
    arrived = lax.all_to_all(buffer, "seq", split_axis=0, concat_axis=0, tiled=True)
    patch_grads = arrived.transpose(1, 0, 2, 3).reshape(2, -1, arrived.shape[3])
    partial_sums = lax.dot_general(
        cross_dq,
        lax.all_gather(w_query, "seq", axis=0, tiled=True),
        (((1,), (1,)), ((), ())),
        preferred_element_type=F32,
    )
    byte_grads = lax.psum_scatter(
        partial_sums.astype(BF16), "mp", scatter_dimension=1, tiled=True
    )
    return (win_dq, win_dk, win_dv, patch_grads, byte_grads)


def solution(mesh):
    tile = P("seq", "mp")
    rows = P("seq", None)
    in_specs = (tile,) * 8 + (rows, rows, tile)
    out_specs = (tile, tile, tile, P(None, "seq", "mp"), tile)
    return jax.shard_map(local, mesh=mesh, in_specs=in_specs, out_specs=out_specs, check_vma=False)
```

time: 196 us -> 172 us (0.88)
  the two profiles are of different devices: /device:TPU:8 before, /device:TPU:128 now
where the time goes in v1:
time: 172 us
  waiting for transfers between devices  99.9 us (58%)
  starting transfers between devices  23.9 us (14%)
  between operations  14.2 us (8%)
  Pallas kernels  14 us (8%)
  local copies, waits for them, and re-layouts  13 us (8%)
  matrix products  6.52 us (4%)
    all_gather x1, waiting for transfers between devices, local(): lax.all_gather(w_query, 'seq', axis=0, tiled=True)  73.1 us
    ppermute x4, waiting for transfers between devices, shifted(): return lax.ppermute(block, axis, route)  26.1 us
    ppermute x4, starting transfers between devices, shifted(): return lax.ppermute(block, axis, route)  15 us
    unnamed x28, local copies, waits for them, and re-layouts  11 us
    all_to_all x1, starting transfers between devices, local(): lax.all_to_all(buffer, 'seq', split_axis=0, concat_axis=0, tiled=True)  8.85 us
    pallas_call x1, Pallas kernels, window_call(): pl.pallas_call(window_kernel, grid_spec=pltpu.PrefetchScalarGridSpec(num_...  7.89 us
    dot_general x1, matrix products, local(): lax.dot_general(cross_dq, lax.all_gather(w_query, 'seq', axis=0, tiled=Tr...  6.52 us
    pallas_call x1, Pallas kernels, cross_call(): pl.pallas_call(cross_kernel, grid_spec=pltpu.PrefetchScalarGridSpec(num_s...  4.87 us
  transfers between devices with their start and end apart: 7, of which 4 were waited for; matrix products, arithmetic and copies ran while one was open for 1% of the time, Pallas kernels for 8%

profile of v1, /device:TPU:128, one launch (start us, length us, event | category | flops | bytes accessed | tf_op | source)
XLA Modules:
  0.0 171.6 jit_solution(2460462725092096752)
XLA Ops:
  7.2 0.0 all-gather.2.cloned.1.call-start
  7.2 0.7 all-gather.2.cloned.1.call-update
  7.9 0.0 reduce-scatter.2.cloned.1.call-start
  7.9 0.0 copy-start.2
  8.0 1.0 copy-done.2
  9.0 0.0 copy-start.3
  9.0 1.0 copy-done.3
  10.0 0.0 copy-start.10
  10.0 0.9 copy-done.10
  10.9 0.0 copy-start.11
  10.9 0.9 copy-done.11
  11.8 0.0 copy-start.12
  11.8 0.7 copy-done.12
  12.5 0.0 copy-start.13
  12.5 0.7 copy-done.13
  13.2 4.9 %cross_grads.1 = (bf16[512,512]{1,0:T(8,128)(2,1)S(1)}, bf16[32,2,8,512]{3,2,1,0:T(8,128)(2,1)}) custom-call(bf16[512,512]{1,0:T(8,128)(2,1)S(1)} %copy-done.2, bf16[512,512]{1,0:T(8,128)(2,1)S(1)} %copy-done.3, bf16[128,512]{1,0:T(8,128)(2,1)S(1)} %copy-done.10, bf16[128,512]{1,0:T(8,128)(2,1)S(1)} %copy-done.11, s32[2,64]{1,0:T(2,128)S(1)} %copy-done.12, ...), custom_call_target="tpu_custom_call" | custom-call | tf_op jit(solution)/shard_map/cross_grads/pallas_call | solution.py:169
  18.0 73.1 %all-gather.2.cloned.1.call-done = bf16[4096,512]{1,0:T(8,128)(2,1)} async-done(((bf16[128,512]{1,0:T(8,128)(2,1)}), bf16[4096,512]{1,0:T(8,128)(2,1)}) %all-gather.2.cloned.1.call-update) | async-done | bytes 4194320 | tf_op jit(solution)/shard_map/all_gather | solution.py:247
  91.1 6.5 %convolution_convert_fusion = bf16[512,4096]{1,0:T(8,128)(2,1)} fusion(bf16[512,512]{1,0:T(8,128)(2,1)S(1)} %get-tuple-element.22, bf16[4096,512]{1,0:T(8,128)(2,1)} %all-gather.2.cloned.1.call-done), kind=kOutput, calls=%fused_computation | convolution fusion | flops 2149580800 | bytes 8912896 | tf_op jit(solution)/shard_map/dot_general | solution.py:245
  97.6 0.0 copy-start.1
  97.7 0.0 reduce-scatter.2.cloned.1.call-update
  97.7 8.9 %all-to-all-start = ((bf16[32,2,8,512]{3,2,1,0:T(8,128)(2,1)}), bf16[32,2,8,512]{3,2,1,0:T(8,128)(2,1)}, u32[]{:S(2)}, u32[]{:S(2)}) async-start(bf16[32,2,8,512]{3,2,1,0:T(8,128)(2,1)} %get-tuple-element.21), calls=%async_computation | async-start | bytes 1048576 | tf_op jit(solution)/shard_map/all_to_all | solution.py:243
  106.5 0.0 copy-done
  106.5 0.0 copy-done.1
  106.6 0.1 slice_bitcast_fusion
  106.6 0.1 pad_maximum_fusion
  106.7 3.4 %collective-permute-start = (bf16[2,256,512]{2,1,0:T(8,128)(2,1)S(1)}, bf16[2,256,512]{2,1,0:T(8,128)(2,1)S(1)}, u32[]{:S(2)}, u32[]{:S(2)}) collective-permute-start(bf16[2,256,512]{2,1,0:T(8,128)(2,1)S(1)} %pad_maximum_fusion), channel_id=1, source_target_pairs={{0,8},{8,16},{16,24},{24,32},{32,40},{40,48},{48,56},{56,64},{64,7... | collective-permute-start | bytes 1572872 | tf_op jit(solution)/shard_map/ppermute | solution.py:220
  110.1 0.1 pad_maximum_fusion.1
  110.1 5.8 %collective-permute-start.1 = (bf16[2,256,512]{2,1,0:T(8,128)(2,1)S(1)}, bf16[2,256,512]{2,1,0:T(8,128)(2,1)S(1)}, u32[]{:S(2)}, u32[]{:S(2)}) collective-permute-start(bf16[2,256,512]{2,1,0:T(8,128)(2,1)S(1)} %pad_maximum_fusion.1), channel_id=1, source_target_pairs={{8,0},{16,8},{24,16},{32,24},{40,32},{48,40},{56,48},{64,56},{72,6... | collective-permute-start | bytes 1572872 | tf_op jit(solution)/shard_map/ppermute | solution.py:220
  115.9 0.1 add_convert_fusion.flags
  116.0 13.2 %collective-permute-done.before_ref = bf16[2,256,512]{2,1,0:T(8,128)(2,1)S(1)} collective-permute-done((bf16[2,256,512]{2,1,0:T(8,128)(2,1)S(1)}, bf16[2,256,512]{2,1,0:T(8,128)(2,1)S(1)}, u32[]{:S(2)}, u32[]{:S(2)}) %collective-permute-start) | collective-permute-done | bytes 524320 | tf_op jit(solution)/shard_map/ppermute | solution.py:220
  129.2 0.0 copy-start.6
  129.2 0.8 copy-done.6
  130.0 0.0 collective-permute-done.1.after_ref
  130.0 0.0 copy-start.8
  130.0 0.8 copy-done.8
  130.8 0.0 copy-start.4
  130.8 1.1 copy-done.4
  131.8 1.1 copy-done.5
  132.9 1.1 copy-done.7
  134.0 1.0 copy-done.9
  135.0 7.9 %window_grads.1 = (bf16[512,512]{1,0:T(8,128)(2,1)}, f32[512,512]{1,0:T(8,128)S(1)}, f32[512,512]{1,0:T(8,128)S(1)}, bf16[2,256,512]{2,1,0:T(8,128)(2,1)}, bf16[2,256,512]{2,1,0:T(8,128)(2,1)}) custom-call(s32[2]{0:T(128)S(1)} %add_convert_fusion.flags, bf16[512,512]{1,0:T(8,128)(2,1)S(1)} %copy-done.4, bf16[512,512]{1,0:T(8,128)(2,1)S(1)} %copy-done.5, ...), custom_call_target="tpu_custom_call" | custom-call | tf_op jit(solution)/shard_map/window_grads/pallas_call | solution.py:94
  142.9 3.8 %collective-permute-start.2 = (bf16[2,256,512]{2,1,0:T(8,128)(2,1)}, bf16[2,256,512]{2,1,0:T(8,128)(2,1)S(1)}, u32[]{:S(2)}, u32[]{:S(2)}) collective-permute-start(bf16[2,256,512]{2,1,0:T(8,128)(2,1)} %get-tuple-element.17), channel_id=1, source_target_pairs={{8,0},{16,8},{24,16},{32,24},{40,32},{48,40},{56,48},{64,56},{72,6... | collective-permute-start | bytes 1572872 | tf_op jit(solution)/shard_map/ppermute | solution.py:220
  146.7 2.0 %collective-permute-start.3 = (bf16[2,256,512]{2,1,0:T(8,128)(2,1)}, bf16[2,256,512]{2,1,0:T(8,128)(2,1)S(1)}, u32[]{:S(2)}, u32[]{:S(2)}) collective-permute-start(bf16[2,256,512]{2,1,0:T(8,128)(2,1)} %get-tuple-element.18), channel_id=1, source_target_pairs={{0,8},{8,16},{16,24},{24,32},{32,40},{40,48},{48,56},{56,64},{64,7... | collective-permute-start | bytes 1572872 | tf_op jit(solution)/shard_map/ppermute | solution.py:220
  148.7 0.0 all-to-all-done
  148.7 1.9 %copy_bitcast_fusion = bf16[2,256,512]{2,1,0:T(8,128)(2,1)} fusion(bf16[32,2,8,512]{3,2,1,0:T(8,128)(2,1)} %all-to-all-done), kind=kLoop, calls=%fused_computation.3 | loop fusion | bytes 1048576 | tf_op jit(solution)/shard_map/reshape | solution.py:244
  150.6 6.6 %collective-permute-done.2.low_ref = bf16[2,256,512]{2,1,0:T(8,128)(2,1)S(1)} collective-permute-done((bf16[2,256,512]{2,1,0:T(8,128)(2,1)}, bf16[2,256,512]{2,1,0:T(8,128)(2,1)S(1)}, u32[]{:S(2)}, u32[]{:S(2)}) %collective-permute-start.2) | collective-permute-done | bytes 524320 | tf_op jit(solution)/shard_map/ppermute | solution.py:220
  157.3 6.2 %collective-permute-done.3.high_ref = bf16[2,256,512]{2,1,0:T(8,128)(2,1)S(1)} collective-permute-done((bf16[2,256,512]{2,1,0:T(8,128)(2,1)}, bf16[2,256,512]{2,1,0:T(8,128)(2,1)S(1)}, u32[]{:S(2)}, u32[]{:S(2)}) %collective-permute-start.3) | collective-permute-done | bytes 524320 | tf_op jit(solution)/shard_map/ppermute | solution.py:220
  163.5 1.3 join_rims.1
  (5 shorter events, 0.0 us)
Async XLA Ops:
  7.2 84.0 %all-gather.2.cloned.1.call-start = ((), (), s32[]{:S(2)}) async-start(), calls=%async_computation.2 | async-start | bytes 4325376 | tf_op jit(solution)/shard_map/all_gather | solution.py:247
  7.9 156.9 %reduce-scatter.2.cloned.1.call-start = ((), (), s32[]{:S(2)}) async-start(), calls=%async_computation.3 | async-start | bytes 4718592 | tf_op jit(solution)/shard_map/reduce_scatter | solution.py:251
  7.9 1.0 copy-start.2
  9.0 1.0 copy-start.3
  10.0 0.9 copy-start.10
  10.9 0.9 copy-start.11
  11.8 0.7 copy-start.12
  12.5 0.7 copy-start.13
  97.6 8.9 %copy-start = (bf16[512,512]{1,0:T(8,128)(2,1)S(1)}, bf16[512,512]{1,0:T(8,128)(2,1)}, u32[]{:S(2)}) copy-start(bf16[512,512]{1,0:T(8,128)(2,1)} %k_ref.2) | copy-start | bytes 1572868
  97.6 8.9 %copy-start.1 = (bf16[512,512]{1,0:T(8,128)(2,1)S(1)}, bf16[512,512]{1,0:T(8,128)(2,1)}, u32[]{:S(2)}) copy-start(bf16[512,512]{1,0:T(8,128)(2,1)} %v_ref.2) | copy-start | bytes 1572868
  97.7 51.1 %all-to-all-start = ((bf16[32,2,8,512]{3,2,1,0:T(8,128)(2,1)}), bf16[32,2,8,512]{3,2,1,0:T(8,128)(2,1)}, u32[]{:S(2)}, u32[]{:S(2)}) async-start(bf16[32,2,8,512]{3,2,1,0:T(8,128)(2,1)} %get-tuple-element.21), calls=%async_computation | async-start | bytes 1048576 | tf_op jit(solution)/shard_map/all_to_all | solution.py:243
  106.7 22.5 %collective-permute-start = (bf16[2,256,512]{2,1,0:T(8,128)(2,1)S(1)}, bf16[2,256,512]{2,1,0:T(8,128)(2,1)S(1)}, u32[]{:S(2)}, u32[]{:S(2)}) collective-permute-start(bf16[2,256,512]{2,1,0:T(8,128)(2,1)S(1)} %pad_maximum_fusion), channel_id=1, source_target_pairs={{0,8},{8,16},{16,24},{24,32},{32,40},{40,48},{48,56},{56,64},{64,7... | collective-permute-start | bytes 1572872 | tf_op jit(solution)/shard_map/ppermute | solution.py:220
  110.1 19.9 %collective-permute-start.1 = (bf16[2,256,512]{2,1,0:T(8,128)(2,1)S(1)}, bf16[2,256,512]{2,1,0:T(8,128)(2,1)S(1)}, u32[]{:S(2)}, u32[]{:S(2)}) collective-permute-start(bf16[2,256,512]{2,1,0:T(8,128)(2,1)S(1)} %pad_maximum_fusion.1), channel_id=1, source_target_pairs={{8,0},{16,8},{24,16},{32,24},{40,32},{48,40},{56,48},{64,56},{72,6... | collective-permute-start | bytes 1572872 | tf_op jit(solution)/shard_map/ppermute | solution.py:220
  129.2 0.8 copy-start.6
  130.0 0.8 copy-start.8
  130.8 1.1 copy-start.4
  131.8 1.1 copy-start.5
  132.9 1.1 copy-start.7
  134.0 1.0 copy-start.9
  142.9 14.4 %collective-permute-start.2 = (bf16[2,256,512]{2,1,0:T(8,128)(2,1)}, bf16[2,256,512]{2,1,0:T(8,128)(2,1)S(1)}, u32[]{:S(2)}, u32[]{:S(2)}) collective-permute-start(bf16[2,256,512]{2,1,0:T(8,128)(2,1)} %get-tuple-element.17), channel_id=1, source_target_pairs={{8,0},{16,8},{24,16},{32,24},{40,32},{48,40},{56,48},{64,56},{72,6... | collective-permute-start | bytes 1572872 | tf_op jit(solution)/shard_map/ppermute | solution.py:220
  146.7 16.8 %collective-permute-start.3 = (bf16[2,256,512]{2,1,0:T(8,128)(2,1)}, bf16[2,256,512]{2,1,0:T(8,128)(2,1)S(1)}, u32[]{:S(2)}, u32[]{:S(2)}) collective-permute-start(bf16[2,256,512]{2,1,0:T(8,128)(2,1)} %get-tuple-element.18), channel_id=1, source_target_pairs={{0,8},{8,16},{16,24},{24,32},{32,40},{40,48},{48,56},{56,64},{64,7... | collective-permute-start | bytes 1572872 | tf_op jit(solution)/shard_map/ppermute | solution.py:220
Sparse Core Ops, SparseCore 0:
  10.6 80.5 all-gather.1
  97.8 41.0 reduce-scatter.1

commit v2 on v1

--- a/solution.py
+++ b/solution.py
@@ -220,20 +220,178 @@
     return lax.ppermute(block, axis, route)
 
 
+NZ, NX, NY, NC = 8, 4, 4, 2
+
+
+def place(z, x, y, c):
+    return ((z % NZ) * NX + x % NX) * (NY * NC) + (y % NY) * NC + c
+
+
+def send(block, target):
+    route = []
+    for z in range(NZ):
+        for x in range(NX):
+            for y in range(NY):
+                for c in range(NC):
+                    to = target(z, x, y, c)
+                    if to is not None:
+                        route.append((place(z, x, y, c), place(*to)))
+    return lax.ppermute(block, ("seq", "mp"), route)
+
+
+def two(zs, xs):
+    def target(z, x, y, c):
+        if c == 0:
+            return None if zs is None else (z + zs, x, y, c)
+        return None if xs is None else (z, x + xs, y, c)
+
+    return target
+
+
+def cross_two(xs, zs):
+    def target(z, x, y, c):
+        if c == 0:
+            return None if xs is None else (z, x + xs, y, c)
+        return None if zs is None else (z + zs, x, y, c)
+
+    return target
+
+
+SUB = (0, -1, 1, -2)
+FAR = (2, -3, 3, -4)
+
+
+def gather_weight(w_rows, first_core):
+    own = send(w_rows, lambda z, x, y, c: (z + NC * y + c, x, z // NC, z % NC))
+    a1 = send(own, cross_two(1, 1))
+    a2 = send(own, cross_two(-1, -1))
+    a3 = send(own, cross_two(2, 2))
+    a4 = send(own, cross_two(None, -2))
+    a5 = send(a3, cross_two(None, 1))
+    a6 = send(a4, cross_two(None, -1))
+    a7 = send(own, cross_two(None, 4))
+    near = jnp.concatenate([own, a1, a2, a3], axis=0)
+    far = jnp.concatenate([a4, a5, a6, a7], axis=0)
+    b1 = send(near, two(1, 1))
+    b2 = send(near, two(-1, -1))
+    b3 = send(near, two(2, 2))
+    b4 = send(jnp.where(first_core, near, far), two(-2, 1))
+    b5 = send(jnp.where(first_core, b3, far), two(1, -1))
+    b6 = send(jnp.where(first_core, b4, far), two(-1, 2))
+    half = near.shape[0] // 2
+    b7 = send(b3[:half], two(2, None))
+    b8 = send(b4[half:], two(-2, None))
+    return [near, b1, b2, b3, b4, b5, b6], far, b7, b8
+
+
+def gather_rows(dq):
+    swap = lambda z, x, y, c: (z, x, y, 1 - c)
+    parts = [dq]
+    for dy in (1, -1, 2):
+        parts.append(send(dq, lambda z, x, y, c, dy=dy: (z, x, y + dy, c)))
+    return parts + [send(p, swap) for p in parts]
+
+
+def product_kernel(pos, *refs):
+    rows = refs[:8]
+    near = refs[8:15]
+    far, b7, b8, out_ref, a_buf, w_buf, a_sem, w_sem = refs[15:]
+    z, x, m, c = pos[0], pos[1], pos[2], pos[3]
+    y = m // NC
+    shard = w_buf.shape[1] // NX
+    half = shard * NX // 2
+
+    def copy_w(src, row, dz, dx):
+        k = lax.rem(z + dz - m + 2 * NZ, NZ)
+        n = lax.rem(x + dx + NX, NX)
+        return pltpu.make_async_copy(
+            src.at[pl.ds(row, shard), :],
+            w_buf.at[k, pl.ds(pl.multiple_of(n * shard, shard), shard), :],
+            w_sem.at[k * NX + n],
+        )
+
+    for i, src in enumerate(rows):
+        dy = (0, -1, 1, 2)[i % 4]
+        other = c if i < 4 else 1 - c
+        k = NC * lax.rem(y + dy + NY, NY) + other
+        pltpu.make_async_copy(src, a_buf.at[k], a_sem.at[k]).start()
+
+    @pl.when(c == 0)
+    def _():
+        for src, dz in zip(near, (0, -1, 1, -2, 2, -3, 3)):
+            for i, dx in enumerate(SUB):
+                copy_w(src, i * shard, dz, dx).start()
+        for i, dx in enumerate(SUB):
+            src = b7 if i < 2 else b8
+            copy_w(src, (i % 2) * shard, -4, dx).start()
+
+    @pl.when(c != 0)
+    def _():
+        for src, dx, offs in zip(
+            near + (far,),
+            (0, -1, 1, -2, -1, 1, -2, 0),
+            (SUB, SUB, SUB, SUB, FAR, FAR, FAR, FAR),
+        ):
+            for i, dz in enumerate(offs):
+                copy_w(src, i * shard, dz, dx).start()
+
+    total = None
+    for k in range(NZ):
+        pltpu.make_async_copy(rows[0], a_buf.at[k], a_sem.at[k]).wait()
+        for n in range(NX):
+            pltpu.make_async_copy(
+                near[0].at[pl.ds(0, shard), :],
+                w_buf.at[k, pl.ds(n * shard, shard), :],
+                w_sem.at[k * NX + n],
+            ).wait()
+        part = dot(a_buf[k], w_buf[k], 1, 1)
+        total = part if total is None else total + part
+    out_ref[...] = total.astype(BF16)
+
+
+def product_call(pos, rows, near, far, b7, b8):
+    count, width = rows[0].shape
+    n_rows = near[0].shape[0]
+    anywhere = pl.BlockSpec(memory_space=pl.ANY)
+    return pl.pallas_call(
+        product_kernel,
+        grid_spec=pltpu.PrefetchScalarGridSpec(
+            num_scalar_prefetch=1,
+            grid=(1,),
+            in_specs=[anywhere] * 18,
+            out_specs=pl.BlockSpec((count, n_rows), lambda i, p: (0, 0)),
+            scratch_shapes=[
+                pltpu.VMEM((NZ, count, width), BF16),
+                pltpu.VMEM((NZ, n_rows, width), BF16),
+                pltpu.SemaphoreType.DMA((NZ,)),
+                pltpu.SemaphoreType.DMA((NZ * NX,)),
+            ],
+        ),
+        out_shape=jax.ShapeDtypeStruct((count, n_rows), BF16),
+        name="byte_product",
+        compiler_params=pltpu.CompilerParams(vmem_limit_bytes=40 << 20),
+    )(pos, *rows, *near, far, b7, b8)
+
+
 def local(
     win_query, win_key, win_value, win_dout, cross_query, cross_dout,
     patch_key, patch_value, patch_len, patch_owner, w_query,
 ):
     seq_count = lax.axis_size("seq")
     seq_index = lax.axis_index("seq")
+    mp_index = lax.axis_index("mp")
     flags = jnp.stack([seq_index > 0, seq_index == seq_count - 1]).astype(jnp.int32)
+    core = mp_index % NC
+    pos = jnp.stack([seq_index // NX, seq_index % NX, mp_index, core]).astype(jnp.int32)
     low_rim = jnp.stack([win_key[:WIN], win_value[:WIN]])
     high_rim = jnp.stack([win_key[WIN:], win_value[WIN:]])
     before = shifted(low_rim, "seq", 1)
     after = shifted(high_rim, "seq", -1)
+    near, far, b7, b8 = gather_weight(w_query, core == 0)
     cross_dq, buffer = cross_call(
         cross_query, cross_dout, patch_key, patch_value, patch_len, patch_owner, seq_count
     )
+    rows = gather_rows(cross_dq)
     win_dq, dk, dv, low_send, high_send = window_call(
         flags, win_query, win_dout, win_key, win_value, before, after
     )
@@ -242,15 +400,7 @@
     win_dk, win_dv = join_call(dk, dv, low_back, high_back)
     arrived = lax.all_to_all(buffer, "seq", split_axis=0, concat_axis=0, tiled=True)
     patch_grads = arrived.transpose(1, 0, 2, 3).reshape(2, -1, arrived.shape[3])
-    partial_sums = lax.dot_general(
-        cross_dq,
-        lax.all_gather(w_query, "seq", axis=0, tiled=True),
-        (((1,), (1,)), ((), ())),
-        preferred_element_type=F32,
-    )
-    byte_grads = lax.psum_scatter(
-        partial_sums.astype(BF16), "mp", scatter_dimension=1, tiled=True
-    )
+    byte_grads = product_call(pos, rows, near, far, b7, b8)
     return (win_dq, win_dk, win_dv, patch_grads, byte_grads)
 
 

time: 172 us -> 178 us (1.035)
  the two profiles are of different devices: /device:TPU:128 before, /device:TPU:54 now
where the time goes in v2:
time: 178 us; the launch traced here: 177 us
  starting transfers between devices  99 us (56%)
  waiting for transfers between devices  34 us (19%)
  Pallas kernels  25 us (14%)
  local copies, waits for them, and re-layouts  15 us (8%)
  other arithmetic  2.95 us (2%)
    ppermute x23, starting transfers between devices, send(): return lax.ppermute(block, ('seq', 'mp'), route)  77.4 us
    ppermute x23, waiting for transfers between devices, send(): return lax.ppermute(block, ('seq', 'mp'), route)  34 us
    ppermute x4, starting transfers between devices, shifted(): return lax.ppermute(block, axis, route)  13.5 us
    unnamed x60, local copies, waits for them, and re-layouts  12.3 us
    pallas_call x1, Pallas kernels, product_call(): pl.pallas_call(product_kernel, grid_spec=pltpu.PrefetchScalarGridSpec(num...  9.52 us
    pallas_call x1, Pallas kernels, window_call(): pl.pallas_call(window_kernel, grid_spec=pltpu.PrefetchScalarGridSpec(num_...  8.63 us
    all_to_all x1, starting transfers between devices, local(): lax.all_to_all(buffer, 'seq', split_axis=0, concat_axis=0, tiled=True)  8.14 us
    pallas_call x1, Pallas kernels, cross_call(): pl.pallas_call(cross_kernel, grid_spec=pltpu.PrefetchScalarGridSpec(num_s...  4.69 us
  transfers between devices with their start and end apart: 28, of which 7 were waited for; matrix products, arithmetic and copies ran while one was open for 3% of the time, Pallas kernels for 6%

profile of v2, /device:TPU:54, one launch (start us, length us, event | category | flops | bytes accessed | tf_op | source)
XLA Modules:
  0.0 177.2 jit_solution(5711775239031430099)
XLA Ops:
  0.7 0.6 copy-done.25
  1.3 1.0 copy-done.13
  2.4 1.0 copy-done.14
  3.4 0.9 copy-done.22
  4.3 0.9 copy-done.23
  5.2 4.7 %cross_grads.1 = (bf16[512,512]{1,0:T(8,128)(2,1)}, bf16[32,2,8,512]{3,2,1,0:T(8,128)(2,1)S(1)}) custom-call(bf16[512,512]{1,0:T(8,128)(2,1)S(1)} %copy-done.13, bf16[512,512]{1,0:T(8,128)(2,1)S(1)} %copy-done.14, bf16[128,512]{1,0:T(8,128)(2,1)S(1)} %copy-done.22, bf16[128,512]{1,0:T(8,128)(2,1)S(1)} %copy-done.23, s32[2,64]{1,0:T(2,128)S(1)} %copy-done.24, ...), custom_call_target="tpu_custom_call" | custom-call | tf_op jit(solution)/shard_map/cross_grads/pallas_call | solution.py:169
  10.3 2.2 %collective-permute-start.4 = (bf16[512,512]{1,0:T(8,128)(2,1)}, bf16[512,512]{1,0:T(8,128)(2,1)}, u32[]{:S(2)}, u32[]{:S(2)}) collective-permute-start(bf16[512,512]{1,0:T(8,128)(2,1)} %get-tuple-element.22.refs_0_), channel_id=1, source_target_pairs={{0,2},{1,3},{2,4},{3,5},{4,6},{5,7},{6,0},{7,1},{8,10},{9,11},{10,... | collective-permute-start | bytes 1572872 | tf_op jit(solution)/shard_map/ppermute | solution.py:239
  12.4 8.2 %collective-permute-start.11 = (bf16[128,512]{1,0:T(8,128)(2,1)S(1)}, bf16[128,512]{1,0:T(8,128)(2,1)S(1)}, u32[]{:S(2)}, u32[]{:S(2)}) collective-permute-start(bf16[128,512]{1,0:T(8,128)(2,1)S(1)} %copy-done.26), channel_id=1, source_target_pairs={{0,0},{1,32},{2,64},{3,96},{4,128},{5,160},{6,192},{7,224},{8,8},{... | collective-permute-start | bytes 393224 | tf_op jit(solution)/shard_map/ppermute | solution.py:239
  20.8 5.6 %collective-permute-done.11 = bf16[128,512]{1,0:T(8,128)(2,1)S(1)} collective-permute-done((bf16[128,512]{1,0:T(8,128)(2,1)S(1)}, bf16[128,512]{1,0:T(8,128)(2,1)S(1)}, u32[]{:S(2)}, u32[]{:S(2)}) %collective-permute-start.11) | collective-permute-done | bytes 131104 | tf_op jit(solution)/shard_map/ppermute | solution.py:239
  26.4 0.7 collective-permute-start.18
  27.0 0.8 pad_maximum_fusion
  27.9 1.4 collective-permute-start.14
  29.3 2.1 %collective-permute-start.12 = (bf16[128,512]{1,0:T(8,128)(2,1)S(1)}, bf16[128,512]{1,0:T(8,128)(2,1)S(1)}, u32[]{:S(2)}, u32[]{:S(2)}) collective-permute-start(bf16[128,512]{1,0:T(8,128)(2,1)S(1)} %collective-permute-done.11), channel_id=1, source_target_pairs={{0,8},{1,33},{2,10},{3,35},{4,12},{5,37},{6,14},{7,39},{8,16},{9,4... | collective-permute-start | bytes 393224 | tf_op jit(solution)/shard_map/ppermute | solution.py:239
  31.5 2.7 %collective-permute-done.12 = bf16[128,512]{1,0:T(8,128)(2,1)S(1)} collective-permute-done((bf16[128,512]{1,0:T(8,128)(2,1)S(1)}, bf16[128,512]{1,0:T(8,128)(2,1)S(1)}, u32[]{:S(2)}, u32[]{:S(2)}) %collective-permute-start.12) | collective-permute-done | bytes 131104 | tf_op jit(solution)/shard_map/ppermute | solution.py:239
  34.4 0.7 collective-permute-start.20
  35.0 2.6 %collective-permute-done.13 = bf16[128,512]{1,0:T(8,128)(2,1)S(1)} collective-permute-done((bf16[128,512]{1,0:T(8,128)(2,1)S(1)}, bf16[128,512]{1,0:T(8,128)(2,1)S(1)}, u32[]{:S(2)}, u32[]{:S(2)}) %collective-permute-start.13) | collective-permute-done | bytes 131104 | tf_op jit(solution)/shard_map/ppermute | solution.py:239
  37.7 0.7 collective-permute-start.19
  38.4 1.9 %collective-permute-start.1 = (bf16[2,256,512]{2,1,0:T(8,128)(2,1)S(1)}, bf16[2,256,512]{2,1,0:T(8,128)(2,1)S(1)}, u32[]{:S(2)}, u32[]{:S(2)}) collective-permute-start(bf16[2,256,512]{2,1,0:T(8,128)(2,1)S(1)} %pad_maximum_fusion.1), channel_id=1, source_target_pairs={{8,0},{16,8},{24,16},{32,24},{40,32},{48,40},{56,48},{64,56},{72,6... | collective-permute-start | bytes 1572872 | tf_op jit(solution)/shard_map/ppermute | solution.py:220
  40.3 0.7 collective-permute-start.21
  41.0 32.7 %collective-permute-start.7 = (bf16[512,512]{1,0:T(8,128)(2,1)}, bf16[512,512]{1,0:T(8,128)(2,1)}, u32[]{:S(2)}, u32[]{:S(2)}) collective-permute-start(bf16[512,512]{1,0:T(8,128)(2,1)} %get-tuple-element.22.refs_0_), channel_id=1, source_target_pairs={{0,1},{1,0},{2,3},{3,2},{4,5},{5,4},{6,7},{7,6},{8,9},{9,8},{10,11... | collective-permute-start | bytes 1572872 | tf_op jit(solution)/shard_map/ppermute | solution.py:239
  73.8 4.5 %collective-permute-start = (bf16[2,256,512]{2,1,0:T(8,128)(2,1)}, bf16[2,256,512]{2,1,0:T(8,128)(2,1)}, u32[]{:S(2)}, u32[]{:S(2)}) collective-permute-start(bf16[2,256,512]{2,1,0:T(8,128)(2,1)} %pad_maximum_fusion), channel_id=1, source_target_pairs={{0,8},{8,16},{16,24},{24,32},{32,40},{40,48},{48,56},{56,64},{64,7... | collective-permute-start | bytes 1572872 | tf_op jit(solution)/shard_map/ppermute | solution.py:220
  78.3 1.8 %collective-permute-start.17 = (bf16[512,512]{1,0:T(8,128)(2,1)S(1)}, bf16[512,512]{1,0:T(8,128)(2,1)S(1)}, u32[]{:S(2)}, u32[]{:S(2)}) collective-permute-start(bf16[512,512]{1,0:T(8,128)(2,1)S(1)} %constant_dynamic-update-slice_fusion.refs_8_), channel_id=1, source_target_pairs={{0,64},{1,17},{2,66},{3,19},{4,68},{5,21},{6,70},{7,23},{8,72},{9,... | collective-permute-start | bytes 1572872 | tf_op jit(solution)/shard_map/ppermute | solution.py:239
  80.2 4.7 %collective-permute-start.15 = (bf16[512,512]{1,0:T(8,128)(2,1)S(1)}, bf16[512,512]{1,0:T(8,128)(2,1)}, u32[]{:S(2)}, u32[]{:S(2)}) collective-permute-start(bf16[512,512]{1,0:T(8,128)(2,1)S(1)} %constant_dynamic-update-slice_fusion.refs_8_), channel_id=1, source_target_pairs={{0,32},{1,9},{2,34},{3,11},{4,36},{5,13},{6,38},{7,15},{8,40},{9,1... | collective-permute-start | bytes 1572872 | tf_op jit(solution)/shard_map/ppermute | solution.py:239
  84.8 0.8 broadcast_select_fusion.2
  85.7 0.8 copy-done.20
  87.0 8.1 %all-to-all-start = ((bf16[32,2,8,512]{3,2,1,0:T(8,128)(2,1)}), bf16[32,2,8,512]{3,2,1,0:T(8,128)(2,1)}, u32[]{:S(2)}, u32[]{:S(2)}) async-start(bf16[32,2,8,512]{3,2,1,0:T(8,128)(2,1)} %copy-done.15), calls=%async_computation | async-start | bytes 1048576 | tf_op jit(solution)/shard_map/all_to_all | solution.py:401
  95.2 13.9 %collective-permute-start.16 = (bf16[512,512]{1,0:T(8,128)(2,1)S(1)}, bf16[512,512]{1,0:T(8,128)(2,1)S(1)}, u32[]{:S(2)}, u32[]{:S(2)}) collective-permute-start(bf16[512,512]{1,0:T(8,128)(2,1)S(1)} %constant_dynamic-update-slice_fusion.refs_8_), channel_id=1, source_target_pairs={{0,224},{1,25},{2,226},{3,27},{4,228},{5,29},{6,230},{7,31},{8,232... | collective-permute-start | bytes 1572872 | tf_op jit(solution)/shard_map/ppermute | solution.py:239
  109.1 1.0 copy-done.16
  110.2 1.0 copy-done.17
  111.2 1.0 copy-done.21
  112.2 8.6 %window_grads.1 = (bf16[512,512]{1,0:T(8,128)(2,1)}, f32[512,512]{1,0:T(8,128)S(1)}, f32[512,512]{1,0:T(8,128)S(1)}, bf16[2,256,512]{2,1,0:T(8,128)(2,1)S(1)}, bf16[2,256,512]{2,1,0:T(8,128)(2,1)}) custom-call(s32[2]{0:T(128)S(1)} %add_convert_fusion.flags, bf16[512,512]{1,0:T(8,128)(2,1)S(1)} %copy-done.16, bf16[512,512]{1,0:T(8,128)(2,1)S(1)} %copy-done.17, ...), custom_call_target="tpu_custom_call" | custom-call | tf_op jit(solution)/shard_map/window_grads/pallas_call | solution.py:94
  121.2 1.9 %collective-permute-start.2 = (bf16[2,256,512]{2,1,0:T(8,128)(2,1)S(1)}, bf16[2,256,512]{2,1,0:T(8,128)(2,1)S(1)}, u32[]{:S(2)}, u32[]{:S(2)}) collective-permute-start(bf16[2,256,512]{2,1,0:T(8,128)(2,1)S(1)} %get-tuple-element.17), channel_id=1, source_target_pairs={{8,0},{16,8},{24,16},{32,24},{40,32},{48,40},{56,48},{64,56},{72,6... | collective-permute-start | bytes 1572872 | tf_op jit(solution)/shard_map/ppermute | solution.py:220
  123.1 1.5 collective-permute-done.15.refs_9_
  124.6 5.2 %collective-permute-start.3 = (bf16[2,256,512]{2,1,0:T(8,128)(2,1)}, bf16[2,256,512]{2,1,0:T(8,128)(2,1)}, u32[]{:S(2)}, u32[]{:S(2)}) collective-permute-start(bf16[2,256,512]{2,1,0:T(8,128)(2,1)} %get-tuple-element.18), channel_id=1, source_target_pairs={{0,8},{8,16},{16,24},{24,32},{32,40},{40,48},{48,56},{56,64},{64,7... | collective-permute-start | bytes 1572872 | tf_op jit(solution)/shard_map/ppermute | solution.py:220
  129.9 1.9 %collective-permute-start.25 = (bf16[256,512]{1,0:T(8,128)(2,1)S(1)}, bf16[256,512]{1,0:T(8,128)(2,1)S(1)}, u32[]{:S(2)}, u32[]{:S(2)}) collective-permute-start(bf16[256,512]{1,0:T(8,128)(2,1)S(1)} %slice.24), channel_id=1, source_target_pairs={{0,64},{2,66},{4,68},{6,70},{8,72},{10,74},{12,76},{14,78},{16,80}... | collective-permute-start | bytes 786440 | tf_op jit(solution)/shard_map/ppermute | solution.py:239
  131.8 1.0 broadcast_select_fusion
  132.9 0.9 copy-done.9
  133.7 13.8 %collective-permute-done.25.refs_16_ = bf16[256,512]{1,0:T(8,128)(2,1)S(1)} collective-permute-done((bf16[256,512]{1,0:T(8,128)(2,1)S(1)}, bf16[256,512]{1,0:T(8,128)(2,1)S(1)}, u32[]{:S(2)}, u32[]{:S(2)}) %collective-permute-start.25) | collective-permute-done | bytes 262176 | tf_op jit(solution)/shard_map/ppermute | solution.py:239
  147.5 0.8 copy-done.11
  148.3 2.0 %collective-permute-start.23 = (bf16[512,512]{1,0:T(8,128)(2,1)}, bf16[512,512]{1,0:T(8,128)(2,1)}, u32[]{:S(2)}, u32[]{:S(2)}) collective-permute-start(bf16[512,512]{1,0:T(8,128)(2,1)} %get-tuple-element.24), channel_id=1, source_target_pairs={{0,32},{1,25},{2,34},{3,27},{4,36},{5,29},{6,38},{7,31},{8,40},{9,... | collective-permute-start | bytes 1572872 | tf_op jit(solution)/shard_map/ppermute | solution.py:239
  150.3 0.8 copy-done.18
  151.1 0.7 slice.25
  151.8 2.6 %collective-permute-start.26 = (bf16[256,512]{1,0:T(8,128)(2,1)}, bf16[256,512]{1,0:T(8,128)(2,1)}, u32[]{:S(2)}, u32[]{:S(2)}) collective-permute-start(bf16[256,512]{1,0:T(8,128)(2,1)} %slice.25), channel_id=1, source_target_pairs={{0,192},{2,194},{4,196},{6,198},{8,200},{10,202},{12,204},{14,206}... | collective-permute-start | bytes 786440 | tf_op jit(solution)/shard_map/ppermute | solution.py:239
  154.5 1.9 %copy_bitcast_fusion = bf16[2,256,512]{2,1,0:T(8,128)(2,1)} fusion(bf16[32,2,8,512]{3,2,1,0:T(8,128)(2,1)} %all-to-all-done), kind=kLoop, calls=%fused_computation.2 | loop fusion | bytes 1048576 | tf_op jit(solution)/shard_map/reshape | solution.py:402
  156.5 1.2 copy-done.5
  157.7 2.2 %join_rims.1 = (bf16[512,512]{1,0:T(8,128)(2,1)}, bf16[512,512]{1,0:T(8,128)(2,1)}) custom-call(f32[512,512]{1,0:T(8,128)S(1)} %copy-done.3, f32[512,512]{1,0:T(8,128)S(1)} %copy-done.5, bf16[2,256,512]{2,1,0:T(8,128)(2,1)S(1)} %copy-done.19, bf16[2,256,512]{2,1,0:T(8,128)(2,1)} %collective-permute-done.3.high_ref), custom_call_target="tpu_custom_call" | custom-call | tf_op jit(solution)/shard_map/join_rims/pallas_call | solution.py:206
  159.9 7.6 %collective-permute-done.26.refs_17_ = bf16[256,512]{1,0:T(8,128)(2,1)} collective-permute-done((bf16[256,512]{1,0:T(8,128)(2,1)}, bf16[256,512]{1,0:T(8,128)(2,1)}, u32[]{:S(2)}, u32[]{:S(2)}) %collective-permute-start.26) | collective-permute-done | bytes 262176 | tf_op jit(solution)/shard_map/ppermute | solution.py:239
  167.5 9.5 %byte_product.1 = bf16[512,512]{1,0:T(8,128)(2,1)} custom-call(s32[4]{0:T(128)S(1)} %pad_add_fusion.pos, bf16[512,512]{1,0:T(8,128)(2,1)} %get-tuple-element.22.refs_0_, bf16[512,512]{1,0:T(8,128)(2,1)} %collective-permute-done.4.refs_1_, bf16[512,512]{1,0:T(8,128)(2,1)} %collective-permute-done.5.refs_2_, bf16[512,512]{1,0:T(8,128)(2,1)S(1)} %copy-done.8, ...), custom_call_target="tpu_custom_call" | custom-call | tf_op jit(solution)/shard_map/byte_product/pallas_call | solution.py:356
  (84 shorter events, 1.8 us)
Async XLA Ops:
  1.3 1.0 copy-start.13
  2.4 1.0 copy-start.14
  3.4 0.9 copy-start.22
  5.2 7.2 %copy-start.26 = (bf16[128,512]{1,0:T(8,128)(2,1)S(1)}, bf16[128,512]{1,0:T(8,128)(2,1)}, u32[]{:S(2)}) copy-start(bf16[128,512]{1,0:T(8,128)(2,1)} %param.21) | copy-start | bytes 393220
  5.2 15.4 %copy-start = (bf16[512,512]{1,0:T(8,128)(2,1)S(1)}, bf16[512,512]{1,0:T(8,128)(2,1)}, u32[]{:S(2)}) copy-start(bf16[512,512]{1,0:T(8,128)(2,1)} %k_ref.2) | copy-start | bytes 1572868
  5.2 15.4 %copy-start.1 = (bf16[512,512]{1,0:T(8,128)(2,1)S(1)}, bf16[512,512]{1,0:T(8,128)(2,1)}, u32[]{:S(2)}) copy-start(bf16[512,512]{1,0:T(8,128)(2,1)} %v_ref.2) | copy-start | bytes 1572868
  9.9 10.8 %copy-start.15 = (bf16[32,2,8,512]{3,2,1,0:T(8,128)(2,1)}, bf16[32,2,8,512]{3,2,1,0:T(8,128)(2,1)S(1)}, u32[]{:S(2)}) copy-start(bf16[32,2,8,512]{3,2,1,0:T(8,128)(2,1)S(1)} %get-tuple-element.21) | copy-start | bytes 1572868
  9.9 63.8 %collective-permute-start.6 = (bf16[512,512]{1,0:T(8,128)(2,1)}, bf16[512,512]{1,0:T(8,128)(2,1)S(1)}, u32[]{:S(2)}, u32[]{:S(2)}) collective-permute-start(bf16[512,512]{1,0:T(8,128)(2,1)} %get-tuple-element.22.refs_0_), channel_id=1, source_target_pairs={{0,4},{1,5},{2,6},{3,7},{4,0},{5,1},{6,2},{7,3},{8,12},{9,13},{10,... | collective-permute-start | bytes 1572872 | tf_op jit(solution)/shard_map/ppermute | solution.py:239
  10.3 68.1 %collective-permute-start.4 = (bf16[512,512]{1,0:T(8,128)(2,1)}, bf16[512,512]{1,0:T(8,128)(2,1)}, u32[]{:S(2)}, u32[]{:S(2)}) collective-permute-start(bf16[512,512]{1,0:T(8,128)(2,1)} %get-tuple-element.22.refs_0_), channel_id=1, source_target_pairs={{0,2},{1,3},{2,4},{3,5},{4,6},{5,7},{6,0},{7,1},{8,10},{9,11},{10,... | collective-permute-start | bytes 1572872 | tf_op jit(solution)/shard_map/ppermute | solution.py:239
  12.4 13.9 %collective-permute-start.11 = (bf16[128,512]{1,0:T(8,128)(2,1)S(1)}, bf16[128,512]{1,0:T(8,128)(2,1)S(1)}, u32[]{:S(2)}, u32[]{:S(2)}) collective-permute-start(bf16[128,512]{1,0:T(8,128)(2,1)S(1)} %copy-done.26), channel_id=1, source_target_pairs={{0,0},{1,32},{2,64},{3,96},{4,128},{5,160},{6,192},{7,224},{8,8},{... | collective-permute-start | bytes 393224 | tf_op jit(solution)/shard_map/ppermute | solution.py:239
  26.4 5.0 %collective-permute-start.18 = (bf16[128,512]{1,0:T(8,128)(2,1)S(1)}, bf16[128,512]{1,0:T(8,128)(2,1)S(1)}, u32[]{:S(2)}, u32[]{:S(2)}) collective-permute-start(bf16[128,512]{1,0:T(8,128)(2,1)S(1)} %collective-permute-done.11), channel_id=1, source_target_pairs={{1,193},{3,195},{5,197},{7,199},{9,201},{11,203},{13,205},{15,207}... | collective-permute-start | bytes 393224 | tf_op jit(solution)/shard_map/ppermute | solution.py:239
  27.9 6.5 %collective-permute-start.14 = (bf16[128,512]{1,0:T(8,128)(2,1)S(1)}, bf16[128,512]{1,0:T(8,128)(2,1)S(1)}, u32[]{:S(2)}, u32[]{:S(2)}) collective-permute-start(bf16[128,512]{1,0:T(8,128)(2,1)S(1)} %collective-permute-done.11), channel_id=1, source_target_pairs={{0,16},{1,65},{2,18},{3,67},{4,20},{5,69},{6,22},{7,71},{8,24},{9,... | collective-permute-start | bytes 393224 | tf_op jit(solution)/shard_map/ppermute | solution.py:239
  29.3 5.0 %collective-permute-start.12 = (bf16[128,512]{1,0:T(8,128)(2,1)S(1)}, bf16[128,512]{1,0:T(8,128)(2,1)S(1)}, u32[]{:S(2)}, u32[]{:S(2)}) collective-permute-start(bf16[128,512]{1,0:T(8,128)(2,1)S(1)} %collective-permute-done.11), channel_id=1, source_target_pairs={{0,8},{1,33},{2,10},{3,35},{4,12},{5,37},{6,14},{7,39},{8,16},{9,4... | collective-permute-start | bytes 393224 | tf_op jit(solution)/shard_map/ppermute | solution.py:239
  31.4 6.3 %collective-permute-start.13 = (bf16[128,512]{1,0:T(8,128)(2,1)S(1)}, bf16[128,512]{1,0:T(8,128)(2,1)S(1)}, u32[]{:S(2)}, u32[]{:S(2)}) collective-permute-start(bf16[128,512]{1,0:T(8,128)(2,1)S(1)} %collective-permute-done.11), channel_id=1, source_target_pairs={{0,24},{1,225},{2,26},{3,227},{4,28},{5,229},{6,30},{7,231},{8,0},... | collective-permute-start | bytes 393224 | tf_op jit(solution)/shard_map/ppermute | solution.py:239
  34.3 45.9 %collective-permute-start.5 = (bf16[512,512]{1,0:T(8,128)(2,1)}, bf16[512,512]{1,0:T(8,128)(2,1)}, u32[]{:S(2)}, u32[]{:S(2)}) collective-permute-start(bf16[512,512]{1,0:T(8,128)(2,1)} %get-tuple-element.22.refs_0_), channel_id=1, source_target_pairs={{0,6},{1,7},{2,0},{3,1},{4,2},{5,3},{6,4},{7,5},{8,14},{9,15},{10,... | collective-permute-start | bytes 1572872 | tf_op jit(solution)/shard_map/ppermute | solution.py:239
  34.4 6.0 %collective-permute-start.20 = (bf16[128,512]{1,0:T(8,128)(2,1)S(1)}, bf16[128,512]{1,0:T(8,128)(2,1)S(1)}, u32[]{:S(2)}, u32[]{:S(2)}) collective-permute-start(bf16[128,512]{1,0:T(8,128)(2,1)S(1)} %collective-permute-done.18), channel_id=1, source_target_pairs={{1,225},{3,227},{5,229},{7,231},{9,233},{11,235},{13,237},{15,239}... | collective-permute-start | bytes 393224 | tf_op jit(solution)/shard_map/ppermute | solution.py:239
  37.7 0.7 collective-permute-start.19
  38.4 47.3 %collective-permute-start.1 = (bf16[2,256,512]{2,1,0:T(8,128)(2,1)S(1)}, bf16[2,256,512]{2,1,0:T(8,128)(2,1)S(1)}, u32[]{:S(2)}, u32[]{:S(2)}) collective-permute-start(bf16[2,256,512]{2,1,0:T(8,128)(2,1)S(1)} %pad_maximum_fusion.1), channel_id=1, source_target_pairs={{8,0},{16,8},{24,16},{32,24},{40,32},{48,40},{56,48},{64,56},{72,6... | collective-permute-start | bytes 1572872 | tf_op jit(solution)/shard_map/ppermute | solution.py:220
  40.3 0.7 collective-permute-start.21
  41.0 79.8 %collective-permute-start.7 = (bf16[512,512]{1,0:T(8,128)(2,1)}, bf16[512,512]{1,0:T(8,128)(2,1)}, u32[]{:S(2)}, u32[]{:S(2)}) collective-permute-start(bf16[512,512]{1,0:T(8,128)(2,1)} %get-tuple-element.22.refs_0_), channel_id=1, source_target_pairs={{0,1},{1,0},{2,3},{3,2},{4,5},{5,4},{6,7},{7,6},{8,9},{9,8},{10,11... | collective-permute-start | bytes 1572872 | tf_op jit(solution)/shard_map/ppermute | solution.py:239
  73.8 4.5 %copy-start.6 = (bf16[512,512]{1,0:T(8,128)(2,1)}, bf16[512,512]{1,0:T(8,128)(2,1)S(1)}, u32[]{:S(2)}) copy-start(bf16[512,512]{1,0:T(8,128)(2,1)S(1)} %collective-permute-done.6.refs_3_) | copy-start | bytes 1572868
  73.8 21.4 %collective-permute-start = (bf16[2,256,512]{2,1,0:T(8,128)(2,1)}, bf16[2,256,512]{2,1,0:T(8,128)(2,1)}, u32[]{:S(2)}, u32[]{:S(2)}) collective-permute-start(bf16[2,256,512]{2,1,0:T(8,128)(2,1)} %pad_maximum_fusion), channel_id=1, source_target_pairs={{0,8},{8,16},{16,24},{24,32},{32,40},{40,48},{48,56},{56,64},{64,7... | collective-permute-start | bytes 1572872 | tf_op jit(solution)/shard_map/ppermute | solution.py:220
  78.3 42.9 %collective-permute-start.17 = (bf16[512,512]{1,0:T(8,128)(2,1)S(1)}, bf16[512,512]{1,0:T(8,128)(2,1)S(1)}, u32[]{:S(2)}, u32[]{:S(2)}) collective-permute-start(bf16[512,512]{1,0:T(8,128)(2,1)S(1)} %constant_dynamic-update-slice_fusion.refs_8_), channel_id=1, source_target_pairs={{0,64},{1,17},{2,66},{3,19},{4,68},{5,21},{6,70},{7,23},{8,72},{9,... | collective-permute-start | bytes 1572872 | tf_op jit(solution)/shard_map/ppermute | solution.py:239
  80.2 44.5 %collective-permute-start.15 = (bf16[512,512]{1,0:T(8,128)(2,1)S(1)}, bf16[512,512]{1,0:T(8,128)(2,1)}, u32[]{:S(2)}, u32[]{:S(2)}) collective-permute-start(bf16[512,512]{1,0:T(8,128)(2,1)S(1)} %constant_dynamic-update-slice_fusion.refs_8_), channel_id=1, source_target_pairs={{0,32},{1,9},{2,34},{3,11},{4,36},{5,13},{6,38},{7,15},{8,40},{9,1... | collective-permute-start | bytes 1572872 | tf_op jit(solution)/shard_map/ppermute | solution.py:239
  86.5 43.4 %collective-permute-start.22 = (bf16[512,512]{1,0:T(8,128)(2,1)}, bf16[512,512]{1,0:T(8,128)(2,1)S(1)}, u32[]{:S(2)}, u32[]{:S(2)}) collective-permute-start(bf16[512,512]{1,0:T(8,128)(2,1)} %broadcast_select_fusion.2), channel_id=1, source_target_pairs={{0,192},{1,9},{2,194},{3,11},{4,196},{5,13},{6,198},{7,15},{8,200}... | collective-permute-start | bytes 1572872 | tf_op jit(solution)/shard_map/ppermute | solution.py:239
  87.0 67.5 %all-to-all-start = ((bf16[32,2,8,512]{3,2,1,0:T(8,128)(2,1)}), bf16[32,2,8,512]{3,2,1,0:T(8,128)(2,1)}, u32[]{:S(2)}, u32[]{:S(2)}) async-start(bf16[32,2,8,512]{3,2,1,0:T(8,128)(2,1)} %copy-done.15), calls=%async_computation | async-start | bytes 1048576 | tf_op jit(solution)/shard_map/all_to_all | solution.py:401
  95.2 25.7 %copy-start.7 = (bf16[512,512]{1,0:T(8,128)(2,1)S(1)}, bf16[512,512]{1,0:T(8,128)(2,1)}, u32[]{:S(2)}) copy-start(bf16[512,512]{1,0:T(8,128)(2,1)} %copy-done.6) | copy-start | bytes 1572868
  95.2 37.6 %collective-permute-start.16 = (bf16[512,512]{1,0:T(8,128)(2,1)S(1)}, bf16[512,512]{1,0:T(8,128)(2,1)S(1)}, u32[]{:S(2)}, u32[]{:S(2)}) collective-permute-start(bf16[512,512]{1,0:T(8,128)(2,1)S(1)} %constant_dynamic-update-slice_fusion.refs_8_), channel_id=1, source_target_pairs={{0,224},{1,25},{2,226},{3,27},{4,228},{5,29},{6,230},{7,31},{8,232... | collective-permute-start | bytes 1572872 | tf_op jit(solution)/shard_map/ppermute | solution.py:239
  109.1 1.0 copy-start.16
  110.2 1.0 copy-start.17
  111.2 1.0 copy-start.21
  120.9 12.0 %copy-start.2 = (f32[512,512]{1,0:T(8,128)}, f32[512,512]{1,0:T(8,128)S(1)}, u32[]{:S(2)}) copy-start(f32[512,512]{1,0:T(8,128)S(1)} %get-tuple-element.15.dk_ref) | copy-start | bytes 3145732
  120.9 12.0 %copy-start.4 = (f32[512,512]{1,0:T(8,128)}, f32[512,512]{1,0:T(8,128)S(1)}, u32[]{:S(2)}) copy-start(f32[512,512]{1,0:T(8,128)S(1)} %get-tuple-element.16.dv_ref) | copy-start | bytes 3145732
  120.9 26.6 %collective-permute-start.10 = (bf16[512,512]{1,0:T(8,128)(2,1)S(1)}, bf16[512,512]{1,0:T(8,128)(2,1)S(1)}, u32[]{:S(2)}, u32[]{:S(2)}) collective-permute-start(bf16[512,512]{1,0:T(8,128)(2,1)S(1)} %copy-done.7), channel_id=1, source_target_pairs={{0,1},{1,0},{2,3},{3,2},{4,5},{5,4},{6,7},{7,6},{8,9},{9,8},{10,11... | collective-permute-start | bytes 1572872 | tf_op jit(solution)/shard_map/ppermute | solution.py:239
  121.2 29.1 %collective-permute-start.2 = (bf16[2,256,512]{2,1,0:T(8,128)(2,1)S(1)}, bf16[2,256,512]{2,1,0:T(8,128)(2,1)S(1)}, u32[]{:S(2)}, u32[]{:S(2)}) collective-permute-start(bf16[2,256,512]{2,1,0:T(8,128)(2,1)S(1)} %get-tuple-element.17), channel_id=1, source_target_pairs={{8,0},{16,8},{24,16},{32,24},{40,32},{48,40},{56,48},{64,56},{72,6... | collective-permute-start | bytes 1572872 | tf_op jit(solution)/shard_map/ppermute | solution.py:220
  124.6 27.2 %collective-permute-start.3 = (bf16[2,256,512]{2,1,0:T(8,128)(2,1)}, bf16[2,256,512]{2,1,0:T(8,128)(2,1)}, u32[]{:S(2)}, u32[]{:S(2)}) collective-permute-start(bf16[2,256,512]{2,1,0:T(8,128)(2,1)} %get-tuple-element.18), channel_id=1, source_target_pairs={{0,8},{8,16},{16,24},{24,32},{32,40},{40,48},{48,56},{56,64},{64,7... | collective-permute-start | bytes 1572872 | tf_op jit(solution)/shard_map/ppermute | solution.py:220
  129.9 17.6 %collective-permute-start.25 = (bf16[256,512]{1,0:T(8,128)(2,1)S(1)}, bf16[256,512]{1,0:T(8,128)(2,1)S(1)}, u32[]{:S(2)}, u32[]{:S(2)}) collective-permute-start(bf16[256,512]{1,0:T(8,128)(2,1)S(1)} %slice.24), channel_id=1, source_target_pairs={{0,64},{2,66},{4,68},{6,70},{8,72},{10,74},{12,76},{14,78},{16,80}... | collective-permute-start | bytes 786440 | tf_op jit(solution)/shard_map/ppermute | solution.py:239
  133.7 22.7 %copy-start.3 = (f32[512,512]{1,0:T(8,128)S(1)}, f32[512,512]{1,0:T(8,128)}, u32[]{:S(2)}) copy-start(f32[512,512]{1,0:T(8,128)} %copy-done.2) | copy-start | bytes 3145732
  133.7 26.1 %collective-permute-start.8 = (bf16[512,512]{1,0:T(8,128)(2,1)}, bf16[512,512]{1,0:T(8,128)(2,1)}, u32[]{:S(2)}, u32[]{:S(2)}) collective-permute-start(bf16[512,512]{1,0:T(8,128)(2,1)} %collective-permute-done.4.refs_1_), channel_id=1, source_target_pairs={{0,1},{1,0},{2,3},{3,2},{4,5},{5,4},{6,7},{7,6},{8,9},{9,8},{10,11... | collective-permute-start | bytes 1572872 | tf_op jit(solution)/shard_map/ppermute | solution.py:239
  147.5 12.4 %collective-permute-start.9 = (bf16[512,512]{1,0:T(8,128)(2,1)}, bf16[512,512]{1,0:T(8,128)(2,1)}, u32[]{:S(2)}, u32[]{:S(2)}) collective-permute-start(bf16[512,512]{1,0:T(8,128)(2,1)} %collective-permute-done.5.refs_2_), channel_id=1, source_target_pairs={{0,1},{1,0},{2,3},{3,2},{4,5},{5,4},{6,7},{7,6},{8,9},{9,8},{10,11... | collective-permute-start | bytes 1572872 | tf_op jit(solution)/shard_map/ppermute | solution.py:239
  148.3 19.2 %collective-permute-start.23 = (bf16[512,512]{1,0:T(8,128)(2,1)}, bf16[512,512]{1,0:T(8,128)(2,1)}, u32[]{:S(2)}, u32[]{:S(2)}) collective-permute-start(bf16[512,512]{1,0:T(8,128)(2,1)} %get-tuple-element.24), channel_id=1, source_target_pairs={{0,32},{1,25},{2,34},{3,27},{4,36},{5,29},{6,38},{7,31},{8,40},{9,... | collective-permute-start | bytes 1572872 | tf_op jit(solution)/shard_map/ppermute | solution.py:239
  151.1 16.4 %collective-permute-start.24 = (bf16[512,512]{1,0:T(8,128)(2,1)}, bf16[512,512]{1,0:T(8,128)(2,1)}, u32[]{:S(2)}, u32[]{:S(2)}) collective-permute-start(bf16[512,512]{1,0:T(8,128)(2,1)} %get-tuple-element.23), channel_id=1, source_target_pairs={{0,224},{1,17},{2,226},{3,19},{4,228},{5,21},{6,230},{7,23},{8,232... | collective-permute-start | bytes 1572872 | tf_op jit(solution)/shard_map/ppermute | solution.py:239
  151.8 15.7 %collective-permute-start.26 = (bf16[256,512]{1,0:T(8,128)(2,1)}, bf16[256,512]{1,0:T(8,128)(2,1)}, u32[]{:S(2)}, u32[]{:S(2)}) collective-permute-start(bf16[256,512]{1,0:T(8,128)(2,1)} %slice.25), channel_id=1, source_target_pairs={{0,192},{2,194},{4,196},{6,198},{8,200},{10,202},{12,204},{14,206}... | collective-permute-start | bytes 786440 | tf_op jit(solution)/shard_map/ppermute | solution.py:239
  154.5 1.9 %copy-start.19 = (bf16[2,256,512]{2,1,0:T(8,128)(2,1)S(1)}, bf16[2,256,512]{2,1,0:T(8,128)(2,1)}, u32[]{:S(2)}) copy-start(bf16[2,256,512]{2,1,0:T(8,128)(2,1)} %copy-done.18) | copy-start | bytes 1572868
  156.5 1.2 copy-start.5
  157.7 9.8 %copy-start.8 = (bf16[512,512]{1,0:T(8,128)(2,1)S(1)}, bf16[512,512]{1,0:T(8,128)(2,1)}, u32[]{:S(2)}) copy-start(bf16[512,512]{1,0:T(8,128)(2,1)} %copy-done.6) | copy-start | bytes 1572868
  157.7 9.8 %copy-start.10 = (bf16[512,512]{1,0:T(8,128)(2,1)S(1)}, bf16[512,512]{1,0:T(8,128)(2,1)}, u32[]{:S(2)}) copy-start(bf16[512,512]{1,0:T(8,128)(2,1)} %copy-done.9) | copy-start | bytes 1572868
  157.7 9.9 %copy-start.12 = (bf16[512,512]{1,0:T(8,128)(2,1)S(1)}, bf16[512,512]{1,0:T(8,128)(2,1)}, u32[]{:S(2)}) copy-start(bf16[512,512]{1,0:T(8,128)(2,1)} %copy-done.11) | copy-start | bytes 1572868
  (7 other events, 5.5 us)

commit v3 on v1

--- a/solution.py
+++ b/solution.py
@@ -6,6 +6,7 @@
 from jax import lax
 from jax.experimental import pallas as pl
 from jax.experimental.pallas import tpu as pltpu
+from jax.sharding import Mesh
 from jax.sharding import PartitionSpec as P
 
 HD = 128
@@ -17,6 +18,10 @@
 
 def dot(a, b, ca, cb):
     return lax.dot_general(a, b, (((ca,), (cb,)), ((), ())), preferred_element_type=F32)
+
+
+def in_hbm(*arrays):
+    return [pltpu.with_memory_space_constraint(a, pltpu.HBM) for a in arrays]
 
 
 def window_block(q, do, k_rim, v_rim, k_own, v_own, rim_ok, own_ok):
@@ -107,8 +112,9 @@
             jax.ShapeDtypeStruct((2, WIN, width), BF16),
         ),
         name="window_grads",
+        cost_estimate=pl.CostEstimate(flops=8_000_000_000, transcendentals=0, bytes_accessed=25_000_000),
         compiler_params=pltpu.CompilerParams(vmem_limit_bytes=40 << 20),
-    )(flags, q, do, k, v, before, after)
+    )(flags, *in_hbm(q, do, k, v, before, after))
 
 
 def cross_kernel(q_ref, do_ref, k_ref, v_ref, len_ref, owner_ref, dq_ref, buf_ref, sel_ref):
@@ -151,7 +157,9 @@
         d = dot(v, do, 1, 1)
         delta = jnp.sum(probs * d, axis=0, keepdims=True)
         g = (probs * (d - delta) * INV_ROOT).astype(BF16)
-        dq_ref[r, :] = dot(g, k, 0, 0).astype(BF16)
+        dq = dot(g, k, 0, 0).astype(BF16)
+        for i in range(dq_ref.shape[0]):
+            dq_ref[i, r, :] = dq
         dks.append(dot(g, q, 1, 0).astype(BF16))
         dvs.append(dot(probs.astype(BF16), do, 1, 0).astype(BF16))
     sel = sel_ref[...]
@@ -160,7 +168,7 @@
         buf_ref[:, i] = placed.reshape(slots // cap, cap, HD)
 
 
-def cross_call(q, do, k, v, lens, owners, owner_count):
+def cross_call(q, do, k, v, lens, owners, owner_count, copies):
     rows, width = q.shape
     patches = k.shape[0]
     cap = max(2, 2 * (patches // owner_count))
@@ -177,18 +185,19 @@
                 pl.BlockSpec((1, patches), lambda h: (0, 0)),
             ],
             out_specs=[
-                col,
+                pl.BlockSpec((copies, rows, HD), lambda h: (0, 0, h)),
                 pl.BlockSpec((owner_count, 2, cap, HD), lambda h: (0, 0, 0, h)),
             ],
             scratch_shapes=[pltpu.VMEM((owner_count * cap, patches), BF16)],
         ),
         out_shape=(
-            jax.ShapeDtypeStruct((rows, width), BF16),
+            jax.ShapeDtypeStruct((copies, rows, width), BF16),
             jax.ShapeDtypeStruct((owner_count, 2, cap, width), BF16),
         ),
         name="cross_grads",
+        cost_estimate=pl.CostEstimate(flops=5_000_000_000, transcendentals=0, bytes_accessed=15_000_000),
         compiler_params=pltpu.CompilerParams(vmem_limit_bytes=40 << 20),
-    )(q, do, k, v, lens, owners.reshape(1, patches))
+    )(*in_hbm(q, do, k, v, lens, owners.reshape(1, patches)))
 
 
 def join_kernel(dk_ref, dv_ref, low_ref, high_ref, dk_out, dv_out):
@@ -211,7 +220,29 @@
         out_shape=(out, out),
         name="join_rims",
         compiler_params=pltpu.CompilerParams(vmem_limit_bytes=40 << 20),
-    )(dk, dv, low_back, high_back)
+    )(*in_hbm(dk, dv, low_back, high_back))
+
+
+def pack_kernel(k_ref, v_ref, low_ref, high_ref):
+    for i, ref in enumerate((k_ref, v_ref)):
+        low_ref[i] = ref[:WIN, :]
+        high_ref[i] = ref[WIN:, :]
+
+
+def pack_call(k, v):
+    rows, width = k.shape
+    step = 2 * HD
+    full = pl.BlockSpec((rows, step), lambda h: (0, h))
+    rim = pl.BlockSpec((2, WIN, step), lambda h: (0, 0, h))
+    out = jax.ShapeDtypeStruct((2, WIN, width), BF16)
+    return pl.pallas_call(
+        pack_kernel,
+        grid=(width // step,),
+        in_specs=[full] * 2,
+        out_specs=[rim, rim],
+        out_shape=(out, out),
+        name="pack_rims",
+    )(*in_hbm(k, v))
 
 
 def shifted(block, axis, distance):
@@ -220,43 +251,114 @@
     return lax.ppermute(block, axis, route)
 
 
+NZ, NX, NY, NC = 8, 4, 4, 2
+AXES = ("z", "x", "y", "core")
+SEQ = ("z", "x")
+
+
+def place(z, x, y, c):
+    return ((z % NZ) * NX + x % NX) * (NY * NC) + (y % NY) * NC + c
+
+
+def send(block, target):
+    route = []
+    for z in range(NZ):
+        for x in range(NX):
+            for y in range(NY):
+                for c in range(NC):
+                    route.append((place(z, x, y, c), place(*target(z, x, y, c))))
+    return lax.ppermute(block, AXES, route)
+
+
+def product_kernel(pos, own_ref, other_ref, w_own_ref, w_other_ref, out_ref, total_ref):
+    step = pl.program_id(0)
+    part = dot(own_ref[0], w_own_ref[0], 1, 1) + dot(other_ref[0], w_other_ref[0], 1, 1)
+
+    @pl.when(step == 0)
+    def _():
+        total_ref[...] = part
+
+    @pl.when(step > 0)
+    def _():
+        total_ref[...] += part
+
+    @pl.when(step == pl.num_programs(0) - 1)
+    def _():
+        out_ref[...] = total_ref[...].astype(BF16)
+
+
+def product_call(pos, own_rows, other_rows, whole):
+    count, width = own_rows.shape[1:]
+    n_rows = whole.shape[1]
+    rows = pl.BlockSpec((1, count, width), lambda i, p: (i, 0, 0))
+    return pl.pallas_call(
+        product_kernel,
+        grid_spec=pltpu.PrefetchScalarGridSpec(
+            num_scalar_prefetch=1,
+            grid=(NY,),
+            in_specs=[
+                rows, rows,
+                pl.BlockSpec(
+                    (1, n_rows, width), lambda i, p: (lax.rem(NC * i + p[2] + p[1], NZ), 0, 0)
+                ),
+                pl.BlockSpec(
+                    (1, n_rows, width), lambda i, p: (lax.rem(NC * i + 1 - p[2] + p[1], NZ), 0, 0)
+                ),
+            ],
+            out_specs=pl.BlockSpec((count, n_rows), lambda i, p: (0, 0)),
+            scratch_shapes=[pltpu.VMEM((count, n_rows), F32)],
+        ),
+        out_shape=jax.ShapeDtypeStruct((count, n_rows), BF16),
+        name="byte_product",
+        compiler_params=pltpu.CompilerParams(vmem_limit_bytes=40 << 20),
+    )(pos, *in_hbm(own_rows, other_rows, whole, whole))
+
+
 def local(
     win_query, win_key, win_value, win_dout, cross_query, cross_dout,
     patch_key, patch_value, patch_len, patch_owner, w_query,
 ):
-    seq_count = lax.axis_size("seq")
-    seq_index = lax.axis_index("seq")
+    z, x = lax.axis_index("z"), lax.axis_index("x")
+    y, core = lax.axis_index("y"), lax.axis_index("core")
+    seq_count = NZ * NX
+    seq_index = z * NX + x
     flags = jnp.stack([seq_index > 0, seq_index == seq_count - 1]).astype(jnp.int32)
-    low_rim = jnp.stack([win_key[:WIN], win_value[:WIN]])
-    high_rim = jnp.stack([win_key[WIN:], win_value[WIN:]])
-    before = shifted(low_rim, "seq", 1)
-    after = shifted(high_rim, "seq", -1)
+    pos = jnp.stack([x, y * NC + core, core]).astype(jnp.int32)
+    own = send(w_query, lambda z, x, y, c: (z + NC * y + c, x, z // NC, z % NC))
+    low_rim, high_rim = pack_call(win_key, win_value)
+    cross_query, low_rim = lax.optimization_barrier((cross_query, low_rim))
     cross_dq, buffer = cross_call(
-        cross_query, cross_dout, patch_key, patch_value, patch_len, patch_owner, seq_count
-    )
+        cross_query, cross_dout, patch_key, patch_value, patch_len, patch_owner, seq_count, NY
+    )
+    own, cross_dq, buffer, low_rim, high_rim = lax.optimization_barrier(
+        (own, cross_dq, buffer, low_rim, high_rim)
+    )
+    whole = lax.all_gather(own, SEQ, axis=0, tiled=True)
+    whole = whole.reshape(NZ, NX * own.shape[0], own.shape[1])
+    before = shifted(low_rim, SEQ, 1)
+    after = shifted(high_rim, SEQ, -1)
+    own_rows = lax.all_to_all(cross_dq, "y", split_axis=0, concat_axis=0, tiled=True)
     win_dq, dk, dv, low_send, high_send = window_call(
         flags, win_query, win_dout, win_key, win_value, before, after
     )
-    low_back = shifted(low_send, "seq", -1)
-    high_back = shifted(high_send, "seq", 1)
+    win_dq, buffer = lax.optimization_barrier((win_dq, buffer))
+    arrived = lax.all_to_all(buffer, SEQ, split_axis=0, concat_axis=0, tiled=True)
+    low_back = shifted(low_send, SEQ, -1)
+    high_back = shifted(high_send, SEQ, 1)
+    low_back, high_back, own_rows = lax.optimization_barrier((low_back, high_back, own_rows))
+    other_rows = send(own_rows, lambda z, x, y, c: (z, x, y, 1 - c))
     win_dk, win_dv = join_call(dk, dv, low_back, high_back)
-    arrived = lax.all_to_all(buffer, "seq", split_axis=0, concat_axis=0, tiled=True)
+    arrived, win_dk = lax.optimization_barrier((arrived, win_dk))
     patch_grads = arrived.transpose(1, 0, 2, 3).reshape(2, -1, arrived.shape[3])
-    partial_sums = lax.dot_general(
-        cross_dq,
-        lax.all_gather(w_query, "seq", axis=0, tiled=True),
-        (((1,), (1,)), ((), ())),
-        preferred_element_type=F32,
-    )
-    byte_grads = lax.psum_scatter(
-        partial_sums.astype(BF16), "mp", scatter_dimension=1, tiled=True
-    )
+    byte_grads = product_call(pos, own_rows, other_rows, whole)
     return (win_dq, win_dk, win_dv, patch_grads, byte_grads)
 
 
 def solution(mesh):
-    tile = P("seq", "mp")
-    rows = P("seq", None)
+    mesh = Mesh(mesh.devices.reshape(NZ, NX, NY, NC), AXES)
+    mp = ("y", "core")
+    tile = P(SEQ, mp)
+    rows = P(SEQ, None)
     in_specs = (tile,) * 8 + (rows, rows, tile)
-    out_specs = (tile, tile, tile, P(None, "seq", "mp"), tile)
+    out_specs = (tile, tile, tile, P(None, SEQ, mp), tile)
     return jax.shard_map(local, mesh=mesh, in_specs=in_specs, out_specs=out_specs, check_vma=False)

time: 172 us -> 131 us (0.76)
  the two profiles are of different devices: /device:TPU:128 before, /device:TPU:8 now
where the time goes in v3:
time: 131 us
  waiting for transfers between devices  45.9 us (35%)
  starting transfers between devices  40.2 us (31%)
  Pallas kernels  26.1 us (20%)
  between operations  14.1 us (11%)
  local copies, waits for them, and re-layouts  4.3 us (3%)
    all_to_all x1, waiting for transfers between devices, local(): lax.all_to_all(buffer, SEQ, split_axis=0, concat_axis=0, tiled=True)  20.6 us
    ppermute x4, waiting for transfers between devices, shifted(): return lax.ppermute(block, axis, route)  18.7 us
    all_to_all x1, starting transfers between devices, local(): lax.all_to_all(buffer, SEQ, split_axis=0, concat_axis=0, tiled=True)  15.2 us
    ppermute x4, starting transfers between devices, shifted(): return lax.ppermute(block, axis, route)  11.3 us
    all_to_all x1, starting transfers between devices, local(): lax.all_to_all(cross_dq, 'y', split_axis=0, concat_axis=0, tiled=True)  8.53 us
    pallas_call x1, Pallas kernels, window_call(): pl.pallas_call(window_kernel, grid_spec=pltpu.PrefetchScalarGridSpec(num_...  8.42 us
    pallas_call x1, Pallas kernels, product_call(): pl.pallas_call(product_kernel, grid_spec=pltpu.PrefetchScalarGridSpec(num...  7.11 us
    all_gather x1, waiting for transfers between devices, local(): whole = lax.all_gather(own, SEQ, axis=0, tiled=True)  6.3 us
  transfers between devices with their start and end apart: 9, of which 7 were waited for; matrix products, arithmetic and copies ran while one was open for 1% of the time, Pallas kernels for 15%

profile of v3, /device:TPU:8, one launch (start us, length us, event | category | flops | bytes accessed | tf_op | source)
XLA Modules:
  0.0 130.7 jit_solution(13917770199595287075)
XLA Ops:
  7.2 0.0 all-gather.2.cloned.1.call-start
  7.2 5.1 %collective-permute-start = (bf16[128,512]{1,0:T(8,128)(2,1)}, bf16[128,512]{1,0:T(8,128)(2,1)S(1)}, u32[]{:S(2)}, u32[]{:S(2)}) collective-permute-start(bf16[128,512]{1,0:T(8,128)(2,1)} %param.21), channel_id=1, source_target_pairs={{0,0},{1,32},{2,64},{3,96},{4,128},{5,160},{6,192},{7,224},{8,8},{... | collective-permute-start | bytes 393224 | tf_op jit(solution)/shard_map/ppermute | solution.py:270
  12.3 2.0 %pack_rims.1 = (bf16[2,256,512]{2,1,0:T(8,128)(2,1)}, bf16[2,256,512]{2,1,0:T(8,128)(2,1)}) custom-call(bf16[512,512]{1,0:T(8,128)(2,1)} %k_ref.5, bf16[512,512]{1,0:T(8,128)(2,1)} %v_ref.5), custom_call_target="tpu_custom_call" | custom-call | tf_op jit(solution)/shard_map/pack_rims/pallas_call | solution.py:238
  14.3 0.0 copy-start.7
  14.3 0.0 copy-start.6
  14.3 5.8 %cross_grads.1 = (bf16[4,512,512]{2,1,0:T(8,128)(2,1)}, bf16[32,2,8,512]{3,2,1,0:T(8,128)(2,1)}) custom-call(bf16[512,512]{1,0:T(8,128)(2,1)} %q_ref.1, bf16[512,512]{1,0:T(8,128)(2,1)} %do_ref.2, bf16[128,512]{1,0:T(8,128)(2,1)} %k_ref.4, bf16[128,512]{1,0:T(8,128)(2,1)} %v_ref.4, s32[2,64]{1,0:T(2,128)} %len_ref.1, s32[1,128]{1,0:T(1,128)} %bitcast.14), custom_call_target="tpu_custom_call" | custom-call | flops 5000000000 | bytes 15000000 | tf_op jit(solution)/shard_map/cross_grads/pallas_call | solution.py:177
  20.2 0.2 collective-permute-done
  20.4 0.0 copy-start.5
  20.4 0.6 copy-done.5
  21.0 0.0 all-gather.2.cloned.1.call-update
  21.0 0.0 copy-done.7
  21.0 4.2 %collective-permute-start.1 = (bf16[2,256,512]{2,1,0:T(8,128)(2,1)S(1)}, bf16[2,256,512]{2,1,0:T(8,128)(2,1)}, u32[]{:S(2)}, u32[]{:S(2)}) collective-permute-start(bf16[2,256,512]{2,1,0:T(8,128)(2,1)S(1)} %copy-done.7), channel_id=1, source_target_pairs={{0,8},{8,16},{16,24},{24,32},{32,40},{40,48},{48,56},{56,64},{64,7... | collective-permute-start | bytes 1572872 | tf_op jit(solution)/shard_map/ppermute | solution.py:251
  25.3 0.0 copy-done.6
  25.3 1.3 collective-permute-start.2
  26.5 8.5 %all-to-all-start.1 = ((bf16[4,512,512]{2,1,0:T(8,128)(2,1)}), bf16[4,512,512]{2,1,0:T(8,128)(2,1)S(1)}, u32[]{:S(2)}, u32[]{:S(2)}) async-start(bf16[4,512,512]{2,1,0:T(8,128)(2,1)} %get-tuple-element.46), calls=%async_computation.1 | async-start | bytes 4194304 | tf_op jit(solution)/shard_map/all_to_all | solution.py:340
  35.1 0.1 add_convert_fusion.flags
  35.2 1.3 collective-permute-done.1.before_ref
  36.4 6.3 %collective-permute-done.2.after_ref = bf16[2,256,512]{2,1,0:T(8,128)(2,1)} collective-permute-done((bf16[2,256,512]{2,1,0:T(8,128)(2,1)S(1)}, bf16[2,256,512]{2,1,0:T(8,128)(2,1)}, u32[]{:S(2)}, u32[]{:S(2)}) %collective-permute-start.2) | collective-permute-done | bytes 524320 | tf_op jit(solution)/shard_map/ppermute | solution.py:251
  42.7 8.4 %window_grads.1 = (bf16[512,512]{1,0:T(8,128)(2,1)}, f32[512,512]{1,0:T(8,128)S(1)}, f32[512,512]{1,0:T(8,128)S(1)}, bf16[2,256,512]{2,1,0:T(8,128)(2,1)S(1)}, bf16[2,256,512]{2,1,0:T(8,128)(2,1)S(1)}) custom-call(s32[2]{0:T(128)S(1)} %add_convert_fusion.flags, bf16[512,512]{1,0:T(8,128)(2,1)} %q_ref.2, bf16[512,512]{1,0:T(8,128)(2,1)} %do_ref.3, ...), custom_call_target="tpu_custom_call" | custom-call | flops 8000000000 | bytes 25000000 | tf_op jit(solution)/shard_map/window_grads/pallas_call | solution.py:99
  51.1 0.0 copy-start
  51.2 1.0 copy-done
  52.2 0.0 copy-start.1
  52.2 1.0 copy-done.1
  53.2 1.3 collective-permute-start.3
  54.5 4.6 %collective-permute-start.4 = (bf16[2,256,512]{2,1,0:T(8,128)(2,1)S(1)}, bf16[2,256,512]{2,1,0:T(8,128)(2,1)S(1)}, u32[]{:S(2)}, u32[]{:S(2)}) collective-permute-start(bf16[2,256,512]{2,1,0:T(8,128)(2,1)S(1)} %get-tuple-element.45), channel_id=1, source_target_pairs={{0,8},{8,16},{16,24},{24,32},{32,40},{40,48},{48,56},{56,64},{64,7... | collective-permute-start | bytes 1572872 | tf_op jit(solution)/shard_map/ppermute | solution.py:251
  59.1 9.9 %collective-permute-done.3.low_ref = bf16[2,256,512]{2,1,0:T(8,128)(2,1)S(1)} collective-permute-done((bf16[2,256,512]{2,1,0:T(8,128)(2,1)S(1)}, bf16[2,256,512]{2,1,0:T(8,128)(2,1)S(1)}, u32[]{:S(2)}, u32[]{:S(2)}) %collective-permute-start.3) | collective-permute-done | bytes 524320 | tf_op jit(solution)/shard_map/ppermute | solution.py:251
  69.0 0.0 copy-start.3
  69.0 1.2 collective-permute-done.4.high_ref
  70.2 0.0 copy-start.4
  70.2 0.0 all-to-all-done.1.own_ref
  70.2 0.0 copy-start.2
  70.2 0.0 collective-permute-start.5
  70.2 0.8 copy-done.4
  71.0 15.2 %all-to-all-start = ((bf16[32,2,8,512]{3,2,1,0:T(8,128)(2,1)}), bf16[32,2,8,512]{3,2,1,0:T(8,128)(2,1)S(1)}, u32[]{:S(2)}, u32[]{:S(2)}) async-start(bf16[32,2,8,512]{3,2,1,0:T(8,128)(2,1)} %get-tuple-element.41), calls=%async_computation | async-start | bytes 1048576 | tf_op jit(solution)/shard_map/all_to_all | solution.py:345
  86.2 0.1 pad_add_fusion.pos
  86.3 0.0 copy-done.3
  86.3 2.7 %join_rims.1 = (bf16[512,512]{1,0:T(8,128)(2,1)}, bf16[512,512]{1,0:T(8,128)(2,1)}) custom-call(f32[512,512]{1,0:T(8,128)} %copy-done, f32[512,512]{1,0:T(8,128)} %copy-done.1, bf16[2,256,512]{2,1,0:T(8,128)(2,1)} %copy-done.3, bf16[2,256,512]{2,1,0:T(8,128)(2,1)} %copy-done.4), custom_call_target="tpu_custom_call" | custom-call | tf_op jit(solution)/shard_map/join_rims/pallas_call | solution.py:215
  89.0 0.0 copy-done.2
  89.0 20.6 %all-to-all-done = bf16[32,2,8,512]{3,2,1,0:T(8,128)(2,1)S(1)} async-done(((bf16[32,2,8,512]{3,2,1,0:T(8,128)(2,1)}), bf16[32,2,8,512]{3,2,1,0:T(8,128)(2,1)S(1)}, u32[]{:S(2)}, u32[]{:S(2)}) %all-to-all-start) | async-done | bytes 524320 | tf_op jit(solution)/shard_map/all_to_all | solution.py:345
  109.6 0.8 copy_bitcast_fusion
  110.5 0.0 collective-permute-done.5.other_ref
  110.5 6.3 %all-gather.2.cloned.1.call-done = bf16[4096,512]{1,0:T(8,128)(2,1)} async-done(((bf16[128,512]{1,0:T(8,128)(2,1)}), bf16[4096,512]{1,0:T(8,128)(2,1)}) %all-gather.2.cloned.1.call-update) | async-done | bytes 4194320 | tf_op jit(solution)/shard_map/all_gather | solution.py:336
  116.8 7.1 %byte_product.1 = bf16[512,512]{1,0:T(8,128)(2,1)} custom-call(s32[3]{0:T(128)S(1)} %pad_add_fusion.pos, bf16[4,512,512]{2,1,0:T(8,128)(2,1)} %copy-done.2, bf16[4,512,512]{2,1,0:T(8,128)(2,1)} %collective-permute-done.5.other_ref, bf16[8,512,512]{2,1,0:T(8,128)(2,1)} %bitcast.12, bf16[8,512,512]{2,1,0:T(8,128)(2,1)} %bitcast.13), custom_call_target="tpu_custom_call" | custom-call | tf_op jit(solution)/shard_map/byte_product/pallas_call | solution.py:294
Async XLA Ops:
  7.2 109.6 %all-gather.2.cloned.1.call-start = ((), (), s32[]{:S(2)}) async-start(), calls=%async_computation.2 | async-start | bytes 4325376 | tf_op jit(solution)/shard_map/all_gather | solution.py:336
  7.2 13.2 %collective-permute-start = (bf16[128,512]{1,0:T(8,128)(2,1)}, bf16[128,512]{1,0:T(8,128)(2,1)S(1)}, u32[]{:S(2)}, u32[]{:S(2)}) collective-permute-start(bf16[128,512]{1,0:T(8,128)(2,1)} %param.21), channel_id=1, source_target_pairs={{0,0},{1,32},{2,64},{3,96},{4,128},{5,160},{6,192},{7,224},{8,8},{... | collective-permute-start | bytes 393224 | tf_op jit(solution)/shard_map/ppermute | solution.py:270
  14.3 6.7 %copy-start.7 = (bf16[2,256,512]{2,1,0:T(8,128)(2,1)S(1)}, bf16[2,256,512]{2,1,0:T(8,128)(2,1)}, u32[]{:S(2)}) copy-start(bf16[2,256,512]{2,1,0:T(8,128)(2,1)} %get-tuple-element.36) | copy-start | bytes 1572868
  14.3 10.9 %copy-start.6 = (bf16[2,256,512]{2,1,0:T(8,128)(2,1)S(1)}, bf16[2,256,512]{2,1,0:T(8,128)(2,1)}, u32[]{:S(2)}) copy-start(bf16[2,256,512]{2,1,0:T(8,128)(2,1)} %get-tuple-element.37) | copy-start | bytes 1572868
  20.4 0.6 copy-start.5
  21.0 15.4 %collective-permute-start.1 = (bf16[2,256,512]{2,1,0:T(8,128)(2,1)S(1)}, bf16[2,256,512]{2,1,0:T(8,128)(2,1)}, u32[]{:S(2)}, u32[]{:S(2)}) collective-permute-start(bf16[2,256,512]{2,1,0:T(8,128)(2,1)S(1)} %copy-done.7), channel_id=1, source_target_pairs={{0,8},{8,16},{16,24},{24,32},{32,40},{40,48},{48,56},{56,64},{64,7... | collective-permute-start | bytes 1572872 | tf_op jit(solution)/shard_map/ppermute | solution.py:251
  25.3 17.5 %collective-permute-start.2 = (bf16[2,256,512]{2,1,0:T(8,128)(2,1)S(1)}, bf16[2,256,512]{2,1,0:T(8,128)(2,1)}, u32[]{:S(2)}, u32[]{:S(2)}) collective-permute-start(bf16[2,256,512]{2,1,0:T(8,128)(2,1)S(1)} %copy-done.6), channel_id=1, source_target_pairs={{8,0},{16,8},{24,16},{32,24},{40,32},{48,40},{56,48},{64,56},{72,6... | collective-permute-start | bytes 1572872 | tf_op jit(solution)/shard_map/ppermute | solution.py:251
  26.5 43.6 %all-to-all-start.1 = ((bf16[4,512,512]{2,1,0:T(8,128)(2,1)}), bf16[4,512,512]{2,1,0:T(8,128)(2,1)S(1)}, u32[]{:S(2)}, u32[]{:S(2)}) async-start(bf16[4,512,512]{2,1,0:T(8,128)(2,1)} %get-tuple-element.46), calls=%async_computation.1 | async-start | bytes 4194304 | tf_op jit(solution)/shard_map/all_to_all | solution.py:340
  51.1 1.0 copy-start
  52.2 1.0 copy-start.1
  53.2 15.8 %collective-permute-start.3 = (bf16[2,256,512]{2,1,0:T(8,128)(2,1)S(1)}, bf16[2,256,512]{2,1,0:T(8,128)(2,1)S(1)}, u32[]{:S(2)}, u32[]{:S(2)}) collective-permute-start(bf16[2,256,512]{2,1,0:T(8,128)(2,1)S(1)} %get-tuple-element.44), channel_id=1, source_target_pairs={{8,0},{16,8},{24,16},{32,24},{40,32},{48,40},{56,48},{64,56},{72,6... | collective-permute-start | bytes 1572872 | tf_op jit(solution)/shard_map/ppermute | solution.py:251
  54.5 15.7 %collective-permute-start.4 = (bf16[2,256,512]{2,1,0:T(8,128)(2,1)S(1)}, bf16[2,256,512]{2,1,0:T(8,128)(2,1)S(1)}, u32[]{:S(2)}, u32[]{:S(2)}) collective-permute-start(bf16[2,256,512]{2,1,0:T(8,128)(2,1)S(1)} %get-tuple-element.45), channel_id=1, source_target_pairs={{0,8},{8,16},{16,24},{24,32},{32,40},{40,48},{48,56},{56,64},{64,7... | collective-permute-start | bytes 1572872 | tf_op jit(solution)/shard_map/ppermute | solution.py:251
  69.0 17.3 %copy-start.3 = (bf16[2,256,512]{2,1,0:T(8,128)(2,1)}, bf16[2,256,512]{2,1,0:T(8,128)(2,1)S(1)}, u32[]{:S(2)}) copy-start(bf16[2,256,512]{2,1,0:T(8,128)(2,1)S(1)} %collective-permute-done.3.low_ref) | copy-start | bytes 1572868
  70.2 0.8 copy-start.4
  70.2 18.8 %copy-start.2 = (bf16[4,512,512]{2,1,0:T(8,128)(2,1)}, bf16[4,512,512]{2,1,0:T(8,128)(2,1)S(1)}, u32[]{:S(2)}) copy-start(bf16[4,512,512]{2,1,0:T(8,128)(2,1)S(1)} %all-to-all-done.1.own_ref) | copy-start | bytes 6291460
  70.2 40.3 %collective-permute-start.5 = (bf16[4,512,512]{2,1,0:T(8,128)(2,1)S(1)}, bf16[4,512,512]{2,1,0:T(8,128)(2,1)}, u32[]{:S(2)}, u32[]{:S(2)}) collective-permute-start(bf16[4,512,512]{2,1,0:T(8,128)(2,1)S(1)} %all-to-all-done.1.own_ref), channel_id=1, source_target_pairs={{0,1},{1,0},{2,3},{3,2},{4,5},{5,4},{6,7},{7,6},{8,9},{9,8},{10,11... | collective-permute-start | bytes 6291464 | tf_op jit(solution)/shard_map/ppermute | solution.py:270
  71.0 38.6 %all-to-all-start = ((bf16[32,2,8,512]{3,2,1,0:T(8,128)(2,1)}), bf16[32,2,8,512]{3,2,1,0:T(8,128)(2,1)S(1)}, u32[]{:S(2)}, u32[]{:S(2)}) async-start(bf16[32,2,8,512]{3,2,1,0:T(8,128)(2,1)} %get-tuple-element.41), calls=%async_computation | async-start | bytes 1048576 | tf_op jit(solution)/shard_map/all_to_all | solution.py:345
Sparse Core Ops, SparseCore 0:
  21.2 95.5 all-gather.1

commit v4 on v3

--- a/solution.py
+++ b/solution.py
@@ -270,48 +270,54 @@
     return lax.ppermute(block, AXES, route)
 
 
-def product_kernel(pos, own_ref, other_ref, w_own_ref, w_other_ref, out_ref, total_ref):
-    step = pl.program_id(0)
-    part = dot(own_ref[0], w_own_ref[0], 1, 1) + dot(other_ref[0], w_other_ref[0], 1, 1)
-
-    @pl.when(step == 0)
-    def _():
-        total_ref[...] = part
-
-    @pl.when(step > 0)
-    def _():
-        total_ref[...] += part
-
-    @pl.when(step == pl.num_programs(0) - 1)
-    def _():
-        out_ref[...] = total_ref[...].astype(BF16)
+def product_kernel(
+    pos, own_ref, other_ref, whole_ref, out_ref, a_buf, w_buf, a_sem, w_sem
+):
+    m, c = pos[1], pos[2]
+    copies = []
+    for j in range(NZ):
+        rows, core = (own_ref, c) if j % NC == 0 else (other_ref, 1 - c)
+        slot = lax.rem(NC * (j // NC) + core + m, NZ)
+        copies.append(
+            (
+                pltpu.make_async_copy(rows.at[j // NC], a_buf.at[j], a_sem.at[j]),
+                pltpu.make_async_copy(whole_ref.at[slot], w_buf.at[j], w_sem.at[j]),
+            )
+        )
+    for rows, weight in copies:
+        rows.start()
+        weight.start()
+    total = None
+    for j, (rows, weight) in enumerate(copies):
+        rows.wait()
+        weight.wait()
+        part = dot(a_buf[j], w_buf[j], 1, 1)
+        total = part if total is None else total + part
+    out_ref[...] = total.astype(BF16)
 
 
 def product_call(pos, own_rows, other_rows, whole):
     count, width = own_rows.shape[1:]
     n_rows = whole.shape[1]
-    rows = pl.BlockSpec((1, count, width), lambda i, p: (i, 0, 0))
+    anywhere = pl.BlockSpec(memory_space=pl.ANY)
     return pl.pallas_call(
         product_kernel,
         grid_spec=pltpu.PrefetchScalarGridSpec(
             num_scalar_prefetch=1,
-            grid=(NY,),
-            in_specs=[
-                rows, rows,
-                pl.BlockSpec(
-                    (1, n_rows, width), lambda i, p: (lax.rem(NC * i + p[2] + p[1], NZ), 0, 0)
-                ),
-                pl.BlockSpec(
-                    (1, n_rows, width), lambda i, p: (lax.rem(NC * i + 1 - p[2] + p[1], NZ), 0, 0)
-                ),
+            grid=(1,),
+            in_specs=[anywhere] * 3,
+            out_specs=pl.BlockSpec((count, n_rows), lambda i, p: (0, 0)),
+            scratch_shapes=[
+                pltpu.VMEM((NZ, count, width), BF16),
+                pltpu.VMEM((NZ, n_rows, width), BF16),
+                pltpu.SemaphoreType.DMA((NZ,)),
+                pltpu.SemaphoreType.DMA((NZ,)),
             ],
-            out_specs=pl.BlockSpec((count, n_rows), lambda i, p: (0, 0)),
-            scratch_shapes=[pltpu.VMEM((count, n_rows), F32)],
         ),
         out_shape=jax.ShapeDtypeStruct((count, n_rows), BF16),
         name="byte_product",
         compiler_params=pltpu.CompilerParams(vmem_limit_bytes=40 << 20),
-    )(pos, *in_hbm(own_rows, other_rows, whole, whole))
+    )(pos, *in_hbm(own_rows, other_rows, whole))
 
 
 def local(

time: 131 us -> 130 us (level)
  no operation moved by 1% of the time
where the time goes in v4:
time: 130 us; the launch traced here: 129 us
  waiting for transfers between devices  45.9 us (35%)
  starting transfers between devices  40.2 us (31%)
  Pallas kernels  24.9 us (19%)
  between operations  14.1 us (11%)
  local copies, waits for them, and re-layouts  4.3 us (3%)
    all_to_all x1, waiting for transfers between devices, local(): lax.all_to_all(buffer, SEQ, split_axis=0, concat_axis=0, tiled=True)  20.6 us
    ppermute x4, waiting for transfers between devices, shifted(): return lax.ppermute(block, axis, route)  18.7 us
    all_to_all x1, starting transfers between devices, local(): lax.all_to_all(buffer, SEQ, split_axis=0, concat_axis=0, tiled=True)  15.2 us
    ppermute x4, starting transfers between devices, shifted(): return lax.ppermute(block, axis, route)  11.3 us
    all_to_all x1, starting transfers between devices, local(): lax.all_to_all(cross_dq, 'y', split_axis=0, concat_axis=0, tiled=True)  8.53 us
    pallas_call x1, Pallas kernels, window_call(): pl.pallas_call(window_kernel, grid_spec=pltpu.PrefetchScalarGridSpec(num_...  8.42 us
    all_gather x1, waiting for transfers between devices, local(): whole = lax.all_gather(own, SEQ, axis=0, tiled=True)  6.3 us
    pallas_call x1, Pallas kernels, product_call(): pl.pallas_call(product_kernel, grid_spec=pltpu.PrefetchScalarGridSpec(num...  5.85 us
  transfers between devices with their start and end apart: 9, of which 7 were waited for; matrix products, arithmetic and copies ran while one was open for 1% of the time, Pallas kernels for 15%

profile of v4, /device:TPU:8, one launch (start us, length us, event | category | flops | bytes accessed | tf_op | source)
XLA Modules:
  0.0 129.5 jit_solution(1632013299861473316)
XLA Ops:
  7.2 0.0 all-gather.2.cloned.1.call-start
  7.2 5.1 %collective-permute-start = (bf16[128,512]{1,0:T(8,128)(2,1)}, bf16[128,512]{1,0:T(8,128)(2,1)S(1)}, u32[]{:S(2)}, u32[]{:S(2)}) collective-permute-start(bf16[128,512]{1,0:T(8,128)(2,1)} %param.21), channel_id=1, source_target_pairs={{0,0},{1,32},{2,64},{3,96},{4,128},{5,160},{6,192},{7,224},{8,8},{... | collective-permute-start | bytes 393224 | tf_op jit(solution)/shard_map/ppermute | solution.py:270
  12.3 2.0 %pack_rims.1 = (bf16[2,256,512]{2,1,0:T(8,128)(2,1)}, bf16[2,256,512]{2,1,0:T(8,128)(2,1)}) custom-call(bf16[512,512]{1,0:T(8,128)(2,1)} %k_ref.5, bf16[512,512]{1,0:T(8,128)(2,1)} %v_ref.5), custom_call_target="tpu_custom_call" | custom-call | tf_op jit(solution)/shard_map/pack_rims/pallas_call | solution.py:238
  14.3 0.0 copy-start.7
  14.3 0.0 copy-start.6
  14.3 5.8 %cross_grads.1 = (bf16[4,512,512]{2,1,0:T(8,128)(2,1)}, bf16[32,2,8,512]{3,2,1,0:T(8,128)(2,1)}) custom-call(bf16[512,512]{1,0:T(8,128)(2,1)} %q_ref.1, bf16[512,512]{1,0:T(8,128)(2,1)} %do_ref.2, bf16[128,512]{1,0:T(8,128)(2,1)} %k_ref.4, bf16[128,512]{1,0:T(8,128)(2,1)} %v_ref.4, s32[2,64]{1,0:T(2,128)} %len_ref.1, s32[1,128]{1,0:T(1,128)} %bitcast.13), custom_call_target="tpu_custom_call" | custom-call | flops 5000000000 | bytes 15000000 | tf_op jit(solution)/shard_map/cross_grads/pallas_call | solution.py:177
  20.2 0.2 collective-permute-done
  20.4 0.0 copy-start.5
  20.4 0.6 copy-done.5
  21.0 0.0 all-gather.2.cloned.1.call-update
  21.0 0.0 copy-done.7
  21.0 4.2 %collective-permute-start.1 = (bf16[2,256,512]{2,1,0:T(8,128)(2,1)S(1)}, bf16[2,256,512]{2,1,0:T(8,128)(2,1)}, u32[]{:S(2)}, u32[]{:S(2)}) collective-permute-start(bf16[2,256,512]{2,1,0:T(8,128)(2,1)S(1)} %copy-done.7), channel_id=1, source_target_pairs={{0,8},{8,16},{16,24},{24,32},{32,40},{40,48},{48,56},{56,64},{64,7... | collective-permute-start | bytes 1572872 | tf_op jit(solution)/shard_map/ppermute | solution.py:251
  25.3 0.0 copy-done.6
  25.3 1.3 collective-permute-start.2
  26.5 8.5 %all-to-all-start.1 = ((bf16[4,512,512]{2,1,0:T(8,128)(2,1)}), bf16[4,512,512]{2,1,0:T(8,128)(2,1)S(1)}, u32[]{:S(2)}, u32[]{:S(2)}) async-start(bf16[4,512,512]{2,1,0:T(8,128)(2,1)} %get-tuple-element.46), calls=%async_computation.1 | async-start | bytes 4194304 | tf_op jit(solution)/shard_map/all_to_all | solution.py:346
  35.1 0.1 add_convert_fusion.flags
  35.2 1.3 %collective-permute-done.1.before_ref = bf16[2,256,512]{2,1,0:T(8,128)(2,1)} collective-permute-done((bf16[2,256,512]{2,1,0:T(8,128)(2,1)S(1)}, bf16[2,256,512]{2,1,0:T(8,128)(2,1)}, u32[]{:S(2)}, u32[]{:S(2)}) %collective-permute-start.1) | collective-permute-done | bytes 524320 | tf_op jit(solution)/shard_map/ppermute | solution.py:251
  36.4 6.3 %collective-permute-done.2.after_ref = bf16[2,256,512]{2,1,0:T(8,128)(2,1)} collective-permute-done((bf16[2,256,512]{2,1,0:T(8,128)(2,1)S(1)}, bf16[2,256,512]{2,1,0:T(8,128)(2,1)}, u32[]{:S(2)}, u32[]{:S(2)}) %collective-permute-start.2) | collective-permute-done | bytes 524320 | tf_op jit(solution)/shard_map/ppermute | solution.py:251
  42.7 8.4 %window_grads.1 = (bf16[512,512]{1,0:T(8,128)(2,1)}, f32[512,512]{1,0:T(8,128)S(1)}, f32[512,512]{1,0:T(8,128)S(1)}, bf16[2,256,512]{2,1,0:T(8,128)(2,1)S(1)}, bf16[2,256,512]{2,1,0:T(8,128)(2,1)S(1)}) custom-call(s32[2]{0:T(128)S(1)} %add_convert_fusion.flags, bf16[512,512]{1,0:T(8,128)(2,1)} %q_ref.2, bf16[512,512]{1,0:T(8,128)(2,1)} %do_ref.3, ...), custom_call_target="tpu_custom_call" | custom-call | flops 8000000000 | bytes 25000000 | tf_op jit(solution)/shard_map/window_grads/pallas_call | solution.py:99
  51.1 0.0 copy-start
  51.2 1.0 copy-done
  52.2 0.0 copy-start.1
  52.2 1.0 copy-done.1
  53.2 1.3 collective-permute-start.3
  54.5 4.6 %collective-permute-start.4 = (bf16[2,256,512]{2,1,0:T(8,128)(2,1)S(1)}, bf16[2,256,512]{2,1,0:T(8,128)(2,1)S(1)}, u32[]{:S(2)}, u32[]{:S(2)}) collective-permute-start(bf16[2,256,512]{2,1,0:T(8,128)(2,1)S(1)} %get-tuple-element.45), channel_id=1, source_target_pairs={{0,8},{8,16},{16,24},{24,32},{32,40},{40,48},{48,56},{56,64},{64,7... | collective-permute-start | bytes 1572872 | tf_op jit(solution)/shard_map/ppermute | solution.py:251
  59.1 9.9 %collective-permute-done.3.low_ref = bf16[2,256,512]{2,1,0:T(8,128)(2,1)S(1)} collective-permute-done((bf16[2,256,512]{2,1,0:T(8,128)(2,1)S(1)}, bf16[2,256,512]{2,1,0:T(8,128)(2,1)S(1)}, u32[]{:S(2)}, u32[]{:S(2)}) %collective-permute-start.3) | collective-permute-done | bytes 524320 | tf_op jit(solution)/shard_map/ppermute | solution.py:251
  69.0 0.0 copy-start.3
  69.0 1.2 collective-permute-done.4.high_ref
  70.2 0.0 copy-start.4
  70.2 0.0 all-to-all-done.1.own_ref
  70.2 0.0 copy-start.2
  70.2 0.0 collective-permute-start.5
  70.2 0.8 copy-done.4
  71.0 15.2 %all-to-all-start = ((bf16[32,2,8,512]{3,2,1,0:T(8,128)(2,1)}), bf16[32,2,8,512]{3,2,1,0:T(8,128)(2,1)S(1)}, u32[]{:S(2)}, u32[]{:S(2)}) async-start(bf16[32,2,8,512]{3,2,1,0:T(8,128)(2,1)} %get-tuple-element.41), calls=%async_computation | async-start | bytes 1048576 | tf_op jit(solution)/shard_map/all_to_all | solution.py:351
  86.2 0.1 pad_add_fusion.pos
  86.3 0.0 copy-done.3
  86.3 2.7 %join_rims.1 = (bf16[512,512]{1,0:T(8,128)(2,1)}, bf16[512,512]{1,0:T(8,128)(2,1)}) custom-call(f32[512,512]{1,0:T(8,128)} %copy-done, f32[512,512]{1,0:T(8,128)} %copy-done.1, bf16[2,256,512]{2,1,0:T(8,128)(2,1)} %copy-done.3, bf16[2,256,512]{2,1,0:T(8,128)(2,1)} %copy-done.4), custom_call_target="tpu_custom_call" | custom-call | tf_op jit(solution)/shard_map/join_rims/pallas_call | solution.py:215
  89.0 0.0 copy-done.2
  89.0 20.6 %all-to-all-done = bf16[32,2,8,512]{3,2,1,0:T(8,128)(2,1)S(1)} async-done(((bf16[32,2,8,512]{3,2,1,0:T(8,128)(2,1)}), bf16[32,2,8,512]{3,2,1,0:T(8,128)(2,1)S(1)}, u32[]{:S(2)}, u32[]{:S(2)}) %all-to-all-start) | async-done | bytes 524320 | tf_op jit(solution)/shard_map/all_to_all | solution.py:351
  109.6 0.8 copy_bitcast_fusion
  110.5 0.0 collective-permute-done.5.other_ref
  110.5 6.3 %all-gather.2.cloned.1.call-done = bf16[4096,512]{1,0:T(8,128)(2,1)} async-done(((bf16[128,512]{1,0:T(8,128)(2,1)}), bf16[4096,512]{1,0:T(8,128)(2,1)}) %all-gather.2.cloned.1.call-update) | async-done | bytes 4194320 | tf_op jit(solution)/shard_map/all_gather | solution.py:342
  116.8 5.8 %byte_product.1 = bf16[512,512]{1,0:T(8,128)(2,1)} custom-call(s32[3]{0:T(128)S(1)} %pad_add_fusion.pos, bf16[4,512,512]{2,1,0:T(8,128)(2,1)} %copy-done.2, bf16[4,512,512]{2,1,0:T(8,128)(2,1)} %collective-permute-done.5.other_ref, bf16[8,512,512]{2,1,0:T(8,128)(2,1)} %bitcast.12), custom_call_target="tpu_custom_call" | custom-call | tf_op jit(solution)/shard_map/byte_product/pallas_call | solution.py:303
Async XLA Ops:
  7.2 109.6 %all-gather.2.cloned.1.call-start = ((), (), s32[]{:S(2)}) async-start(), calls=%async_computation.2 | async-start | bytes 4325376 | tf_op jit(solution)/shard_map/all_gather | solution.py:342
  7.2 13.2 %collective-permute-start = (bf16[128,512]{1,0:T(8,128)(2,1)}, bf16[128,512]{1,0:T(8,128)(2,1)S(1)}, u32[]{:S(2)}, u32[]{:S(2)}) collective-permute-start(bf16[128,512]{1,0:T(8,128)(2,1)} %param.21), channel_id=1, source_target_pairs={{0,0},{1,32},{2,64},{3,96},{4,128},{5,160},{6,192},{7,224},{8,8},{... | collective-permute-start | bytes 393224 | tf_op jit(solution)/shard_map/ppermute | solution.py:270
  14.3 6.7 %copy-start.7 = (bf16[2,256,512]{2,1,0:T(8,128)(2,1)S(1)}, bf16[2,256,512]{2,1,0:T(8,128)(2,1)}, u32[]{:S(2)}) copy-start(bf16[2,256,512]{2,1,0:T(8,128)(2,1)} %get-tuple-element.36) | copy-start | bytes 1572868
  14.3 10.9 %copy-start.6 = (bf16[2,256,512]{2,1,0:T(8,128)(2,1)S(1)}, bf16[2,256,512]{2,1,0:T(8,128)(2,1)}, u32[]{:S(2)}) copy-start(bf16[2,256,512]{2,1,0:T(8,128)(2,1)} %get-tuple-element.37) | copy-start | bytes 1572868
  20.4 0.6 copy-start.5
  21.0 15.4 %collective-permute-start.1 = (bf16[2,256,512]{2,1,0:T(8,128)(2,1)S(1)}, bf16[2,256,512]{2,1,0:T(8,128)(2,1)}, u32[]{:S(2)}, u32[]{:S(2)}) collective-permute-start(bf16[2,256,512]{2,1,0:T(8,128)(2,1)S(1)} %copy-done.7), channel_id=1, source_target_pairs={{0,8},{8,16},{16,24},{24,32},{32,40},{40,48},{48,56},{56,64},{64,7... | collective-permute-start | bytes 1572872 | tf_op jit(solution)/shard_map/ppermute | solution.py:251
  25.3 17.5 %collective-permute-start.2 = (bf16[2,256,512]{2,1,0:T(8,128)(2,1)S(1)}, bf16[2,256,512]{2,1,0:T(8,128)(2,1)}, u32[]{:S(2)}, u32[]{:S(2)}) collective-permute-start(bf16[2,256,512]{2,1,0:T(8,128)(2,1)S(1)} %copy-done.6), channel_id=1, source_target_pairs={{8,0},{16,8},{24,16},{32,24},{40,32},{48,40},{56,48},{64,56},{72,6... | collective-permute-start | bytes 1572872 | tf_op jit(solution)/shard_map/ppermute | solution.py:251
  26.5 43.6 %all-to-all-start.1 = ((bf16[4,512,512]{2,1,0:T(8,128)(2,1)}), bf16[4,512,512]{2,1,0:T(8,128)(2,1)S(1)}, u32[]{:S(2)}, u32[]{:S(2)}) async-start(bf16[4,512,512]{2,1,0:T(8,128)(2,1)} %get-tuple-element.46), calls=%async_computation.1 | async-start | bytes 4194304 | tf_op jit(solution)/shard_map/all_to_all | solution.py:346
  51.1 1.0 copy-start
  52.2 1.0 copy-start.1
  53.2 15.8 %collective-permute-start.3 = (bf16[2,256,512]{2,1,0:T(8,128)(2,1)S(1)}, bf16[2,256,512]{2,1,0:T(8,128)(2,1)S(1)}, u32[]{:S(2)}, u32[]{:S(2)}) collective-permute-start(bf16[2,256,512]{2,1,0:T(8,128)(2,1)S(1)} %get-tuple-element.44), channel_id=1, source_target_pairs={{8,0},{16,8},{24,16},{32,24},{40,32},{48,40},{56,48},{64,56},{72,6... | collective-permute-start | bytes 1572872 | tf_op jit(solution)/shard_map/ppermute | solution.py:251
  54.5 15.7 %collective-permute-start.4 = (bf16[2,256,512]{2,1,0:T(8,128)(2,1)S(1)}, bf16[2,256,512]{2,1,0:T(8,128)(2,1)S(1)}, u32[]{:S(2)}, u32[]{:S(2)}) collective-permute-start(bf16[2,256,512]{2,1,0:T(8,128)(2,1)S(1)} %get-tuple-element.45), channel_id=1, source_target_pairs={{0,8},{8,16},{16,24},{24,32},{32,40},{40,48},{48,56},{56,64},{64,7... | collective-permute-start | bytes 1572872 | tf_op jit(solution)/shard_map/ppermute | solution.py:251
  69.0 17.3 %copy-start.3 = (bf16[2,256,512]{2,1,0:T(8,128)(2,1)}, bf16[2,256,512]{2,1,0:T(8,128)(2,1)S(1)}, u32[]{:S(2)}) copy-start(bf16[2,256,512]{2,1,0:T(8,128)(2,1)S(1)} %collective-permute-done.3.low_ref) | copy-start | bytes 1572868
  70.2 0.8 copy-start.4
  70.2 18.8 %copy-start.2 = (bf16[4,512,512]{2,1,0:T(8,128)(2,1)}, bf16[4,512,512]{2,1,0:T(8,128)(2,1)S(1)}, u32[]{:S(2)}) copy-start(bf16[4,512,512]{2,1,0:T(8,128)(2,1)S(1)} %all-to-all-done.1.own_ref) | copy-start | bytes 6291460
  70.2 40.3 %collective-permute-start.5 = (bf16[4,512,512]{2,1,0:T(8,128)(2,1)S(1)}, bf16[4,512,512]{2,1,0:T(8,128)(2,1)}, u32[]{:S(2)}, u32[]{:S(2)}) collective-permute-start(bf16[4,512,512]{2,1,0:T(8,128)(2,1)S(1)} %all-to-all-done.1.own_ref), channel_id=1, source_target_pairs={{0,1},{1,0},{2,3},{3,2},{4,5},{5,4},{6,7},{7,6},{8,9},{9,8},{10,11... | collective-permute-start | bytes 6291464 | tf_op jit(solution)/shard_map/ppermute | solution.py:270
  71.0 38.6 %all-to-all-start = ((bf16[32,2,8,512]{3,2,1,0:T(8,128)(2,1)}), bf16[32,2,8,512]{3,2,1,0:T(8,128)(2,1)S(1)}, u32[]{:S(2)}, u32[]{:S(2)}) async-start(bf16[32,2,8,512]{3,2,1,0:T(8,128)(2,1)} %get-tuple-element.41), calls=%async_computation | async-start | bytes 1048576 | tf_op jit(solution)/shard_map/all_to_all | solution.py:351
Sparse Core Ops, SparseCore 0:
  21.2 95.5 all-gather.1

commit v5 on v4

--- a/solution.py
+++ b/solution.py
@@ -254,6 +254,7 @@
 NZ, NX, NY, NC = 8, 4, 4, 2
 AXES = ("z", "x", "y", "core")
 SEQ = ("z", "x")
+SHIFTS = (0, 1, -1, 2)
 
 
 def place(z, x, y, c):
@@ -270,17 +271,19 @@
     return lax.ppermute(block, AXES, route)
 
 
-def product_kernel(
-    pos, own_ref, other_ref, whole_ref, out_ref, a_buf, w_buf, a_sem, w_sem
-):
+def product_kernel(pos, *refs):
+    row_refs = refs[:NZ]
+    whole_ref, out_ref, a_buf, w_buf, a_sem, w_sem = refs[NZ:]
     m, c = pos[1], pos[2]
+    y = lax.div(m, NC)
     copies = []
     for j in range(NZ):
-        rows, core = (own_ref, c) if j % NC == 0 else (other_ref, 1 - c)
-        slot = lax.rem(NC * (j // NC) + core + m, NZ)
+        core = c if j < NY else 1 - c
+        from_y = lax.rem(y - SHIFTS[j % NY] + NY, NY)
+        slot = lax.rem(NC * from_y + core + m, NZ)
         copies.append(
             (
-                pltpu.make_async_copy(rows.at[j // NC], a_buf.at[j], a_sem.at[j]),
+                pltpu.make_async_copy(row_refs[j], a_buf.at[j], a_sem.at[j]),
                 pltpu.make_async_copy(whole_ref.at[slot], w_buf.at[j], w_sem.at[j]),
             )
         )
@@ -296,8 +299,8 @@
     out_ref[...] = total.astype(BF16)
 
 
-def product_call(pos, own_rows, other_rows, whole):
-    count, width = own_rows.shape[1:]
+def product_call(pos, rows, whole):
+    count, width = rows[0].shape
     n_rows = whole.shape[1]
     anywhere = pl.BlockSpec(memory_space=pl.ANY)
     return pl.pallas_call(
@@ -305,7 +308,7 @@
         grid_spec=pltpu.PrefetchScalarGridSpec(
             num_scalar_prefetch=1,
             grid=(1,),
-            in_specs=[anywhere] * 3,
+            in_specs=[anywhere] * (len(rows) + 1),
             out_specs=pl.BlockSpec((count, n_rows), lambda i, p: (0, 0)),
             scratch_shapes=[
                 pltpu.VMEM((NZ, count, width), BF16),
@@ -317,7 +320,7 @@
         out_shape=jax.ShapeDtypeStruct((count, n_rows), BF16),
         name="byte_product",
         compiler_params=pltpu.CompilerParams(vmem_limit_bytes=40 << 20),
-    )(pos, *in_hbm(own_rows, other_rows, whole))
+    )(pos, *in_hbm(*rows, whole))
 
 
 def local(
@@ -332,31 +335,33 @@
     pos = jnp.stack([x, y * NC + core, core]).astype(jnp.int32)
     own = send(w_query, lambda z, x, y, c: (z + NC * y + c, x, z // NC, z % NC))
     low_rim, high_rim = pack_call(win_key, win_value)
-    cross_query, low_rim = lax.optimization_barrier((cross_query, low_rim))
-    cross_dq, buffer = cross_call(
-        cross_query, cross_dout, patch_key, patch_value, patch_len, patch_owner, seq_count, NY
-    )
-    own, cross_dq, buffer, low_rim, high_rim = lax.optimization_barrier(
-        (own, cross_dq, buffer, low_rim, high_rim)
+    own, low_rim, high_rim, cross_query = lax.optimization_barrier(
+        (own, low_rim, high_rim, cross_query)
     )
     whole = lax.all_gather(own, SEQ, axis=0, tiled=True)
     whole = whole.reshape(NZ, NX * own.shape[0], own.shape[1])
+    cross_dq, buffer = cross_call(
+        cross_query, cross_dout, patch_key, patch_value, patch_len, patch_owner, seq_count, 1
+    )
     before = shifted(low_rim, SEQ, 1)
     after = shifted(high_rim, SEQ, -1)
-    own_rows = lax.all_to_all(cross_dq, "y", split_axis=0, concat_axis=0, tiled=True)
+    cross_dq = cross_dq.reshape(cross_dq.shape[1:])
+    rows = [cross_dq] + [
+        send(cross_dq, lambda z, x, y, c, dy=dy: (z, x, y + dy, c)) for dy in SHIFTS[1:]
+    ]
     win_dq, dk, dv, low_send, high_send = window_call(
         flags, win_query, win_dout, win_key, win_value, before, after
     )
     win_dq, buffer = lax.optimization_barrier((win_dq, buffer))
     arrived = lax.all_to_all(buffer, SEQ, split_axis=0, concat_axis=0, tiled=True)
+    rows, win_dq = lax.optimization_barrier((rows, win_dq))
+    rows = rows + [send(r, lambda z, x, y, c: (z, x, y, 1 - c)) for r in rows]
+    rows, low_send, high_send = lax.optimization_barrier((rows, low_send, high_send))
     low_back = shifted(low_send, SEQ, -1)
     high_back = shifted(high_send, SEQ, 1)
-    low_back, high_back, own_rows = lax.optimization_barrier((low_back, high_back, own_rows))
-    other_rows = send(own_rows, lambda z, x, y, c: (z, x, y, 1 - c))
     win_dk, win_dv = join_call(dk, dv, low_back, high_back)
-    arrived, win_dk = lax.optimization_barrier((arrived, win_dk))
     patch_grads = arrived.transpose(1, 0, 2, 3).reshape(2, -1, arrived.shape[3])
-    byte_grads = product_call(pos, own_rows, other_rows, whole)
+    byte_grads = product_call(pos, rows, whole)
     return (win_dq, win_dk, win_dv, patch_grads, byte_grads)
 
 

time: 130 us -> 132 us (1.015)
  waiting for transfers between devices: 45.9 us -> 48.4 us
  starting transfers between devices: 40.2 us -> 38.3 us
    all_to_all x1, waiting for transfers between devices: 20.6 us -> 4.25 us  [local(): lax.all_to_all(buffer, SEQ, split_axis=0, concat_axis=0, tiled=True)]
    all_gather x1, waiting for transfers between devices: 6.3 us -> 18 us  [local(): whole = lax.all_gather(own, SEQ, axis=0, tiled=True)]
    ppermute x2 -> x8, waiting for transfers between devices: 0.21 us -> 9.19 us  [send(): return lax.ppermute(block, AXES, route)]
    all_to_all x1 -> x0, starting transfers between devices: 8.53 us -> none  [local(): lax.all_to_all(cross_dq, 'y', split_axis=0, concat_axis=0, tiled=True)]
    ppermute x2 -> x8, starting transfers between devices: 5.07 us -> 13.3 us  [send(): return lax.ppermute(block, AXES, route)]
    ppermute x4, waiting for transfers between devices: 18.7 us -> 16.9 us  [shifted(): return lax.ppermute(block, axis, route)]
    all_to_all x1, starting transfers between devices: 15.2 us -> 13.6 us  [local(): lax.all_to_all(buffer, SEQ, split_axis=0, concat_axis=0, tiled=True)]
    unnamed x16 -> x24, local copies, waits for them, and re-layouts: 3.47 us -> 4.26 us
  transfers between devices with their start and end apart: 9 -> 14, of which waited for: 7 -> 8; matrix products, arithmetic and copies ran while one was open for 1% -> 1% of each run, Pallas kernels for 15% -> 14%
where the time goes in v5:
time: 132 us; the launch traced here: 131 us
  waiting for transfers between devices  48.4 us (37%)
  starting transfers between devices  38.3 us (29%)
  Pallas kernels  24.8 us (19%)
  between operations  14.2 us (11%)
  local copies, waits for them, and re-layouts  5.09 us (4%)
    all_gather x1, waiting for transfers between devices, local(): whole = lax.all_gather(own, SEQ, axis=0, tiled=True)  18 us
    ppermute x4, waiting for transfers between devices, shifted(): return lax.ppermute(block, axis, route)  16.9 us
    all_to_all x1, starting transfers between devices, local(): lax.all_to_all(buffer, SEQ, split_axis=0, concat_axis=0, tiled=True)  13.6 us
    ppermute x8, starting transfers between devices, send(): return lax.ppermute(block, AXES, route)  13.3 us
    ppermute x4, starting transfers between devices, shifted(): return lax.ppermute(block, axis, route)  11.4 us
    ppermute x8, waiting for transfers between devices, send(): return lax.ppermute(block, AXES, route)  9.19 us
    pallas_call x1, Pallas kernels, window_call(): pl.pallas_call(window_kernel, grid_spec=pltpu.PrefetchScalarGridSpec(num_...  8.39 us
    pallas_call x1, Pallas kernels, product_call(): pl.pallas_call(product_kernel, grid_spec=pltpu.PrefetchScalarGridSpec(num...  6.01 us
  transfers between devices with their start and end apart: 14, of which 8 were waited for; matrix products, arithmetic and copies ran while one was open for 1% of the time, Pallas kernels for 14%

profile of v5, /device:TPU:8, one launch (start us, length us, event | category | flops | bytes accessed | tf_op | source)
XLA Modules:
  0.0 130.9 jit_solution(10352209107793154793)
XLA Ops:
  7.2 0.0 all-gather.2.cloned.1.call-start
  7.2 5.1 %collective-permute-start = (bf16[128,512]{1,0:T(8,128)(2,1)}, bf16[128,512]{1,0:T(8,128)(2,1)S(1)}, u32[]{:S(2)}, u32[]{:S(2)}) collective-permute-start(bf16[128,512]{1,0:T(8,128)(2,1)} %param.21), channel_id=1, source_target_pairs={{0,0},{1,32},{2,64},{3,96},{4,128},{5,160},{6,192},{7,224},{8,8},{... | collective-permute-start | bytes 393224 | tf_op jit(solution)/shard_map/ppermute | solution.py:271
  12.3 2.0 %pack_rims.1 = (bf16[2,256,512]{2,1,0:T(8,128)(2,1)}, bf16[2,256,512]{2,1,0:T(8,128)(2,1)}) custom-call(bf16[512,512]{1,0:T(8,128)(2,1)} %k_ref.5, bf16[512,512]{1,0:T(8,128)(2,1)} %v_ref.5), custom_call_target="tpu_custom_call" | custom-call | tf_op jit(solution)/shard_map/pack_rims/pallas_call | solution.py:238
  14.3 6.0 %collective-permute-done = bf16[128,512]{1,0:T(8,128)(2,1)S(1)} collective-permute-done((bf16[128,512]{1,0:T(8,128)(2,1)}, bf16[128,512]{1,0:T(8,128)(2,1)S(1)}, u32[]{:S(2)}, u32[]{:S(2)}) %collective-permute-start) | collective-permute-done | bytes 131104 | tf_op jit(solution)/shard_map/ppermute | solution.py:271
  20.4 0.6 copy-done.9
  21.0 0.0 all-gather.2.cloned.1.call-update
  21.1 3.4 %collective-permute-start.4 = (bf16[2,256,512]{2,1,0:T(8,128)(2,1)}, bf16[2,256,512]{2,1,0:T(8,128)(2,1)S(1)}, u32[]{:S(2)}, u32[]{:S(2)}) collective-permute-start(bf16[2,256,512]{2,1,0:T(8,128)(2,1)} %get-tuple-element.41), channel_id=1, source_target_pairs={{0,8},{8,16},{16,24},{24,32},{32,40},{40,48},{48,56},{56,64},{64,7... | collective-permute-start | bytes 1572872 | tf_op jit(solution)/shard_map/ppermute | solution.py:251
  24.5 1.3 collective-permute-start.5
  25.8 0.1 add_convert_fusion.flags
  25.9 5.7 %cross_grads.1 = (bf16[1,512,512]{2,1,0:T(8,128)(2,1)S(1)}, bf16[32,2,8,512]{3,2,1,0:T(8,128)(2,1)}) custom-call(bf16[512,512]{1,0:T(8,128)(2,1)} %q_ref.1, bf16[512,512]{1,0:T(8,128)(2,1)} %do_ref.2, bf16[128,512]{1,0:T(8,128)(2,1)} %k_ref.4, bf16[128,512]{1,0:T(8,128)(2,1)} %v_ref.4, s32[2,64]{1,0:T(2,128)} %len_ref.1, s32[1,128]{1,0:T(1,128)} %bitcast.19), custom_call_target="tpu_custom_call" | custom-call | flops 5000000000 | bytes 15000000 | tf_op jit(solution)/shard_map/cross_grads/pallas_call | solution.py:177
  31.5 1.5 %collective-permute-start.1 = (bf16[512,512]{1,0:T(8,128)(2,1)S(1)}, bf16[512,512]{1,0:T(8,128)(2,1)S(1)}, u32[]{:S(2)}, u32[]{:S(2)}) collective-permute-start(bf16[512,512]{1,0:T(8,128)(2,1)S(1)} %bitcast.13), channel_id=1, source_target_pairs={{0,2},{1,3},{2,4},{3,5},{4,6},{5,7},{6,0},{7,1},{8,10},{9,11},{10,... | collective-permute-start | bytes 1572872 | tf_op jit(solution)/shard_map/ppermute | solution.py:271
  33.0 0.5 collective-permute-start.2
  33.6 5.1 %collective-permute-start.3 = (bf16[512,512]{1,0:T(8,128)(2,1)S(1)}, bf16[512,512]{1,0:T(8,128)(2,1)}, u32[]{:S(2)}, u32[]{:S(2)}) collective-permute-start(bf16[512,512]{1,0:T(8,128)(2,1)S(1)} %bitcast.15), channel_id=1, source_target_pairs={{0,4},{1,5},{2,6},{3,7},{4,0},{5,1},{6,2},{7,3},{8,12},{9,13},{10,... | collective-permute-start | bytes 1572872 | tf_op jit(solution)/shard_map/ppermute | solution.py:271
  38.7 0.0 collective-permute-done.4.before_ref
  38.7 0.0 collective-permute-done.5.after_ref
  38.7 0.8 copy-done.10
  39.5 0.8 copy-done.11
  40.3 8.4 %window_grads.1 = (bf16[512,512]{1,0:T(8,128)(2,1)}, f32[512,512]{1,0:T(8,128)S(1)}, f32[512,512]{1,0:T(8,128)S(1)}, bf16[2,256,512]{2,1,0:T(8,128)(2,1)S(1)}, bf16[2,256,512]{2,1,0:T(8,128)(2,1)S(1)}) custom-call(s32[2]{0:T(128)S(1)} %add_convert_fusion.flags, bf16[512,512]{1,0:T(8,128)(2,1)} %q_ref.2, bf16[512,512]{1,0:T(8,128)(2,1)} %do_ref.3, ...), custom_call_target="tpu_custom_call" | custom-call | flops 8000000000 | bytes 25000000 | tf_op jit(solution)/shard_map/window_grads/pallas_call | solution.py:99
  48.7 1.0 copy-done
  49.7 1.0 copy-done.1
  50.7 13.6 %all-to-all-start = ((bf16[32,2,8,512]{3,2,1,0:T(8,128)(2,1)}), bf16[32,2,8,512]{3,2,1,0:T(8,128)(2,1)S(1)}, u32[]{:S(2)}, u32[]{:S(2)}) async-start(bf16[32,2,8,512]{3,2,1,0:T(8,128)(2,1)} %get-tuple-element.59), calls=%async_computation | async-start | bytes 1048576 | tf_op jit(solution)/shard_map/all_to_all | solution.py:356
  64.2 0.0 collective-permute-done.1.refs_1_
  64.3 0.0 copy-start.3
  64.3 0.0 collective-permute-done.2.refs_2_
  64.3 0.0 collective-permute-done.3.refs_3_
  64.3 0.0 copy-done.2
  64.3 0.1 collective-permute-start.6
  64.4 0.5 collective-permute-start.7
  64.9 0.1 collective-permute-start.8
  65.0 0.4 collective-permute-start.9
  65.4 0.9 collective-permute-done.6.refs_4_
  66.3 1.5 %collective-permute-done.7.refs_5_ = bf16[512,512]{1,0:T(8,128)(2,1)S(1)} collective-permute-done((bf16[512,512]{1,0:T(8,128)(2,1)S(1)}, bf16[512,512]{1,0:T(8,128)(2,1)S(1)}, u32[]{:S(2)}, u32[]{:S(2)}) %collective-permute-start.7) | collective-permute-done | bytes 524320 | tf_op jit(solution)/shard_map/ppermute | solution.py:271
  67.8 0.7 collective-permute-done.8.refs_6_
  68.6 0.0 collective-permute-done.9.refs_7_
  68.6 1.3 collective-permute-start.10
  69.9 0.0 copy-done.5
  69.9 0.0 copy-done.6
  69.9 0.0 copy-done.7
  69.9 0.0 copy-done.8
  69.9 5.3 %collective-permute-start.11 = (bf16[2,256,512]{2,1,0:T(8,128)(2,1)S(1)}, bf16[2,256,512]{2,1,0:T(8,128)(2,1)}, u32[]{:S(2)}, u32[]{:S(2)}) collective-permute-start(bf16[2,256,512]{2,1,0:T(8,128)(2,1)S(1)} %get-tuple-element.56), channel_id=1, source_target_pairs={{0,8},{8,16},{16,24},{24,32},{32,40},{40,48},{48,56},{56,64},{64,7... | collective-permute-start | bytes 1572872 | tf_op jit(solution)/shard_map/ppermute | solution.py:251
  75.2 0.1 pad_add_fusion.pos
  75.3 4.2 %all-to-all-done = bf16[32,2,8,512]{3,2,1,0:T(8,128)(2,1)S(1)} async-done(((bf16[32,2,8,512]{3,2,1,0:T(8,128)(2,1)}), bf16[32,2,8,512]{3,2,1,0:T(8,128)(2,1)S(1)}, u32[]{:S(2)}, u32[]{:S(2)}) %all-to-all-start) | async-done | bytes 524320 | tf_op jit(solution)/shard_map/all_to_all | solution.py:356
  79.6 0.8 copy_bitcast_fusion
  80.4 14.0 %collective-permute-done.10.low_ref = bf16[2,256,512]{2,1,0:T(8,128)(2,1)} collective-permute-done((bf16[2,256,512]{2,1,0:T(8,128)(2,1)S(1)}, bf16[2,256,512]{2,1,0:T(8,128)(2,1)}, u32[]{:S(2)}, u32[]{:S(2)}) %collective-permute-start.10) | collective-permute-done | bytes 524320 | tf_op jit(solution)/shard_map/ppermute | solution.py:251
  94.4 3.0 %collective-permute-done.11.high_ref = bf16[2,256,512]{2,1,0:T(8,128)(2,1)} collective-permute-done((bf16[2,256,512]{2,1,0:T(8,128)(2,1)S(1)}, bf16[2,256,512]{2,1,0:T(8,128)(2,1)}, u32[]{:S(2)}, u32[]{:S(2)}) %collective-permute-start.11) | collective-permute-done | bytes 524320 | tf_op jit(solution)/shard_map/ppermute | solution.py:251
  97.3 2.7 %join_rims.1 = (bf16[512,512]{1,0:T(8,128)(2,1)}, bf16[512,512]{1,0:T(8,128)(2,1)}) custom-call(f32[512,512]{1,0:T(8,128)} %copy-done, f32[512,512]{1,0:T(8,128)} %copy-done.1, bf16[2,256,512]{2,1,0:T(8,128)(2,1)} %collective-permute-done.10.low_ref, bf16[2,256,512]{2,1,0:T(8,128)(2,1)} %collective-permute-done.11.high_ref), custom_call_target="tpu_custom_call" | custom-call | tf_op jit(solution)/shard_map/join_rims/pallas_call | solution.py:215
  100.0 18.0 %all-gather.2.cloned.1.call-done = bf16[4096,512]{1,0:T(8,128)(2,1)} async-done(((bf16[128,512]{1,0:T(8,128)(2,1)}), bf16[4096,512]{1,0:T(8,128)(2,1)}) %all-gather.2.cloned.1.call-update) | async-done | bytes 4194320 | tf_op jit(solution)/shard_map/all_gather | solution.py:341
  118.0 6.0 %byte_product.1 = bf16[512,512]{1,0:T(8,128)(2,1)} custom-call(s32[3]{0:T(128)S(1)} %pad_add_fusion.pos, bf16[512,512]{1,0:T(8,128)(2,1)} %bitcast.17, bf16[512,512]{1,0:T(8,128)(2,1)} %copy-done.3, bf16[512,512]{1,0:T(8,128)(2,1)} %copy-done.4, bf16[512,512]{1,0:T(8,128)(2,1)} %collective-permute-done.3.refs_3_, bf16[512,512]{1,0:T(8,128)(2,1)} %copy-done.5, ...), custom_call_target="tpu_custom_call" | custom-call | tf_op jit(solution)/shard_map/byte_product/pallas_call | solution.py:306
  (13 shorter events, 0.0 us)
Async XLA Ops:
  7.2 110.8 %all-gather.2.cloned.1.call-start = ((), (), s32[]{:S(2)}) async-start(), calls=%async_computation.1 | async-start | bytes 4325376 | tf_op jit(solution)/shard_map/all_gather | solution.py:341
  7.2 13.2 %collective-permute-start = (bf16[128,512]{1,0:T(8,128)(2,1)}, bf16[128,512]{1,0:T(8,128)(2,1)S(1)}, u32[]{:S(2)}, u32[]{:S(2)}) collective-permute-start(bf16[128,512]{1,0:T(8,128)(2,1)} %param.21), channel_id=1, source_target_pairs={{0,0},{1,32},{2,64},{3,96},{4,128},{5,160},{6,192},{7,224},{8,8},{... | collective-permute-start | bytes 393224 | tf_op jit(solution)/shard_map/ppermute | solution.py:271
  20.4 0.7 copy-start.9
  21.1 17.6 %collective-permute-start.4 = (bf16[2,256,512]{2,1,0:T(8,128)(2,1)}, bf16[2,256,512]{2,1,0:T(8,128)(2,1)S(1)}, u32[]{:S(2)}, u32[]{:S(2)}) collective-permute-start(bf16[2,256,512]{2,1,0:T(8,128)(2,1)} %get-tuple-element.41), channel_id=1, source_target_pairs={{0,8},{8,16},{16,24},{24,32},{32,40},{40,48},{48,56},{56,64},{64,7... | collective-permute-start | bytes 1572872 | tf_op jit(solution)/shard_map/ppermute | solution.py:251
  24.5 14.2 %collective-permute-start.5 = (bf16[2,256,512]{2,1,0:T(8,128)(2,1)}, bf16[2,256,512]{2,1,0:T(8,128)(2,1)S(1)}, u32[]{:S(2)}, u32[]{:S(2)}) collective-permute-start(bf16[2,256,512]{2,1,0:T(8,128)(2,1)} %get-tuple-element.42), channel_id=1, source_target_pairs={{8,0},{16,8},{24,16},{32,24},{40,32},{48,40},{56,48},{64,56},{72,6... | collective-permute-start | bytes 1572872 | tf_op jit(solution)/shard_map/ppermute | solution.py:251
  31.5 32.8 %copy-start.2 = (bf16[1,512,512]{2,1,0:T(8,128)(2,1)}, bf16[1,512,512]{2,1,0:T(8,128)(2,1)S(1)}, u32[]{:S(2)}) copy-start(bf16[1,512,512]{2,1,0:T(8,128)(2,1)S(1)} %get-tuple-element.40) | copy-start | bytes 1572868
  31.5 32.7 %collective-permute-start.1 = (bf16[512,512]{1,0:T(8,128)(2,1)S(1)}, bf16[512,512]{1,0:T(8,128)(2,1)S(1)}, u32[]{:S(2)}, u32[]{:S(2)}) collective-permute-start(bf16[512,512]{1,0:T(8,128)(2,1)S(1)} %bitcast.13), channel_id=1, source_target_pairs={{0,2},{1,3},{2,4},{3,5},{4,6},{5,7},{6,0},{7,1},{8,10},{9,11},{10,... | collective-permute-start | bytes 1572872 | tf_op jit(solution)/shard_map/ppermute | solution.py:271
  33.0 31.2 %collective-permute-start.2 = (bf16[512,512]{1,0:T(8,128)(2,1)S(1)}, bf16[512,512]{1,0:T(8,128)(2,1)S(1)}, u32[]{:S(2)}, u32[]{:S(2)}) collective-permute-start(bf16[512,512]{1,0:T(8,128)(2,1)S(1)} %bitcast.14), channel_id=1, source_target_pairs={{0,6},{1,7},{2,0},{3,1},{4,2},{5,3},{6,4},{7,5},{8,14},{9,15},{10,... | collective-permute-start | bytes 1572872 | tf_op jit(solution)/shard_map/ppermute | solution.py:271
  33.6 30.7 %collective-permute-start.3 = (bf16[512,512]{1,0:T(8,128)(2,1)S(1)}, bf16[512,512]{1,0:T(8,128)(2,1)}, u32[]{:S(2)}, u32[]{:S(2)}) collective-permute-start(bf16[512,512]{1,0:T(8,128)(2,1)S(1)} %bitcast.15), channel_id=1, source_target_pairs={{0,4},{1,5},{2,6},{3,7},{4,0},{5,1},{6,2},{7,3},{8,12},{9,13},{10,... | collective-permute-start | bytes 1572872 | tf_op jit(solution)/shard_map/ppermute | solution.py:271
  38.7 0.8 copy-start.10
  39.5 0.8 copy-start.11
  48.7 1.0 copy-start
  49.7 1.0 copy-start.1
  50.7 28.9 %all-to-all-start = ((bf16[32,2,8,512]{3,2,1,0:T(8,128)(2,1)}), bf16[32,2,8,512]{3,2,1,0:T(8,128)(2,1)S(1)}, u32[]{:S(2)}, u32[]{:S(2)}) async-start(bf16[32,2,8,512]{3,2,1,0:T(8,128)(2,1)} %get-tuple-element.59), calls=%async_computation | async-start | bytes 1048576 | tf_op jit(solution)/shard_map/all_to_all | solution.py:356
  64.3 53.7 %copy-start.3 = (bf16[512,512]{1,0:T(8,128)(2,1)}, bf16[512,512]{1,0:T(8,128)(2,1)S(1)}, u32[]{:S(2)}) copy-start(bf16[512,512]{1,0:T(8,128)(2,1)S(1)} %collective-permute-done.1.refs_1_) | copy-start | bytes 1572868
  64.3 53.7 %copy-start.4 = (bf16[512,512]{1,0:T(8,128)(2,1)}, bf16[512,512]{1,0:T(8,128)(2,1)S(1)}, u32[]{:S(2)}) copy-start(bf16[512,512]{1,0:T(8,128)(2,1)S(1)} %collective-permute-done.2.refs_2_) | copy-start | bytes 1572868
  64.3 2.0 %collective-permute-start.6 = (bf16[512,512]{1,0:T(8,128)(2,1)S(1)}, bf16[512,512]{1,0:T(8,128)(2,1)S(1)}, u32[]{:S(2)}, u32[]{:S(2)}) collective-permute-start(bf16[512,512]{1,0:T(8,128)(2,1)S(1)} %bitcast.16), channel_id=1, source_target_pairs={{0,1},{1,0},{2,3},{3,2},{4,5},{5,4},{6,7},{7,6},{8,9},{9,8},{10,11... | collective-permute-start | bytes 1572872 | tf_op jit(solution)/shard_map/ppermute | solution.py:271
  64.4 3.4 %collective-permute-start.7 = (bf16[512,512]{1,0:T(8,128)(2,1)S(1)}, bf16[512,512]{1,0:T(8,128)(2,1)S(1)}, u32[]{:S(2)}, u32[]{:S(2)}) collective-permute-start(bf16[512,512]{1,0:T(8,128)(2,1)S(1)} %collective-permute-done.1.refs_1_), channel_id=1, source_target_pairs={{0,1},{1,0},{2,3},{3,2},{4,5},{5,4},{6,7},{7,6},{8,9},{9,8},{10,11... | collective-permute-start | bytes 1572872 | tf_op jit(solution)/shard_map/ppermute | solution.py:271
  64.9 3.6 %collective-permute-start.8 = (bf16[512,512]{1,0:T(8,128)(2,1)S(1)}, bf16[512,512]{1,0:T(8,128)(2,1)S(1)}, u32[]{:S(2)}, u32[]{:S(2)}) collective-permute-start(bf16[512,512]{1,0:T(8,128)(2,1)S(1)} %collective-permute-done.2.refs_2_), channel_id=1, source_target_pairs={{0,1},{1,0},{2,3},{3,2},{4,5},{5,4},{6,7},{7,6},{8,9},{9,8},{10,11... | collective-permute-start | bytes 1572872 | tf_op jit(solution)/shard_map/ppermute | solution.py:271
  65.0 3.6 %collective-permute-start.9 = (bf16[512,512]{1,0:T(8,128)(2,1)}, bf16[512,512]{1,0:T(8,128)(2,1)S(1)}, u32[]{:S(2)}, u32[]{:S(2)}) collective-permute-start(bf16[512,512]{1,0:T(8,128)(2,1)} %collective-permute-done.3.refs_3_), channel_id=1, source_target_pairs={{0,1},{1,0},{2,3},{3,2},{4,5},{5,4},{6,7},{7,6},{8,9},{9,8},{10,11... | collective-permute-start | bytes 1572872 | tf_op jit(solution)/shard_map/ppermute | solution.py:271
  66.3 3.6 %copy-start.5 = (bf16[512,512]{1,0:T(8,128)(2,1)}, bf16[512,512]{1,0:T(8,128)(2,1)S(1)}, u32[]{:S(2)}) copy-start(bf16[512,512]{1,0:T(8,128)(2,1)S(1)} %collective-permute-done.6.refs_4_) | copy-start | bytes 1572868
  67.8 2.1 %copy-start.6 = (bf16[512,512]{1,0:T(8,128)(2,1)}, bf16[512,512]{1,0:T(8,128)(2,1)S(1)}, u32[]{:S(2)}) copy-start(bf16[512,512]{1,0:T(8,128)(2,1)S(1)} %collective-permute-done.7.refs_5_) | copy-start | bytes 1572868
  68.6 1.3 %copy-start.7 = (bf16[512,512]{1,0:T(8,128)(2,1)}, bf16[512,512]{1,0:T(8,128)(2,1)S(1)}, u32[]{:S(2)}) copy-start(bf16[512,512]{1,0:T(8,128)(2,1)S(1)} %collective-permute-done.8.refs_6_) | copy-start | bytes 1572868
  68.6 1.3 %copy-start.8 = (bf16[512,512]{1,0:T(8,128)(2,1)}, bf16[512,512]{1,0:T(8,128)(2,1)S(1)}, u32[]{:S(2)}) copy-start(bf16[512,512]{1,0:T(8,128)(2,1)S(1)} %collective-permute-done.9.refs_7_) | copy-start | bytes 1572868
  68.6 25.8 %collective-permute-start.10 = (bf16[2,256,512]{2,1,0:T(8,128)(2,1)S(1)}, bf16[2,256,512]{2,1,0:T(8,128)(2,1)}, u32[]{:S(2)}, u32[]{:S(2)}) collective-permute-start(bf16[2,256,512]{2,1,0:T(8,128)(2,1)S(1)} %get-tuple-element.55), channel_id=1, source_target_pairs={{8,0},{16,8},{24,16},{32,24},{40,32},{48,40},{56,48},{64,56},{72,6... | collective-permute-start | bytes 1572872 | tf_op jit(solution)/shard_map/ppermute | solution.py:251
  69.9 27.4 %collective-permute-start.11 = (bf16[2,256,512]{2,1,0:T(8,128)(2,1)S(1)}, bf16[2,256,512]{2,1,0:T(8,128)(2,1)}, u32[]{:S(2)}, u32[]{:S(2)}) collective-permute-start(bf16[2,256,512]{2,1,0:T(8,128)(2,1)S(1)} %get-tuple-element.56), channel_id=1, source_target_pairs={{0,8},{8,16},{16,24},{24,32},{32,40},{40,48},{48,56},{56,64},{64,7... | collective-permute-start | bytes 1572872 | tf_op jit(solution)/shard_map/ppermute | solution.py:251
Sparse Core Ops, SparseCore 0:
  21.2 96.7 all-gather.1

commit v6 on v4

--- a/solution.py
+++ b/solution.py
@@ -347,14 +347,14 @@
     win_dq, dk, dv, low_send, high_send = window_call(
         flags, win_query, win_dout, win_key, win_value, before, after
     )
-    win_dq, buffer = lax.optimization_barrier((win_dq, buffer))
     arrived = lax.all_to_all(buffer, SEQ, split_axis=0, concat_axis=0, tiled=True)
     low_back = shifted(low_send, SEQ, -1)
     high_back = shifted(high_send, SEQ, 1)
-    low_back, high_back, own_rows = lax.optimization_barrier((low_back, high_back, own_rows))
+    low_back, high_back, arrived, own_rows = lax.optimization_barrier(
+        (low_back, high_back, arrived, own_rows)
+    )
     other_rows = send(own_rows, lambda z, x, y, c: (z, x, y, 1 - c))
     win_dk, win_dv = join_call(dk, dv, low_back, high_back)
-    arrived, win_dk = lax.optimization_barrier((arrived, win_dk))
     patch_grads = arrived.transpose(1, 0, 2, 3).reshape(2, -1, arrived.shape[3])
     byte_grads = product_call(pos, own_rows, other_rows, whole)
     return (win_dq, win_dk, win_dv, patch_grads, byte_grads)

time: 130 us -> 131 us (level)
  waiting for transfers between devices: 45.9 us -> 50.8 us
  starting transfers between devices: 40.2 us -> 36.6 us
    all_gather x1, waiting for transfers between devices: 6.3 us -> 19 us  [local(): whole = lax.all_gather(own, SEQ, axis=0, tiled=True)]
    all_to_all x1, waiting for transfers between devices: 20.6 us -> 14.1 us  [local(): lax.all_to_all(buffer, SEQ, split_axis=0, concat_axis=0, tiled=True)]
    all_to_all x1, starting transfers between devices: 15.2 us -> 12 us  [local(): lax.all_to_all(buffer, SEQ, split_axis=0, concat_axis=0, tiled=True)]
    ppermute x4, waiting for transfers between devices: 18.7 us -> 17.3 us  [shifted(): return lax.ppermute(block, axis, route)]
    all_to_all x1, starting transfers between devices: 8.53 us -> 7.13 us  [local(): lax.all_to_all(cross_dq, 'y', split_axis=0, concat_axis=0, tiled=True)]
    unnamed x16 -> x12, local copies, waits for them, and re-layouts: 3.47 us -> 2.7 us
  transfers between devices with their start and end apart: 9 -> 9, of which waited for: 7 -> 5; matrix products, arithmetic and copies ran while one was open for 1% -> 1% of each run, Pallas kernels for 15% -> 15%
where the time goes in v6:
time: 131 us
  waiting for transfers between devices  50.8 us (39%)
  starting transfers between devices  36.6 us (28%)
  Pallas kernels  25.4 us (19%)
  between operations  14.1 us (11%)
  local copies, waits for them, and re-layouts  3.53 us (3%)
    all_gather x1, waiting for transfers between devices, local(): whole = lax.all_gather(own, SEQ, axis=0, tiled=True)  19 us
    ppermute x4, waiting for transfers between devices, shifted(): return lax.ppermute(block, axis, route)  17.3 us
    all_to_all x1, waiting for transfers between devices, local(): lax.all_to_all(buffer, SEQ, split_axis=0, concat_axis=0, tiled=True)  14.1 us
    ppermute x4, starting transfers between devices, shifted(): return lax.ppermute(block, axis, route)  12.4 us
    all_to_all x1, starting transfers between devices, local(): lax.all_to_all(buffer, SEQ, split_axis=0, concat_axis=0, tiled=True)  12 us
    pallas_call x1, Pallas kernels, window_call(): pl.pallas_call(window_kernel, grid_spec=pltpu.PrefetchScalarGridSpec(num_...  8.39 us
    all_to_all x1, starting transfers between devices, local(): lax.all_to_all(cross_dq, 'y', split_axis=0, concat_axis=0, tiled=True)  7.13 us
    pallas_call x1, Pallas kernels, product_call(): pl.pallas_call(product_kernel, grid_spec=pltpu.PrefetchScalarGridSpec(num...  5.85 us
  transfers between devices with their start and end apart: 9, of which 5 were waited for; matrix products, arithmetic and copies ran while one was open for 1% of the time, Pallas kernels for 15%

profile of v6, /device:TPU:8, one launch (start us, length us, event | category | flops | bytes accessed | tf_op | source)
XLA Modules:
  0.0 130.6 jit_solution(8365795609522674561)
XLA Ops:
  7.2 0.0 all-gather.2.cloned.1.call-start
  7.2 5.1 %collective-permute-start = (bf16[128,512]{1,0:T(8,128)(2,1)}, bf16[128,512]{1,0:T(8,128)(2,1)S(1)}, u32[]{:S(2)}, u32[]{:S(2)}) collective-permute-start(bf16[128,512]{1,0:T(8,128)(2,1)} %param.21), channel_id=1, source_target_pairs={{0,0},{1,32},{2,64},{3,96},{4,128},{5,160},{6,192},{7,224},{8,8},{... | collective-permute-start | bytes 393224 | tf_op jit(solution)/shard_map/ppermute | solution.py:270
  12.3 2.0 %pack_rims.1 = (bf16[2,256,512]{2,1,0:T(8,128)(2,1)}, bf16[2,256,512]{2,1,0:T(8,128)(2,1)}) custom-call(bf16[512,512]{1,0:T(8,128)(2,1)} %k_ref.5, bf16[512,512]{1,0:T(8,128)(2,1)} %v_ref.5), custom_call_target="tpu_custom_call" | custom-call | tf_op jit(solution)/shard_map/pack_rims/pallas_call | solution.py:238
  14.3 0.0 copy-start.5
  14.3 5.7 %cross_grads.1 = (bf16[4,512,512]{2,1,0:T(8,128)(2,1)}, bf16[32,2,8,512]{3,2,1,0:T(8,128)(2,1)}) custom-call(bf16[512,512]{1,0:T(8,128)(2,1)} %q_ref.1, bf16[512,512]{1,0:T(8,128)(2,1)} %do_ref.2, bf16[128,512]{1,0:T(8,128)(2,1)} %k_ref.4, bf16[128,512]{1,0:T(8,128)(2,1)} %v_ref.4, s32[2,64]{1,0:T(2,128)} %len_ref.1, s32[1,128]{1,0:T(1,128)} %bitcast.13), custom_call_target="tpu_custom_call" | custom-call | flops 5000000000 | bytes 15000000 | tf_op jit(solution)/shard_map/cross_grads/pallas_call | solution.py:177
  20.1 0.3 collective-permute-done
  20.4 0.0 copy-start.4
  20.4 0.6 copy-done.4
  21.0 0.0 all-gather.2.cloned.1.call-update
  21.0 12.0 %all-to-all-start = ((bf16[32,2,8,512]{3,2,1,0:T(8,128)(2,1)}), bf16[32,2,8,512]{3,2,1,0:T(8,128)(2,1)S(1)}, u32[]{:S(2)}, u32[]{:S(2)}) async-start(bf16[32,2,8,512]{3,2,1,0:T(8,128)(2,1)} %get-tuple-element.40), calls=%async_computation | async-start | bytes 1048576 | tf_op jit(solution)/shard_map/all_to_all | solution.py:350
  33.1 4.5 %collective-permute-start.1 = (bf16[2,256,512]{2,1,0:T(8,128)(2,1)}, bf16[2,256,512]{2,1,0:T(8,128)(2,1)}, u32[]{:S(2)}, u32[]{:S(2)}) collective-permute-start(bf16[2,256,512]{2,1,0:T(8,128)(2,1)} %get-tuple-element.33), channel_id=1, source_target_pairs={{0,8},{8,16},{16,24},{24,32},{32,40},{40,48},{48,56},{56,64},{64,7... | collective-permute-start | bytes 1572872 | tf_op jit(solution)/shard_map/ppermute | solution.py:251
  37.6 0.0 copy-done.5
  37.6 1.3 collective-permute-start.2
  38.8 14.1 %all-to-all-done = bf16[32,2,8,512]{3,2,1,0:T(8,128)(2,1)S(1)} async-done(((bf16[32,2,8,512]{3,2,1,0:T(8,128)(2,1)}), bf16[32,2,8,512]{3,2,1,0:T(8,128)(2,1)S(1)}, u32[]{:S(2)}, u32[]{:S(2)}) %all-to-all-start) | async-done | bytes 524320 | tf_op jit(solution)/shard_map/all_to_all | solution.py:350
  53.0 7.1 %all-to-all-start.1 = ((bf16[4,512,512]{2,1,0:T(8,128)(2,1)}), bf16[4,512,512]{2,1,0:T(8,128)(2,1)S(1)}, u32[]{:S(2)}, u32[]{:S(2)}) async-start(bf16[4,512,512]{2,1,0:T(8,128)(2,1)} %get-tuple-element.41), calls=%async_computation.1 | async-start | bytes 4194304 | tf_op jit(solution)/shard_map/all_to_all | solution.py:346
  60.1 0.1 add_convert_fusion.flags
  60.2 0.0 collective-permute-done.1.before_ref
  60.2 0.0 collective-permute-done.2.after_ref
  60.2 8.4 %window_grads.1 = (bf16[512,512]{1,0:T(8,128)(2,1)}, f32[512,512]{1,0:T(8,128)S(1)}, f32[512,512]{1,0:T(8,128)S(1)}, bf16[2,256,512]{2,1,0:T(8,128)(2,1)S(1)}, bf16[2,256,512]{2,1,0:T(8,128)(2,1)S(1)}) custom-call(s32[2]{0:T(128)S(1)} %add_convert_fusion.flags, bf16[512,512]{1,0:T(8,128)(2,1)} %q_ref.2, bf16[512,512]{1,0:T(8,128)(2,1)} %do_ref.3, ...), custom_call_target="tpu_custom_call" | custom-call | flops 8000000000 | bytes 25000000 | tf_op jit(solution)/shard_map/window_grads/pallas_call | solution.py:99
  68.6 0.0 copy-start
  68.6 1.1 copy-done
  69.6 0.0 copy-start.1
  69.6 1.0 copy-done.1
  70.6 1.3 collective-permute-start.3
  71.9 5.4 %collective-permute-start.4 = (bf16[2,256,512]{2,1,0:T(8,128)(2,1)S(1)}, bf16[2,256,512]{2,1,0:T(8,128)(2,1)}, u32[]{:S(2)}, u32[]{:S(2)}) collective-permute-start(bf16[2,256,512]{2,1,0:T(8,128)(2,1)S(1)} %get-tuple-element.39), channel_id=1, source_target_pairs={{0,8},{8,16},{16,24},{24,32},{32,40},{40,48},{48,56},{56,64},{64,7... | collective-permute-start | bytes 1572872 | tf_op jit(solution)/shard_map/ppermute | solution.py:251
  77.3 14.2 %collective-permute-done.3.low_ref = bf16[2,256,512]{2,1,0:T(8,128)(2,1)S(1)} collective-permute-done((bf16[2,256,512]{2,1,0:T(8,128)(2,1)S(1)}, bf16[2,256,512]{2,1,0:T(8,128)(2,1)S(1)}, u32[]{:S(2)}, u32[]{:S(2)}) %collective-permute-start.3) | collective-permute-done | bytes 524320 | tf_op jit(solution)/shard_map/ppermute | solution.py:251
  91.5 0.0 copy-start.3
  91.5 3.0 %collective-permute-done.4.high_ref = bf16[2,256,512]{2,1,0:T(8,128)(2,1)} collective-permute-done((bf16[2,256,512]{2,1,0:T(8,128)(2,1)S(1)}, bf16[2,256,512]{2,1,0:T(8,128)(2,1)}, u32[]{:S(2)}, u32[]{:S(2)}) %collective-permute-start.4) | collective-permute-done | bytes 524320 | tf_op jit(solution)/shard_map/ppermute | solution.py:251
  94.5 0.0 all-to-all-done.1.own_ref
  94.5 0.0 copy-start.2
  94.5 0.0 collective-permute-start.5
  94.5 0.1 pad_add_fusion.pos
  94.6 0.0 copy-done.3
  94.6 3.4 %join_rims.1 = (bf16[512,512]{1,0:T(8,128)(2,1)}, bf16[512,512]{1,0:T(8,128)(2,1)}) custom-call(f32[512,512]{1,0:T(8,128)} %copy-done, f32[512,512]{1,0:T(8,128)} %copy-done.1, bf16[2,256,512]{2,1,0:T(8,128)(2,1)} %copy-done.3, bf16[2,256,512]{2,1,0:T(8,128)(2,1)} %collective-permute-done.4.high_ref), custom_call_target="tpu_custom_call" | custom-call | tf_op jit(solution)/shard_map/join_rims/pallas_call | solution.py:215
  98.0 0.8 copy_bitcast_fusion
  98.8 0.0 copy-done.2
  98.8 0.0 collective-permute-done.5.other_ref
  98.8 19.0 %all-gather.2.cloned.1.call-done = bf16[4096,512]{1,0:T(8,128)(2,1)} async-done(((bf16[128,512]{1,0:T(8,128)(2,1)}), bf16[4096,512]{1,0:T(8,128)(2,1)}) %all-gather.2.cloned.1.call-update) | async-done | bytes 4194320 | tf_op jit(solution)/shard_map/all_gather | solution.py:342
  117.9 5.8 %byte_product.1 = bf16[512,512]{1,0:T(8,128)(2,1)} custom-call(s32[3]{0:T(128)S(1)} %pad_add_fusion.pos, bf16[4,512,512]{2,1,0:T(8,128)(2,1)} %copy-done.2, bf16[4,512,512]{2,1,0:T(8,128)(2,1)} %collective-permute-done.5.other_ref, bf16[8,512,512]{2,1,0:T(8,128)(2,1)} %bitcast.12), custom_call_target="tpu_custom_call" | custom-call | tf_op jit(solution)/shard_map/byte_product/pallas_call | solution.py:303
Async XLA Ops:
  7.2 110.7 %all-gather.2.cloned.1.call-start = ((), (), s32[]{:S(2)}) async-start(), calls=%async_computation.2 | async-start | bytes 4325376 | tf_op jit(solution)/shard_map/all_gather | solution.py:342
  7.2 13.2 %collective-permute-start = (bf16[128,512]{1,0:T(8,128)(2,1)}, bf16[128,512]{1,0:T(8,128)(2,1)S(1)}, u32[]{:S(2)}, u32[]{:S(2)}) collective-permute-start(bf16[128,512]{1,0:T(8,128)(2,1)} %param.21), channel_id=1, source_target_pairs={{0,0},{1,32},{2,64},{3,96},{4,128},{5,160},{6,192},{7,224},{8,8},{... | collective-permute-start | bytes 393224 | tf_op jit(solution)/shard_map/ppermute | solution.py:270
  14.3 23.2 %copy-start.5 = (bf16[2,256,512]{2,1,0:T(8,128)(2,1)S(1)}, bf16[2,256,512]{2,1,0:T(8,128)(2,1)}, u32[]{:S(2)}) copy-start(bf16[2,256,512]{2,1,0:T(8,128)(2,1)} %get-tuple-element.34) | copy-start | bytes 1572868
  20.4 0.6 copy-start.4
  21.0 31.9 %all-to-all-start = ((bf16[32,2,8,512]{3,2,1,0:T(8,128)(2,1)}), bf16[32,2,8,512]{3,2,1,0:T(8,128)(2,1)S(1)}, u32[]{:S(2)}, u32[]{:S(2)}) async-start(bf16[32,2,8,512]{3,2,1,0:T(8,128)(2,1)} %get-tuple-element.40), calls=%async_computation | async-start | bytes 1048576 | tf_op jit(solution)/shard_map/all_to_all | solution.py:350
  33.1 27.1 %collective-permute-start.1 = (bf16[2,256,512]{2,1,0:T(8,128)(2,1)}, bf16[2,256,512]{2,1,0:T(8,128)(2,1)}, u32[]{:S(2)}, u32[]{:S(2)}) collective-permute-start(bf16[2,256,512]{2,1,0:T(8,128)(2,1)} %get-tuple-element.33), channel_id=1, source_target_pairs={{0,8},{8,16},{16,24},{24,32},{32,40},{40,48},{48,56},{56,64},{64,7... | collective-permute-start | bytes 1572872 | tf_op jit(solution)/shard_map/ppermute | solution.py:251
  37.6 22.6 %collective-permute-start.2 = (bf16[2,256,512]{2,1,0:T(8,128)(2,1)S(1)}, bf16[2,256,512]{2,1,0:T(8,128)(2,1)}, u32[]{:S(2)}, u32[]{:S(2)}) collective-permute-start(bf16[2,256,512]{2,1,0:T(8,128)(2,1)S(1)} %copy-done.5), channel_id=1, source_target_pairs={{8,0},{16,8},{24,16},{32,24},{40,32},{48,40},{56,48},{64,56},{72,6... | collective-permute-start | bytes 1572872 | tf_op jit(solution)/shard_map/ppermute | solution.py:251
  53.0 41.6 %all-to-all-start.1 = ((bf16[4,512,512]{2,1,0:T(8,128)(2,1)}), bf16[4,512,512]{2,1,0:T(8,128)(2,1)S(1)}, u32[]{:S(2)}, u32[]{:S(2)}) async-start(bf16[4,512,512]{2,1,0:T(8,128)(2,1)} %get-tuple-element.41), calls=%async_computation.1 | async-start | bytes 4194304 | tf_op jit(solution)/shard_map/all_to_all | solution.py:346
  68.6 1.1 copy-start
  69.6 1.0 copy-start.1
  70.6 20.9 %collective-permute-start.3 = (bf16[2,256,512]{2,1,0:T(8,128)(2,1)S(1)}, bf16[2,256,512]{2,1,0:T(8,128)(2,1)S(1)}, u32[]{:S(2)}, u32[]{:S(2)}) collective-permute-start(bf16[2,256,512]{2,1,0:T(8,128)(2,1)S(1)} %get-tuple-element.38), channel_id=1, source_target_pairs={{8,0},{16,8},{24,16},{32,24},{40,32},{48,40},{56,48},{64,56},{72,6... | collective-permute-start | bytes 1572872 | tf_op jit(solution)/shard_map/ppermute | solution.py:251
  71.9 22.6 %collective-permute-start.4 = (bf16[2,256,512]{2,1,0:T(8,128)(2,1)S(1)}, bf16[2,256,512]{2,1,0:T(8,128)(2,1)}, u32[]{:S(2)}, u32[]{:S(2)}) collective-permute-start(bf16[2,256,512]{2,1,0:T(8,128)(2,1)S(1)} %get-tuple-element.39), channel_id=1, source_target_pairs={{0,8},{8,16},{16,24},{24,32},{32,40},{40,48},{48,56},{56,64},{64,7... | collective-permute-start | bytes 1572872 | tf_op jit(solution)/shard_map/ppermute | solution.py:251
  91.5 3.1 %copy-start.3 = (bf16[2,256,512]{2,1,0:T(8,128)(2,1)}, bf16[2,256,512]{2,1,0:T(8,128)(2,1)S(1)}, u32[]{:S(2)}) copy-start(bf16[2,256,512]{2,1,0:T(8,128)(2,1)S(1)} %collective-permute-done.3.low_ref) | copy-start | bytes 1572868
  94.5 4.3 %copy-start.2 = (bf16[4,512,512]{2,1,0:T(8,128)(2,1)}, bf16[4,512,512]{2,1,0:T(8,128)(2,1)S(1)}, u32[]{:S(2)}) copy-start(bf16[4,512,512]{2,1,0:T(8,128)(2,1)S(1)} %all-to-all-done.1.own_ref) | copy-start | bytes 6291460
  94.5 4.3 %collective-permute-start.5 = (bf16[4,512,512]{2,1,0:T(8,128)(2,1)S(1)}, bf16[4,512,512]{2,1,0:T(8,128)(2,1)}, u32[]{:S(2)}, u32[]{:S(2)}) collective-permute-start(bf16[4,512,512]{2,1,0:T(8,128)(2,1)S(1)} %all-to-all-done.1.own_ref), channel_id=1, source_target_pairs={{0,1},{1,0},{2,3},{3,2},{4,5},{5,4},{6,7},{7,6},{8,9},{9,8},{10,11... | collective-permute-start | bytes 6291464 | tf_op jit(solution)/shard_map/ppermute | solution.py:270
Sparse Core Ops, SparseCore 0:
  21.2 96.6 all-gather.1
